TPU v7x, 768 devices: a whole 4x8x12 slice. The times are simulated.
768 devices in a mesh: section: 48 (over x, z), row: 2 (over core), col: 8 (over y).
Axes of the slice: x: 4, y: 8, z: 12, core: 2. Of those that a mesh axis runs over, the one named last changes fastest.
Arguments:
- arriving: bfloat16 [48, 16, 16384], P('section', ('row', 'col')), may hold values from -64 to 64
- entering: bfloat16 [3, 16, 16384], P(None, ('row', 'col')), may hold values from -64 to 64
- gain: bfloat16 [48, 16384], P('section'), may hold values from 0.099609375 to 1.8984375
- kv_weight: bfloat16 [48, 16384, 1024], P('section', 'row', 'col'), may hold values from -0.046875 to 0.046875
- queries: bfloat16 [48, 4, 16, 8192], P('section', None, ('row', 'col')), may hold values from -150 to 150
- cache_keys: bfloat16 [48, 4, 16, 128, 512], P('section', None, ('row', 'col')), may hold values from -6 to 6
- cache_values: bfloat16 [48, 4, 16, 128, 512], P('section', None, ('row', 'col')), may hold values from -6 to 6
- lengths: int32 [51, 16], P(None, ('row', 'col')), may hold values from 2 to 128, as said below
Outputs:
- layer_out: bfloat16 [48, 4, 16, 16384], P('section', None, ('row', 'col'))
Inputs may be any that keep to these rules, and one draw needn't show every extreme that they name: Every row of lengths has a request with exactly 128 cached tokens, at a position drawn from the seed.
All inputs are finite; a program needn't handle non-finite values.
Results may differ from a plain program's by a relative error of at most 0.0034.
Values may be sent and summed in bfloat16 or wider, within the bound.
No kernel may reach another device: no remote copies, remote signals or barrier semaphores. Data moves between devices by JAX's collectives and lax.ppermute only.
A program may use at most 32 MiB of HBM per device.

v0:
```python
import jax
import jax.numpy as jnp
import numpy as np
from jax import lax
from jax.sharding import PartitionSpec as P

QH = 64
KVH = 4
HD = 128


def shifted(array, axis, by):
    devices = lax.axis_size(axis)
    pairs = [(i, i + by) for i in range(devices) if 0 <= i + by < devices]
    return lax.ppermute(array, axis, pairs)


def rotate(keys, positions):
    half = HD // 2
    steps_up = jnp.arange(half).astype(jnp.float32)
    inverse = jnp.exp(-jnp.log(jnp.float32(500000.0)) * steps_up / half)
    angle = positions.astype(jnp.float32)[:, None] * inverse[None, :]
    cosine = jnp.cos(angle)[:, None, :]
    sine = jnp.sin(angle)[:, None, :]
    first = keys[..., :half]
    second = keys[..., half:]
    return jnp.concatenate(
        [first * cosine - second * sine, second * cosine + first * sine], axis=-1
    )


def attend(query_row, keys, values, new_key, new_value, length):
    slots = keys.shape[0]
    factor = 1.0 / np.sqrt(HD)
    grouped = query_row.reshape(KVH, QH // KVH, HD)
    cached = keys.reshape(slots, KVH, HD)
    stored = values.reshape(slots, KVH, HD)
    scores = (
        jnp.einsum("ghd,lgd->ghl", grouped, cached, preferred_element_type=jnp.float32) * factor
    )
    live = jnp.arange(slots) < length
    scores = jnp.where(live[None, None, :], scores, jnp.float32(-1e30))
    own = jnp.einsum("ghd,gd->gh", grouped, new_key, preferred_element_type=jnp.float32) * factor
    top = jnp.maximum(jnp.max(scores, axis=-1), own)
    weights = jnp.exp(scores - top[..., None])
    own_weight = jnp.exp(own - top)
    total = jnp.sum(weights, axis=-1) + own_weight
    probs = (weights / total[..., None]).astype(jnp.bfloat16)
    own_prob = (own_weight / total).astype(jnp.bfloat16)
    mixed = jnp.einsum("ghl,lgd->ghd", probs, stored, preferred_element_type=jnp.float32)
    mixed = (
        mixed + own_prob.astype(jnp.float32)[..., None] * new_value.astype(jnp.float32)[:, None, :]
    )
    return mixed.reshape(1, QH * HD)


def per_device(arriving, entering, gain, kv_weight, queries, cache_keys, cache_values, lengths):
    section_at = lax.axis_index("section")
    row_at = lax.axis_index("row")
    rows_count = lax.axis_size("row")
    cols_count = lax.axis_size("col")
    ticks = queries.shape[1]
    layers_all = lengths.shape[0] - ticks + 1
    width = arriving.shape[2]
    half_width = width // rows_count
    heads_width = QH * HD
    weight = kv_weight[0]
    gain_row = gain[0].astype(jnp.float32)
    current = arriving[0]
    outputs = []
    for tick in range(ticks):
        if tick > 0:
            passed = shifted(current, "section", 1)
            current = jnp.where(section_at == 0, entering[tick - 1], passed)
        length = lax.dynamic_index_in_dim(
            lengths[:, 0], tick - section_at + layers_all - 1, 0, keepdims=False
        )
        wide = current.astype(jnp.float32)
        scale = lax.rsqrt(jnp.mean(wide * wide, axis=1, keepdims=True) + 1e-05)
        normed = (wide * scale * gain_row[None, :]).astype(jnp.bfloat16)
        mine = lax.dynamic_slice_in_dim(
            lax.all_gather(normed, ("row", "col"), axis=0, tiled=True),
            row_at * half_width,
            half_width,
            1,
        )
        gathered = jnp.dot(mine, weight, preferred_element_type=jnp.float32)
        partial_rows = jnp.swapaxes(gathered.reshape(rows_count, cols_count, -1), 0, 1)
        summed = lax.psum_scatter(partial_rows, "row", scatter_dimension=1, tiled=True)
        fresh = lax.all_to_all(summed, "col", split_axis=0, concat_axis=2, tiled=True)
        fresh = fresh.reshape(KVH, 2, HD)
        new_key = rotate(fresh[None, :, 0, :], length[None])[0].astype(jnp.bfloat16)
        new_value = fresh[:, 1, :].astype(jnp.bfloat16)
        mixed = attend(
            queries[0, tick, 0],
            cache_keys[0, tick, 0],
            cache_values[0, tick, 0],
            new_key,
            new_value,
            length,
        )
        joined = jnp.concatenate([wide[:, :heads_width] + mixed, wide[:, heads_width:]], axis=1)
        current = joined.astype(jnp.bfloat16)
        outputs.append(current)
    return jnp.stack(outputs, axis=0)[None]


def solution(mesh):
    placed = (
        P("section", ("row", "col"), None),
        P(None, ("row", "col"), None),
        P("section", None),
        P("section", "row", "col"),
        P("section", None, ("row", "col"), None),
        P("section", None, ("row", "col"), None, None),
        P("section", None, ("row", "col"), None, None),
        P(None, ("row", "col")),
    )
    return jax.shard_map(
        per_device,
        mesh=mesh,
        in_specs=placed,
        out_specs=P("section", None, ("row", "col"), None),
        check_vma=False,
    )
```

profile of v0, /device:TPU:6, one launch (start us, length us, event | category | flops | bytes accessed | tf_op | source)
XLA Modules:
  0.0 265.7 jit_solution(6036430377037827125)
XLA Ops:
  0.0 1.7 multiply_reduce_fusion.3
  3.4 33.8 %all-gather = bf16[16,1,16384]{2,1,0:T(2,128)(2,1)S(1)} all-gather(bf16[1,1,16384]{2,1,0:T(2,128)(2,1)S(1)} %convert_bitcast_fusion.3), channel_id=1, replica_groups=mesh['section'=48,'row'=2,'col'=8] {'row','col'}, dimensions={0}, use_global_device_ids=true | all-gather | bytes 557056 | tf_op jit(solution)/shard_map/all_gather | solution.py:82
  38.3 2.6 all-reduce
  40.9 1.2 dynamic-slice.8
  43.2 6.3 %all-to-all-start = ((f32[8,1,128]{2,1,0:T(1,128)}), f32[8,1,128]{2,1,0:T(1,128)}, u32[]{:S(2)}, u32[]{:S(2)}) async-start(f32[8,1,128]{2,1,0:T(1,128)} %bitcast.9), calls=%async_computation | async-start | bytes 8192 | tf_op jit(solution)/shard_map/all_to_all | solution.py:90
  51.0 1.2 iota_compare_fusion
  53.3 1.2 iota_compare_fusion.3
  54.5 1.3 iota_compare_fusion.1
  55.8 2.0 slice_reduce_fusion
  62.2 1.4 fusion.78
  71.8 4.3 %collective-permute-start = (bf16[1,16384]{1,0:T(2,128)(2,1)S(1)}, bf16[1,16384]{1,0:T(2,128)(2,1)S(1)}, u32[]{:S(2)}, u32[]{:S(2)}) collective-permute-start(bf16[1,16384]{1,0:T(2,128)(2,1)S(1)} %pad_maximum_fusion), channel_id=1, source_target_pairs={{0,16},{16,32},{32,48},{48,64},{64,80},{80,96},{96,112},{112,128},... | collective-permute-start | bytes 98312 | tf_op jit(solution)/shard_map/ppermute | solution.py:15
  77.9 11.0 %collective-permute-done = bf16[1,16384]{1,0:T(2,128)(2,1)S(1)} collective-permute-done((bf16[1,16384]{1,0:T(2,128)(2,1)S(1)}, bf16[1,16384]{1,0:T(2,128)(2,1)S(1)}, u32[]{:S(2)}, u32[]{:S(2)}) %collective-permute-start) | collective-permute-done | bytes 32800 | tf_op jit(solution)/shard_map/ppermute | solution.py:15
  88.9 1.6 multiply_reduce_fusion.2
  91.4 33.2 %all-gather.1 = bf16[16,1,16384]{2,1,0:T(2,128)(2,1)S(1)} all-gather(bf16[1,1,16384]{2,1,0:T(2,128)(2,1)S(1)} %convert_bitcast_fusion.2), channel_id=1, replica_groups=mesh['section'=48,'row'=2,'col'=8] {'row','col'}, dimensions={0}, use_global_device_ids=true | all-gather | bytes 557056 | tf_op jit(solution)/shard_map/all_gather | solution.py:82
  125.7 3.4 %all-reduce.1 = f32[8,2,128]{2,0,1:T(8,128)S(1)} all-reduce(f32[8,2,128]{2,0,1:T(8,128)S(1)} %fusion.15), channel_id=3, replica_groups=mesh['section'=48,'row'=2,'col'=8] {'row'}, use_global_device_ids=true, to_apply=%region_6.7.clone | all-reduce | flops 2048 | bytes 16384
  129.1 1.1 constant_dynamic-slice_fusion.10
  130.2 5.9 %all-to-all-start.1 = ((f32[8,1,128]{2,1,0:T(1,128)}), f32[8,1,128]{2,1,0:T(1,128)S(1)}, u32[]{:S(2)}, u32[]{:S(2)}) async-start(f32[8,1,128]{2,1,0:T(1,128)} %bitcast.28), calls=%async_computation.1 | async-start | bytes 8192 | tf_op jit(solution)/shard_map/all_to_all | solution.py:90
  136.2 7.6 %all-to-all-done.1 = f32[8,1,128]{2,1,0:T(1,128)S(1)} async-done(((f32[8,1,128]{2,1,0:T(1,128)}), f32[8,1,128]{2,1,0:T(1,128)S(1)}, u32[]{:S(2)}, u32[]{:S(2)}) %all-to-all-start.1) | async-done | bytes 4128 | tf_op jit(solution)/shard_map/all_to_all | solution.py:90
  144.6 1.9 collective-permute-start.1
  147.4 5.5 %collective-permute-done.1 = bf16[1,16384]{1,0:T(2,128)(2,1)S(1)} collective-permute-done((bf16[1,16384]{1,0:T(2,128)(2,1)S(1)}, bf16[1,16384]{1,0:T(2,128)(2,1)S(1)}, u32[]{:S(2)}, u32[]{:S(2)}) %collective-permute-start.1) | collective-permute-done | bytes 32800 | tf_op jit(solution)/shard_map/ppermute | solution.py:15
  154.4 30.3 %all-gather.2 = bf16[16,1,16384]{2,1,0:T(2,128)(2,1)S(1)} all-gather(bf16[1,1,16384]{2,1,0:T(2,128)(2,1)S(1)} %convert_bitcast_fusion.1), channel_id=1, replica_groups=mesh['section'=48,'row'=2,'col'=8] {'row','col'}, dimensions={0}, use_global_device_ids=true | all-gather | bytes 557056 | tf_op jit(solution)/shard_map/all_gather | solution.py:82
  185.8 3.1 %all-reduce.2 = f32[8,2,128]{2,0,1:T(8,128)S(1)} all-reduce(f32[8,2,128]{2,0,1:T(8,128)S(1)} %fusion.18), channel_id=4, replica_groups=mesh['section'=48,'row'=2,'col'=8] {'row'}, use_global_device_ids=true, to_apply=%region_10.11.clone | all-reduce | flops 2048 | bytes 16384
  189.0 1.1 constant_dynamic-slice_fusion.9
  190.1 6.0 %all-to-all-start.2 = ((f32[8,1,128]{2,1,0:T(1,128)}), f32[8,1,128]{2,1,0:T(1,128)S(1)}, u32[]{:S(2)}, u32[]{:S(2)}) async-start(f32[8,1,128]{2,1,0:T(1,128)} %bitcast.47), calls=%async_computation.2 | async-start | bytes 8192 | tf_op jit(solution)/shard_map/all_to_all | solution.py:90
  196.2 7.6 %all-to-all-done.2 = f32[8,1,128]{2,1,0:T(1,128)S(1)} async-done(((f32[8,1,128]{2,1,0:T(1,128)}), f32[8,1,128]{2,1,0:T(1,128)S(1)}, u32[]{:S(2)}, u32[]{:S(2)}) %all-to-all-start.2) | async-done | bytes 4128 | tf_op jit(solution)/shard_map/all_to_all | solution.py:90
  204.6 1.9 collective-permute-start.2
  206.7 6.2 %collective-permute-done.2 = bf16[1,16384]{1,0:T(2,128)(2,1)S(1)} collective-permute-done((bf16[1,16384]{1,0:T(2,128)(2,1)S(1)}, bf16[1,16384]{1,0:T(2,128)(2,1)S(1)}, u32[]{:S(2)}, u32[]{:S(2)}) %collective-permute-start.2) | collective-permute-done | bytes 32800 | tf_op jit(solution)/shard_map/ppermute | solution.py:15
  214.6 30.3 %all-gather.3 = bf16[16,1,16384]{2,1,0:T(2,128)(2,1)S(1)} all-gather(bf16[1,1,16384]{2,1,0:T(2,128)(2,1)S(1)} %convert_bitcast_fusion), channel_id=1, replica_groups=mesh['section'=48,'row'=2,'col'=8] {'row','col'}, dimensions={0}, use_global_device_ids=true | all-gather | bytes 557056 | tf_op jit(solution)/shard_map/all_gather | solution.py:82
  246.0 3.1 %all-reduce.3 = f32[8,2,128]{2,0,1:T(8,128)S(1)} all-reduce(f32[8,2,128]{2,0,1:T(8,128)S(1)} %fusion.21), channel_id=5, replica_groups=mesh['section'=48,'row'=2,'col'=8] {'row'}, use_global_device_ids=true, to_apply=%region_14.15.clone | all-reduce | flops 2048 | bytes 16384
  249.1 1.1 constant_dynamic-slice_fusion.8
  250.3 6.0 %all-to-all-start.3 = ((f32[8,1,128]{2,1,0:T(1,128)}), f32[8,1,128]{2,1,0:T(1,128)S(1)}, u32[]{:S(2)}, u32[]{:S(2)}) async-start(f32[8,1,128]{2,1,0:T(1,128)} %bitcast.66), calls=%async_computation.3 | async-start | bytes 8192 | tf_op jit(solution)/shard_map/all_to_all | solution.py:90
  256.3 7.6 %all-to-all-done.3 = f32[8,1,128]{2,1,0:T(1,128)S(1)} async-done(((f32[8,1,128]{2,1,0:T(1,128)}), f32[8,1,128]{2,1,0:T(1,128)S(1)}, u32[]{:S(2)}, u32[]{:S(2)}) %all-to-all-start.3) | async-done | bytes 4128 | tf_op jit(solution)/shard_map/all_to_all | solution.py:90
  (111 shorter events, 27.1 us)
Async XLA Ops:
  0.0 37.7 %copy-start = (bf16[1,8192,128]{2,1,0:T(8,128)(2,1)S(1)}, bf16[1,8192,128]{2,1,0:T(8,128)(2,1)}, u32[]{:S(2)}) copy-start(bf16[1,8192,128]{2,1,0:T(8,128)(2,1)} %param.11) | copy-start | bytes 6291460
  3.4 46.1 %copy-start.2 = (bf16[1,1,16384]{2,1,0:T(2,128)(2,1)S(1)}, bf16[1,1,16384]{2,1,0:T(2,128)(2,1)}, u32[]{:S(2)}) copy-start(bf16[1,1,16384]{2,1,0:T(2,128)(2,1)} %param.8) | copy-start | bytes 98308
  37.2 12.4 %copy-start.10 = (s32[51,1]{0,1:T(1,128)S(1)}, s32[51,1]{0,1:T(1,128)}, u32[]{:S(2)}) copy-start(s32[51,1]{0,1:T(1,128)} %param.15) | copy-start | bytes 616
  37.7 20.7 %copy-start.3 = (bf16[1,4,1,128,512]{4,3,2,1,0:T(8,128)(2,1)S(1)}, bf16[1,4,1,128,512]{4,3,2,1,0:T(8,128)(2,1)}, u32[]{:S(2)}) copy-start(bf16[1,4,1,128,512]{4,3,2,1,0:T(8,128)(2,1)} %param.13) | copy-start | bytes 1572868
  37.8 23.7 %copy-start.4 = (bf16[1,4,1,128,512]{4,3,2,1,0:T(8,128)(2,1)S(1)}, bf16[1,4,1,128,512]{4,3,2,1,0:T(8,128)(2,1)}, u32[]{:S(2)}) copy-start(bf16[1,4,1,128,512]{4,3,2,1,0:T(8,128)(2,1)} %param.14) | copy-start | bytes 1572868
  43.2 24.9 %all-to-all-start = ((f32[8,1,128]{2,1,0:T(1,128)}), f32[8,1,128]{2,1,0:T(1,128)}, u32[]{:S(2)}, u32[]{:S(2)}) async-start(f32[8,1,128]{2,1,0:T(1,128)} %bitcast.9), calls=%async_computation | async-start | bytes 8192 | tf_op jit(solution)/shard_map/all_to_all | solution.py:90
  59.1 32.1 %copy-start.1 = (bf16[1,16384]{1,0:T(2,128)(2,1)S(1)}, bf16[1,16384]{1,0:T(2,128)(2,1)}, u32[]{:S(2)}) copy-start(bf16[1,16384]{1,0:T(2,128)(2,1)} %param.10) | copy-start | bytes 98308
  71.8 17.1 %collective-permute-start = (bf16[1,16384]{1,0:T(2,128)(2,1)S(1)}, bf16[1,16384]{1,0:T(2,128)(2,1)S(1)}, u32[]{:S(2)}, u32[]{:S(2)}) collective-permute-start(bf16[1,16384]{1,0:T(2,128)(2,1)S(1)} %pad_maximum_fusion), channel_id=1, source_target_pairs={{0,16},{16,32},{32,48},{48,64},{64,80},{80,96},{96,112},{112,128},... | collective-permute-start | bytes 98312 | tf_op jit(solution)/shard_map/ppermute | solution.py:15
  91.4 52.6 %copy-start.8 = (bf16[8192]{0:T(1024)(128)(2,1)S(1)}, bf16[8192]{0:T(1024)(128)(2,1)}, u32[]{:S(2)}) copy-start(bf16[8192]{0:T(1024)(128)(2,1)} %get-tuple-element.6) | copy-start | bytes 49156
  124.6 28.3 %copy-start.5 = (bf16[3,1,16384]{2,0,1:T(4,128)(2,1)S(1)}, bf16[3,1,16384]{2,0,1:T(4,128)(2,1)}, u32[]{:S(2)}) copy-start(bf16[3,1,16384]{2,0,1:T(4,128)(2,1)} %param.9) | copy-start | bytes 294916
  130.2 13.6 %all-to-all-start.1 = ((f32[8,1,128]{2,1,0:T(1,128)}), f32[8,1,128]{2,1,0:T(1,128)S(1)}, u32[]{:S(2)}, u32[]{:S(2)}) async-start(f32[8,1,128]{2,1,0:T(1,128)} %bitcast.28), calls=%async_computation.1 | async-start | bytes 8192 | tf_op jit(solution)/shard_map/all_to_all | solution.py:90
  144.6 8.3 %collective-permute-start.1 = (bf16[1,16384]{1,0:T(2,128)(2,1)S(1)}, bf16[1,16384]{1,0:T(2,128)(2,1)S(1)}, u32[]{:S(2)}, u32[]{:S(2)}) collective-permute-start(bf16[1,16384]{1,0:T(2,128)(2,1)S(1)} %pad_maximum_fusion.1), channel_id=1, source_target_pairs={{0,16},{16,32},{32,48},{48,64},{64,80},{80,96},{96,112},{112,128},... | collective-permute-start | bytes 98312 | tf_op jit(solution)/shard_map/ppermute | solution.py:15
  154.4 49.5 %copy-start.7 = (bf16[8192]{0:T(1024)(128)(2,1)S(1)}, bf16[8192]{0:T(1024)(128)(2,1)}, u32[]{:S(2)}) copy-start(bf16[8192]{0:T(1024)(128)(2,1)} %get-tuple-element.8) | copy-start | bytes 49156
  190.1 13.7 %all-to-all-start.2 = ((f32[8,1,128]{2,1,0:T(1,128)}), f32[8,1,128]{2,1,0:T(1,128)S(1)}, u32[]{:S(2)}, u32[]{:S(2)}) async-start(f32[8,1,128]{2,1,0:T(1,128)} %bitcast.47), calls=%async_computation.2 | async-start | bytes 8192 | tf_op jit(solution)/shard_map/all_to_all | solution.py:90
  204.6 8.3 %collective-permute-start.2 = (bf16[1,16384]{1,0:T(2,128)(2,1)S(1)}, bf16[1,16384]{1,0:T(2,128)(2,1)S(1)}, u32[]{:S(2)}, u32[]{:S(2)}) collective-permute-start(bf16[1,16384]{1,0:T(2,128)(2,1)S(1)} %pad_maximum_fusion.2), channel_id=1, source_target_pairs={{0,16},{16,32},{32,48},{48,64},{64,80},{80,96},{96,112},{112,128},... | collective-permute-start | bytes 98312 | tf_op jit(solution)/shard_map/ppermute | solution.py:15
  214.6 49.7 %copy-start.9 = (f32[4,16]{1,0:T(4,128)S(1)}, f32[4,16]{1,0:T(4,128)}, u32[]{:S(2)}) copy-start(f32[4,16]{1,0:T(4,128)} %get-tuple-element.55) | copy-start | bytes 772
  244.9 19.8 %copy-start.6 = (bf16[1,1,8192]{2,0,1:T(2,128)(2,1)S(1)}, bf16[1,1,8192]{2,0,1:T(2,128)(2,1)}, u32[]{:S(2)}) copy-start(bf16[1,1,8192]{2,0,1:T(2,128)(2,1)} %get-tuple-element.23) | copy-start | bytes 49156
  250.3 13.7 %all-to-all-start.3 = ((f32[8,1,128]{2,1,0:T(1,128)}), f32[8,1,128]{2,1,0:T(1,128)S(1)}, u32[]{:S(2)}, u32[]{:S(2)}) async-start(f32[8,1,128]{2,1,0:T(1,128)} %bitcast.66), calls=%async_computation.3 | async-start | bytes 8192 | tf_op jit(solution)/shard_map/all_to_all | solution.py:90
where the time goes:
time: 267 us; the launch traced here: 266 us
  blocking collectives  140 us (52%)
  waiting for transfers between devices  45.4 us (17%)
  starting transfers between devices  32.4 us (12%)
  local copies, waits for them, and re-layouts  18.9 us (7%)
  other arithmetic  14.8 us (6%)
  matrix products  8.51 us (3%)
  between operations  5.81 us (2%)
    all_gather x4, blocking collectives, per_device(): lax.all_gather(normed, ('row', 'col'), axis=0, tiled=True)  128 us
    all_to_all x4, starting transfers between devices, per_device(): lax.all_to_all(summed, 'col', split_axis=0, concat_axis=2, tiled=True)  24.3 us
    all_to_all x4, waiting for transfers between devices, per_device(): lax.all_to_all(summed, 'col', split_axis=0, concat_axis=2, tiled=True)  22.8 us
    ppermute x3, waiting for transfers between devices, shifted(): return lax.ppermute(array, axis, pairs)  22.6 us
    unnamed x4, blocking collectives  12.2 us
    unnamed x35, local copies, waits for them, and re-layouts  10.4 us
    ppermute x3, starting transfers between devices, shifted(): return lax.ppermute(array, axis, pairs)  8.12 us
  transfers between devices with their start and end apart: 7, of which 6 were waited for; matrix products, arithmetic and copies ran while one was open for 7% of the time, Pallas kernels for 0%

commit v1 on v0

v1 whole, which is shorter than its diff:
```python
import jax
import jax.numpy as jnp
import numpy as np
from jax import lax
from jax.sharding import PartitionSpec as P

QH = 64
KVH = 4
HD = 128
PER = QH // KVH
ALL = ("section", "row", "col")
RC = ("row", "col")
FACTOR = 1.0 / np.sqrt(HD)
bf16 = jnp.bfloat16
f32 = jnp.float32


def angles(positions):
    half = HD // 2
    steps_up = jnp.arange(half).astype(f32)
    inverse = jnp.exp(-jnp.log(f32(500000.0)) * steps_up / half)
    angle = positions.astype(f32)[:, None] * inverse[None, :]
    cosine = jnp.cos(angle)
    sine = jnp.sin(angle)
    return jnp.concatenate([cosine, cosine], 1), jnp.concatenate([-sine, sine], 1)


def cached_attention(queries, keys, values, lens):
    ticks, slots = keys.shape[:2]
    grouped = queries.reshape(ticks, KVH, PER, HD)
    cached = keys.reshape(ticks, slots, KVH, HD)
    stored = values.reshape(ticks, slots, KVH, HD)
    scores = jnp.einsum("tghd,tlgd->tghl", grouped, cached, preferred_element_type=f32)
    scores = scores * FACTOR
    live = jnp.arange(slots)[None, :] < lens[:, None]
    scores = jnp.where(live[:, None, None, :], scores, f32(-1e30))
    top = jnp.max(scores, axis=-1)
    weights = jnp.exp(scores - top[..., None])
    total = jnp.sum(weights, axis=-1)
    probs = (weights / total[..., None]).astype(bf16)
    mean = jnp.einsum("tghl,tlgd->tghd", probs, stored, preferred_element_type=f32)
    return mean, top + jnp.log(total)


def split3(x):
    hi = lax.reduce_precision(x, 8, 7)
    mid = lax.reduce_precision(x - hi, 8, 7)
    return hi, mid, (x - hi) - mid


def combine(x, mean, messages, keep):
    rows = x.shape[0]
    own = jnp.stack([messages[2 * g, :, :PER] for g in range(KVH)], 1).astype(f32)
    own = jnp.where(keep, own, 0.0)[..., None]
    new = jnp.stack([messages[2 * g + 1] for g in range(KVH)], 1).astype(f32)[:, :, None, :]
    mean = mean.reshape(rows, KVH, PER, HD).astype(f32)
    mixed = mean + own * (new - mean)
    return (x.astype(f32) + mixed.reshape(rows, QH * HD)).astype(bf16)


def project(x, gain_row, w_here, w_there, row_at, q, lse, cosine, sine, is_key):
    half = w_here.shape[0]
    wide = x.astype(f32)
    scale = lax.rsqrt(jnp.mean(wide * wide, axis=1, keepdims=True) + 1e-05)
    scaled = (wide * gain_row).astype(bf16)
    mine = lax.dynamic_slice_in_dim(scaled, row_at * half, half, 1)
    other = lax.dynamic_slice_in_dim(scaled, (1 - row_at) * half, half, 1)
    fresh = jnp.dot(mine, w_here, preferred_element_type=f32)
    fresh = fresh + jnp.dot(other, w_there, preferred_element_type=f32)
    fresh = fresh * scale
    swapped = jnp.concatenate([fresh[:, HD // 2 :], fresh[:, : HD // 2]], 1)
    key = lax.reduce_precision(fresh * cosine + swapped * sine, 8, 7)
    score = jnp.sum(q.reshape(-1, PER, HD).astype(f32) * key[:, None, :], axis=-1) * FACTOR
    own = 1.0 / (1.0 + jnp.exp(lse - score))
    own = jnp.pad(own, ((0, 0), (0, HD - PER)))
    return jnp.where(is_key, own, fresh).astype(bf16)


def per_device(arriving, entering, gain, kv_weight, queries, cache_keys, cache_values, lengths):
    section_at = lax.axis_index("section")
    row_at = lax.axis_index("row")
    col_at = lax.axis_index("col")
    sections = lax.axis_size("section")
    cols = lax.axis_size("col")
    ticks = queries.shape[1]
    width = arriving.shape[2]
    half = width // 2
    last = section_at == sections - 1
    first = section_at == 0

    def at(s, r, c):
        return ((s % sections) * 2 + r) * cols + c

    def links(pairs):
        return [(at(s, r, c), at(v, w, c)) for s, r, v, w in pairs for c in range(cols)]

    def relay_group(r):
        return [
            [at(s, r, c) for c in range(cols)] + [at(s + 1, 1 - r, c) for c in range(cols)]
            for s in range(sections)
        ]

    w_here = kv_weight[0]
    w_there = lax.ppermute(w_here, "row", [(0, 1), (1, 0)])
    gain_row = gain[0].astype(f32)[None, :]
    lens = lax.dynamic_slice_in_dim(lengths[:, 0], sections - 1 - section_at, ticks, 0)
    mean, lse = cached_attention(queries[0, :, 0], cache_keys[0, :, 0], cache_values[0, :, 0], lens)

    flat = mean.reshape(ticks, half).astype(bf16)
    fed = jnp.where(last, entering[:, 0, :half], flat[: ticks - 1])
    tail = jnp.where(first, entering[0, 0, half:], jnp.where(last, entering[1, 0, half:], entering[2, 0, half:]))
    parts = jnp.stack(split3(lse), 1).astype(bf16)
    asked = queries[0, :, 0].reshape(ticks, KVH, PER * HD)

    def block(body, slots):
        per_group = []
        for g in range(KVH):
            aux = [jnp.stack([lens[t] for t in slots]).astype(bf16), jnp.zeros((14,), bf16)]
            aux += [parts[t, :, g].reshape(-1) for t in slots]
            aux = jnp.concatenate(aux)
            aux = jnp.pad(aux, (0, 8 * HD - aux.shape[0]))
            one = jnp.concatenate([*body, *[asked[t, g] for t in slots], aux])
            per_group += [one, one]
        return per_group

    sent = block([arriving[0, 0], fed[1]], (0, 2)) + block([fed[2], tail, fed[0]], (1, 3))
    sent = jnp.stack(sent).reshape(2 * cols, -1, HD)
    got = lax.all_to_all(sent, RC, split_axis=0, concat_axis=0, tiled=True)
    got = got.reshape(2 * cols, -1)

    around = range(sections)
    mean_a = lax.ppermute(got[:, width : width + half], ALL, links([(s, r, s + 1, r) for s in around for r in (0, 1)]))
    mean_b = lax.ppermute(got[:, :half], ALL, links([(s, 1, s + 1, 1) for s in around]))
    tails = lax.ppermute(got[:, half:width], ALL, links([(sections - 1, 1, 0, 0), (1, 1, 0, 1)]))
    q_at = width + half
    aux_at = q_at + 2 * PER * HD
    asks, lses, turns = [], [], []
    for k in range(2):
        asks.append(got[:, q_at + k * PER * HD : q_at + (k + 1) * PER * HD])
        three = got[:, aux_at + 16 + 48 * k : aux_at + 64 + 48 * k].astype(f32)
        lses.append(three[:, :16] + three[:, 16:32] + three[:, 32:])
        turns.append(angles(got[:, aux_at + k].astype(f32)))
    is_key = col_at % 2 == 0

    x = got[:, :width]
    rows, messages = [], []
    for tick in range(ticks):
        if tick > 0:
            there = (tick - 1) % 2
            relayed = lax.ppermute(x, ALL, links([(s, there, s + 1, 1 - there) for s in range(sections - 1)]))
            send = jnp.broadcast_to(message[None], (2 * cols, *message.shape))
            heard = lax.all_to_all(send, ALL, split_axis=0, concat_axis=0, axis_index_groups=relay_group(there), tiled=True)
            head = combine(relayed[:, :half], mean_b if tick == 3 else mean_a, heard[:cols], jnp.logical_not(first))
            rest = jnp.where(first, got[:, half:width] if tick == 1 else tails, relayed[:, half:])
            x = jnp.concatenate([head, rest], axis=1)
        k = tick // 2
        message = project(x, gain_row, w_here, w_there, row_at, asks[k], lses[k], *turns[k], is_key)
        rows.append(x)
        messages.append(message)

    mine, other, told = [], [], []
    for k in range(2):
        for keep, r in ((mine, row_at), (other, 1 - row_at)):
            a = lax.dynamic_slice_in_dim(rows[2 * k], r * cols + col_at, 1, 0)
            b = lax.dynamic_slice_in_dim(rows[2 * k + 1], r * cols + col_at, 1, 0)
            keep.append(jnp.where(row_at == 0, a, b))
        told.append(jnp.where(row_at == 0, messages[2 * k], messages[2 * k + 1]))
    swapped = lax.ppermute(jnp.concatenate(other, 0), "row", [(0, 1), (1, 0)])
    told = lax.all_to_all(jnp.stack(told, 1), RC, split_axis=0, concat_axis=0, tiled=True)
    outputs = []
    for tick in range(ticks):
        k, r = tick // 2, tick % 2
        row = jnp.where(row_at == r, mine[k], swapped[k : k + 1])
        heard = told[r * cols : (r + 1) * cols, k][:, None, :]
        head = combine(row[:, :half], mean[tick].reshape(1, half), heard, True)
        outputs.append(jnp.concatenate([head, row[:, half:]], axis=1))
    return jnp.stack(outputs, axis=0)[None]


def solution(mesh):
    placed = (
        P("section", ("row", "col"), None),
        P(None, ("row", "col"), None),
        P("section", None),
        P("section", "row", "col"),
        P("section", None, ("row", "col"), None),
        P("section", None, ("row", "col"), None, None),
        P("section", None, ("row", "col"), None, None),
        P(None, ("row", "col")),
    )
    return jax.shard_map(
        per_device,
        mesh=mesh,
        in_specs=placed,
        out_specs=P("section", None, ("row", "col"), None),
        check_vma=False,
    )
```

time: 267 us -> 181 us (0.68)
  blocking collectives: 140 us -> 0 us
  starting transfers between devices: 32.4 us -> 54.4 us
  local copies, waits for them, and re-layouts: 18.9 us -> 34.4 us
  waiting for transfers between devices: 45.4 us -> 60.1 us
  between operations: 5.81 us -> 1.12 us
  other arithmetic: 14.8 us -> 18.5 us
    all_gather x4 -> x0, blocking collectives: 128 us -> none  [per_device(): lax.all_gather(normed, ('row', 'col'), axis=0, tiled=True)]
    all_to_all x4 -> x5, waiting for transfers between devices: 22.8 us -> 43 us  [the longest x1 21.1 us: per_device(): got = lax.all_to_all(sent, RC, split_axis=0, concat_axis=0, tiled=True)]
    ppermute x3 -> x8, starting transfers between devices: 8.12 us -> 23.3 us  [the longest x3 11.7 us: per_device(): lax.ppermute(x, ALL, links([(s, there, s + 1, 1 - there) for s in range(s...]
    unnamed x4 -> x0, blocking collectives: 12.2 us -> none
    concatenate x4 -> x16, local copies, waits for them, and re-layouts: 0.76 us -> 10.9 us  [the longest x8 10.8 us: block(): aux = jnp.concatenate(aux)]
    all_to_all x4 -> x5, starting transfers between devices: 24.3 us -> 31 us  [the longest x3 16.4 us: per_device(): lax.all_to_all(send, ALL, split_axis=0, concat_axis=0, axis_index_groups=...]
    another operation x0 -> x30, local copies, waits for them, and re-layouts: none -> 5.73 us  [the longest x16 1.34 us: block(): aux += [parts[t, :, g].reshape(-1) for t in slots]]
    ppermute x3 -> x8, waiting for transfers between devices: 22.6 us -> 17.1 us  [the longest x1 13.8 us: per_device(): lax.ppermute(got[:, width:width + half], ALL, links([(s, r, s + 1, r) for...]
  transfers between devices with their start and end apart: 7 -> 13, of which waited for: 6 -> 7; matrix products, arithmetic and copies ran while one was open for 7% -> 13% of each run, Pallas kernels for 0% -> 0%
where the time goes in v1:
time: 181 us; the launch traced here: 179 us
  waiting for transfers between devices  60.1 us (33%)
  starting transfers between devices  54.4 us (30%)
  local copies, waits for them, and re-layouts  34.4 us (19%)
  other arithmetic  18.5 us (10%)
  matrix products  10.3 us (6%)
    all_to_all x1, waiting for transfers between devices, per_device(): got = lax.all_to_all(sent, RC, split_axis=0, concat_axis=0, tiled=True)  21.1 us
    all_to_all x3, waiting for transfers between devices, per_device(): lax.all_to_all(send, ALL, split_axis=0, concat_axis=0, axis_index_groups=...  16.8 us
    all_to_all x3, starting transfers between devices, per_device(): lax.all_to_all(send, ALL, split_axis=0, concat_axis=0, axis_index_groups=...  16.4 us
    ppermute x1, waiting for transfers between devices, per_device(): lax.ppermute(got[:, width:width + half], ALL, links([(s, r, s + 1, r) for...  13.8 us
    unnamed x89, local copies, waits for them, and re-layouts  12.5 us
    ppermute x3, starting transfers between devices, per_device(): lax.ppermute(x, ALL, links([(s, there, s + 1, 1 - there) for s in range(s...  11.7 us
    concatenate x8, local copies, waits for them, and re-layouts, block(): aux = jnp.concatenate(aux)  10.8 us
    dot_general x4, matrix products, project(): fresh = fresh + jnp.dot(other, w_there, preferred_element_type=f32)  7.98 us
  transfers between devices with their start and end apart: 13, of which 7 were waited for; matrix products, arithmetic and copies ran while one was open for 13% of the time, Pallas kernels for 0%

profile of v1, /device:TPU:6, one launch (start us, length us, event | category | flops | bytes accessed | tf_op | source)
XLA Modules:
  0.0 178.8 jit_solution(172709862402389216)
XLA Ops:
  6.8 1.4 concatenate.177
  9.6 1.4 concatenate.179
  12.5 1.4 concatenate.181
  15.3 1.4 concatenate.183
  28.9 7.2 %all-to-all-start = ((bf16[16,232,128]{2,1,0:T(8,128)(2,1)}), bf16[16,232,128]{2,1,0:T(8,128)(2,1)}, u32[]{:S(2)}, u32[]{:S(2)}) async-start(bf16[16,232,128]{2,1,0:T(8,128)(2,1)} %bitcast_dynamic-update-slice_fusion.1), calls=%async_computation | async-start | bytes 1900544 | tf_op jit(solution)/shard_map/all_to_all | solution.py:128
  36.2 2.3 %collective-permute-start.2 = (bf16[8192,128]{1,0:T(8,128)(2,1)S(1)}, bf16[8192,128]{1,0:T(8,128)(2,1)}, u32[]{:S(2)}, u32[]{:S(2)}) collective-permute-start(bf16[8192,128]{1,0:T(8,128)(2,1)S(1)} %bitcast.233), channel_id=1, source_target_pairs={{0,8},{8,0},{1,9},{9,1},{2,10},{10,2},{3,11},{11,3},{4,12},{12,4},... | collective-permute-start | bytes 6291464 | tf_op jit(solution)/shard_map/ppermute | solution.py:104
  38.6 21.1 %all-to-all-done = bf16[16,232,128]{2,1,0:T(8,128)(2,1)} async-done(((bf16[16,232,128]{2,1,0:T(8,128)(2,1)}), bf16[16,232,128]{2,1,0:T(8,128)(2,1)}, u32[]{:S(2)}, u32[]{:S(2)}) %all-to-all-start) | async-done | bytes 950304 | tf_op jit(solution)/shard_map/all_to_all | solution.py:128
  59.8 1.3 copy.79
  61.9 6.2 %collective-permute-start = (bf16[16,16384]{1,0:T(8,128)(2,1)}, bf16[16,16384]{1,0:T(8,128)(2,1)}, u32[]{:S(2)}, u32[]{:S(2)}) collective-permute-start(bf16[16,16384]{1,0:T(8,128)(2,1)} %slice.714), channel_id=1, source_target_pairs={{0,24},{1,25},{2,26},{3,27},{4,28},{5,29},{6,30},{7,31},{16,40},{1... | collective-permute-start | bytes 1572872 | tf_op jit(solution)/shard_map/ppermute | solution.py:150
  69.3 2.0 %fusion.4 = f32[16,128]{1,0:T(8,128)S(1)} fusion(f32[16,128]{1,0:T(8,128)S(1)} %fusion.35, bf16[8192,128]{1,0:T(8,128)(2,1)} %collective-permute-done.2, bf16[16,16384]{1,0:T(8,128)(2,1)S(1)} %get-tuple-element.57, s32[]{:T(128)S(6)} %select_n.203, f32[16]{0:T(128)S(1)} %add_rsqrt_fusion.3), kind=kOutput, calls=%fused_computation.17 | convolution fusion | flops 33558528 | bytes 2376196 | tf_op jit(solution)/shard_map/dot_general | solution.py:69
  72.3 4.3 %all-to-all-start.1 = ((bf16[16,16,128]{2,1,0:T(8,128)(2,1)}), bf16[16,16,128]{2,1,0:T(8,128)(2,1)S(1)}, u32[]{:S(2)}, u32[]{:S(2)}) async-start(bf16[16,16,128]{2,1,0:T(8,128)(2,1)} %broadcast_in_dim.32), calls=%async_computation.1 | async-start | bytes 131072 | tf_op jit(solution)/shard_map/all_to_all | solution.py:152
  76.7 7.9 %all-to-all-done.1 = bf16[16,16,128]{2,1,0:T(8,128)(2,1)S(1)} async-done(((bf16[16,16,128]{2,1,0:T(8,128)(2,1)}), bf16[16,16,128]{2,1,0:T(8,128)(2,1)S(1)}, u32[]{:S(2)}, u32[]{:S(2)}) %all-to-all-start.1) | async-done | bytes 65568 | tf_op jit(solution)/shard_map/all_to_all | solution.py:152
  85.2 1.8 %fusion.82 = (bf16[16,8192]{1,0:T(8,128)(2,1)}, bf16[16,8192]{1,0:T(8,128)(2,1)S(1)}, bf16[16,8192]{1,0:T(8,128)(2,1)}, bf16[16,8192]{1,0:T(8,128)(2,1)S(1)}) fusion(bf16[16,29696]{1,0:T(8,128)(2,1)S(1)} %bitcast.239, bf16[16,16384]{1,0:T(8,128)(2,1)} %collective-permute-done, pred[]{:T(512)S(6)} %eq.14), kind=kLoop, calls=%fused_computation.362 | loop fusion | flops 131072 | bytes 2097153 | tf_op jit(solution)/shard_map/slice | solution.py:133
  87.0 4.3 %collective-permute-start.1 = (bf16[16,8192]{1,0:T(8,128)(2,1)S(1)}, bf16[16,8192]{1,0:T(8,128)(2,1)S(1)}, u32[]{:S(2)}, u32[]{:S(2)}) collective-permute-start(bf16[16,8192]{1,0:T(8,128)(2,1)S(1)} %get-tuple-element.55), channel_id=1, source_target_pairs={{0,16},{1,17},{2,18},{3,19},{4,20},{5,21},{6,22},{7,23},{8,24},{9,... | collective-permute-start | bytes 786440 | tf_op jit(solution)/shard_map/ppermute | solution.py:132
  92.0 1.4 collective-permute-start.4
  93.4 1.4 collective-permute-start.6
  94.8 13.8 %collective-permute-done.1 = bf16[16,8192]{1,0:T(8,128)(2,1)S(1)} collective-permute-done((bf16[16,8192]{1,0:T(8,128)(2,1)S(1)}, bf16[16,8192]{1,0:T(8,128)(2,1)S(1)}, u32[]{:S(2)}, u32[]{:S(2)}) %collective-permute-start.1) | collective-permute-done | bytes 262176 | tf_op jit(solution)/shard_map/ppermute | solution.py:132
  108.8 1.5 fusion.18
  113.2 2.0 %fusion.3 = f32[16,128]{1,0:T(8,128)S(1)} fusion(f32[16,128]{1,0:T(8,128)S(1)} %fusion.32, bf16[8192,128]{1,0:T(8,128)(2,1)} %collective-permute-done.2, bf16[16,16384]{1,0:T(8,128)(2,1)S(1)} %get-tuple-element.63, s32[]{:T(128)S(6)} %select_n.203, f32[16]{0:T(128)S(1)} %add_rsqrt_fusion.2), kind=kOutput, calls=%fused_computation.15 | convolution fusion | flops 33558528 | bytes 2376196 | tf_op jit(solution)/shard_map/dot_general | solution.py:69
  116.2 8.6 %all-to-all-start.2 = ((bf16[16,16,128]{2,1,0:T(8,128)(2,1)}), bf16[16,16,128]{2,1,0:T(8,128)(2,1)S(1)}, u32[]{:S(2)}, u32[]{:S(2)}) async-start(bf16[16,16,128]{2,1,0:T(8,128)(2,1)} %broadcast_in_dim.34), calls=%async_computation.2 | async-start | bytes 131072 | tf_op jit(solution)/shard_map/all_to_all | solution.py:152
  125.9 6.1 %all-to-all-done.2 = bf16[16,16,128]{2,1,0:T(8,128)(2,1)S(1)} async-done(((bf16[16,16,128]{2,1,0:T(8,128)(2,1)}), bf16[16,16,128]{2,1,0:T(8,128)(2,1)S(1)}, u32[]{:S(2)}, u32[]{:S(2)}) %all-to-all-start.2) | async-done | bytes 65568 | tf_op jit(solution)/shard_map/all_to_all | solution.py:152
  133.4 1.6 fusion.21
  135.7 2.0 %fusion.2 = f32[16,128]{1,0:T(8,128)S(1)} fusion(f32[16,128]{1,0:T(8,128)S(1)} %fusion.29, bf16[8192,128]{1,0:T(8,128)(2,1)} %collective-permute-done.2, bf16[16,16384]{1,0:T(8,128)(2,1)S(1)} %get-tuple-element.61, s32[]{:T(128)S(6)} %select_n.203, f32[16]{0:T(128)S(1)} %add_rsqrt_fusion.1), kind=kOutput, calls=%fused_computation.13 | convolution fusion | flops 33558528 | bytes 2376196 | tf_op jit(solution)/shard_map/dot_general | solution.py:69
  138.7 3.5 %all-to-all-start.3 = ((bf16[16,16,128]{2,1,0:T(8,128)(2,1)}), bf16[16,16,128]{2,1,0:T(8,128)(2,1)S(1)}, u32[]{:S(2)}, u32[]{:S(2)}) async-start(bf16[16,16,128]{2,1,0:T(8,128)(2,1)} %broadcast_in_dim.35), calls=%async_computation.3 | async-start | bytes 131072 | tf_op jit(solution)/shard_map/all_to_all | solution.py:152
  143.0 4.3 %collective-permute-start.5 = (bf16[16,16384]{1,0:T(8,128)(2,1)}, bf16[16,16384]{1,0:T(8,128)(2,1)}, u32[]{:S(2)}, u32[]{:S(2)}) collective-permute-start(bf16[16,16384]{1,0:T(8,128)(2,1)} %pad_maximum_fusion.1), channel_id=1, source_target_pairs={{0,24},{1,25},{2,26},{3,27},{4,28},{5,29},{6,30},{7,31},{16,40},{1... | collective-permute-start | bytes 1572872 | tf_op jit(solution)/shard_map/ppermute | solution.py:150
  147.3 2.8 %all-to-all-done.3 = bf16[16,16,128]{2,1,0:T(8,128)(2,1)S(1)} async-done(((bf16[16,16,128]{2,1,0:T(8,128)(2,1)}), bf16[16,16,128]{2,1,0:T(8,128)(2,1)S(1)}, u32[]{:S(2)}, u32[]{:S(2)}) %all-to-all-start.3) | async-done | bytes 65568 | tf_op jit(solution)/shard_map/all_to_all | solution.py:152
  150.2 3.3 %collective-permute-done.5 = bf16[16,16384]{1,0:T(8,128)(2,1)} collective-permute-done((bf16[16,16384]{1,0:T(8,128)(2,1)}, bf16[16,16384]{1,0:T(8,128)(2,1)}, u32[]{:S(2)}, u32[]{:S(2)}) %collective-permute-start.5) | collective-permute-done | bytes 524320 | tf_op jit(solution)/shard_map/ppermute | solution.py:150
  154.7 1.6 fusion.15
  157.2 2.0 %fusion.1 = f32[16,128]{1,0:T(8,128)S(1)} fusion(f32[16,128]{1,0:T(8,128)S(1)} %fusion.26, bf16[8192,128]{1,0:T(8,128)(2,1)} %collective-permute-done.2, bf16[16,16384]{1,0:T(8,128)(2,1)S(1)} %get-tuple-element.59, s32[]{:T(128)S(6)} %select_n.203, f32[16]{0:T(128)S(1)} %add_rsqrt_fusion), kind=kOutput, calls=%fused_computation.11 | convolution fusion | flops 33558528 | bytes 2376196 | tf_op jit(solution)/shard_map/dot_general | solution.py:69
  160.3 7.4 %all-to-all-start.4 = ((bf16[16,2,128]{2,1,0:T(2,128)(2,1)}), bf16[16,2,128]{2,1,0:T(2,128)(2,1)S(1)}, u32[]{:S(2)}, u32[]{:S(2)}) async-start(bf16[16,2,128]{2,1,0:T(2,128)(2,1)} %copy.53), calls=%async_computation.4 | async-start | bytes 16384 | tf_op jit(solution)/shard_map/all_to_all | solution.py:169
  167.8 2.3 %collective-permute-start.7 = (bf16[2,16384]{1,0:T(2,128)(2,1)S(1)}, bf16[2,16384]{1,0:T(2,128)(2,1)S(1)}, u32[]{:S(2)}, u32[]{:S(2)}) collective-permute-start(bf16[2,16384]{1,0:T(2,128)(2,1)S(1)} %pad_maximum_fusion.3), channel_id=1, source_target_pairs={{0,8},{8,0},{1,9},{9,1},{2,10},{10,2},{3,11},{11,3},{4,12},{12,4},... | collective-permute-start | bytes 196616 | tf_op jit(solution)/shard_map/ppermute | solution.py:168
  170.2 5.0 %all-to-all-done.4 = bf16[16,2,128]{2,1,0:T(2,128)(2,1)S(1)} async-done(((bf16[16,2,128]{2,1,0:T(2,128)(2,1)}), bf16[16,2,128]{2,1,0:T(2,128)(2,1)S(1)}, u32[]{:S(2)}, u32[]{:S(2)}) %all-to-all-start.4) | async-done | bytes 8224 | tf_op jit(solution)/shard_map/all_to_all | solution.py:169
  (245 shorter events, 43.0 us)
Async XLA Ops:
  0.0 3.3 %copy-start.21 = (s32[51,1]{0,1:T(1,128)S(1)}, s32[51,1]{0,1:T(1,128)}, u32[]{:S(2)}) copy-start(s32[51,1]{0,1:T(1,128)} %param.15) | copy-start | bytes 616
  0.0 4.5 %copy-start.11 = (bf16[3,1,16384]{2,0,1:T(4,128)(2,1)S(1)}, bf16[3,1,16384]{2,0,1:T(4,128)(2,1)}, u32[]{:S(2)}) copy-start(bf16[3,1,16384]{2,0,1:T(4,128)(2,1)} %param.9) | copy-start | bytes 294916
  0.0 4.9 %copy-start.17 = (bf16[1,1,16384]{2,1,0:T(2,128)(2,1)S(1)}, bf16[1,1,16384]{2,1,0:T(2,128)(2,1)}, u32[]{:S(2)}) copy-start(bf16[1,1,16384]{2,1,0:T(2,128)(2,1)} %param.8) | copy-start | bytes 98308
  1.2 3.9 %copy-start.8 = (bf16[1,4,1,8192]{3,1,2,0:T(4,128)(2,1)S(1)}, bf16[1,4,1,8192]{3,1,2,0:T(4,128)(2,1)}, u32[]{:S(2)}) copy-start(bf16[1,4,1,8192]{3,1,2,0:T(4,128)(2,1)} %param.12) | copy-start | bytes 196612
  5.8 30.4 %copy-start = (bf16[1,8192,128]{2,1,0:T(8,128)(2,1)S(1)}, bf16[1,8192,128]{2,1,0:T(8,128)(2,1)}, u32[]{:S(2)}) copy-start(bf16[1,8192,128]{2,1,0:T(8,128)(2,1)} %param.11) | copy-start | bytes 6291460
  6.5 32.0 %copy-start.18 = (bf16[1,16384]{1,0:T(2,128)(2,1)S(1)}, bf16[1,16384]{1,0:T(2,128)(2,1)}, u32[]{:S(2)}) copy-start(bf16[1,16384]{1,0:T(2,128)(2,1)} %param.10) | copy-start | bytes 98308
  28.9 30.8 %all-to-all-start = ((bf16[16,232,128]{2,1,0:T(8,128)(2,1)}), bf16[16,232,128]{2,1,0:T(8,128)(2,1)}, u32[]{:S(2)}, u32[]{:S(2)}) async-start(bf16[16,232,128]{2,1,0:T(8,128)(2,1)} %bitcast_dynamic-update-slice_fusion.1), calls=%async_computation | async-start | bytes 1900544 | tf_op jit(solution)/shard_map/all_to_all | solution.py:128
  36.2 33.0 %collective-permute-start.2 = (bf16[8192,128]{1,0:T(8,128)(2,1)S(1)}, bf16[8192,128]{1,0:T(8,128)(2,1)}, u32[]{:S(2)}, u32[]{:S(2)}) collective-permute-start(bf16[8192,128]{1,0:T(8,128)(2,1)S(1)} %bitcast.233), channel_id=1, source_target_pairs={{0,8},{8,0},{1,9},{9,1},{2,10},{10,2},{3,11},{11,3},{4,12},{12,4},... | collective-permute-start | bytes 6291464 | tf_op jit(solution)/shard_map/ppermute | solution.py:104
  61.9 23.3 %collective-permute-start = (bf16[16,16384]{1,0:T(8,128)(2,1)}, bf16[16,16384]{1,0:T(8,128)(2,1)}, u32[]{:S(2)}, u32[]{:S(2)}) collective-permute-start(bf16[16,16384]{1,0:T(8,128)(2,1)} %slice.714), channel_id=1, source_target_pairs={{0,24},{1,25},{2,26},{3,27},{4,28},{5,29},{6,30},{7,31},{16,40},{1... | collective-permute-start | bytes 1572872 | tf_op jit(solution)/shard_map/ppermute | solution.py:150
  68.1 3.3 %copy-start.5 = (f32[2,8,16,128]{3,2,1,0:T(8,128)}, f32[2,8,16,128]{3,2,1,0:T(8,128)S(1)}, u32[]{:S(2)}) copy-start(f32[2,8,16,128]{3,2,1,0:T(8,128)S(1)} %copy.57) | copy-start | bytes 393220
  68.8 2.5 %copy-start.13 = (f32[16,64]{1,0:T(8,128)}, f32[16,64]{1,0:T(8,128)S(1)}, u32[]{:S(2)}) copy-start(f32[16,64]{1,0:T(8,128)S(1)} %get-tuple-element.143) | copy-start | bytes 12292
  68.9 2.5 %copy-start.15 = (f32[16,64]{1,0:T(8,128)}, f32[16,64]{1,0:T(8,128)S(1)}, u32[]{:S(2)}) copy-start(f32[16,64]{1,0:T(8,128)S(1)} %get-tuple-element.144) | copy-start | bytes 12292
  71.6 5.0 %copy-start.19 = (bf16[16,128]{1,0:T(8,128)(2,1)}, bf16[16,128]{1,0:T(8,128)(2,1)S(1)}, u32[]{:S(2)}) copy-start(bf16[16,128]{1,0:T(8,128)(2,1)S(1)} %select_convert_fusion.3) | copy-start | bytes 12292
  72.3 12.3 %all-to-all-start.1 = ((bf16[16,16,128]{2,1,0:T(8,128)(2,1)}), bf16[16,16,128]{2,1,0:T(8,128)(2,1)S(1)}, u32[]{:S(2)}, u32[]{:S(2)}) async-start(bf16[16,16,128]{2,1,0:T(8,128)(2,1)} %broadcast_in_dim.32), calls=%async_computation.1 | async-start | bytes 131072 | tf_op jit(solution)/shard_map/all_to_all | solution.py:152
  87.0 21.6 %collective-permute-start.1 = (bf16[16,8192]{1,0:T(8,128)(2,1)S(1)}, bf16[16,8192]{1,0:T(8,128)(2,1)S(1)}, u32[]{:S(2)}, u32[]{:S(2)}) collective-permute-start(bf16[16,8192]{1,0:T(8,128)(2,1)S(1)} %get-tuple-element.55), channel_id=1, source_target_pairs={{0,16},{1,17},{2,18},{3,19},{4,20},{5,21},{6,22},{7,23},{8,24},{9,... | collective-permute-start | bytes 786440 | tf_op jit(solution)/shard_map/ppermute | solution.py:132
  92.0 40.1 %collective-permute-start.4 = (bf16[16,8192]{1,0:T(8,128)(2,1)}, bf16[16,8192]{1,0:T(8,128)(2,1)}, u32[]{:S(2)}, u32[]{:S(2)}) collective-permute-start(bf16[16,8192]{1,0:T(8,128)(2,1)} %get-tuple-element.54), channel_id=1, source_target_pairs={{760,0},{761,1},{762,2},{763,3},{764,4},{765,5},{766,6},{767,7},{2... | collective-permute-start | bytes 786440 | tf_op jit(solution)/shard_map/ppermute | solution.py:134
  93.4 61.1 %collective-permute-start.6 = (bf16[16,8192]{1,0:T(8,128)(2,1)}, bf16[16,8192]{1,0:T(8,128)(2,1)}, u32[]{:S(2)}, u32[]{:S(2)}) collective-permute-start(bf16[16,8192]{1,0:T(8,128)(2,1)} %get-tuple-element.52), channel_id=1, source_target_pairs={{8,24},{9,25},{10,26},{11,27},{12,28},{13,29},{14,30},{15,31},{24,... | collective-permute-start | bytes 786440 | tf_op jit(solution)/shard_map/ppermute | solution.py:133
  108.6 1.8 %copy-start.7 = (bf16[16,8192]{1,0:T(8,128)(2,1)}, bf16[16,8192]{1,0:T(8,128)(2,1)S(1)}, u32[]{:S(2)}) copy-start(bf16[16,8192]{1,0:T(8,128)(2,1)S(1)} %collective-permute-done.1) | copy-start | bytes 786436
  111.5 20.7 %collective-permute-start.3 = (bf16[16,16384]{1,0:T(8,128)(2,1)}, bf16[16,16384]{1,0:T(8,128)(2,1)}, u32[]{:S(2)}, u32[]{:S(2)}) collective-permute-start(bf16[16,16384]{1,0:T(8,128)(2,1)} %pad_maximum_fusion), channel_id=1, source_target_pairs={{8,16},{9,17},{10,18},{11,19},{12,20},{13,21},{14,22},{15,23},{24,... | collective-permute-start | bytes 1572872 | tf_op jit(solution)/shard_map/ppermute | solution.py:150
  112.8 2.5 %copy-start.14 = (f32[16,64]{1,0:T(8,128)S(1)}, f32[16,64]{1,0:T(8,128)}, u32[]{:S(2)}) copy-start(f32[16,64]{1,0:T(8,128)} %copy-done.13) | copy-start | bytes 12292
  112.8 2.5 %copy-start.16 = (f32[16,64]{1,0:T(8,128)S(1)}, f32[16,64]{1,0:T(8,128)}, u32[]{:S(2)}) copy-start(f32[16,64]{1,0:T(8,128)} %copy-done.15) | copy-start | bytes 12292
  112.8 2.6 %copy-start.6 = (f32[2,8,16,128]{3,2,1,0:T(8,128)S(1)}, f32[2,8,16,128]{3,2,1,0:T(8,128)}, u32[]{:S(2)}) copy-start(f32[2,8,16,128]{3,2,1,0:T(8,128)} %copy-done.5) | copy-start | bytes 393220
  112.8 2.8 %copy-start.20 = (bf16[16,128]{1,0:T(8,128)(2,1)S(1)}, bf16[16,128]{1,0:T(8,128)(2,1)}, u32[]{:S(2)}) copy-start(bf16[16,128]{1,0:T(8,128)(2,1)} %copy-done.19) | copy-start | bytes 12292
  116.2 15.8 %all-to-all-start.2 = ((bf16[16,16,128]{2,1,0:T(8,128)(2,1)}), bf16[16,16,128]{2,1,0:T(8,128)(2,1)S(1)}, u32[]{:S(2)}, u32[]{:S(2)}) async-start(bf16[16,16,128]{2,1,0:T(8,128)(2,1)} %broadcast_in_dim.34), calls=%async_computation.2 | async-start | bytes 131072 | tf_op jit(solution)/shard_map/all_to_all | solution.py:152
  138.7 11.4 %all-to-all-start.3 = ((bf16[16,16,128]{2,1,0:T(8,128)(2,1)}), bf16[16,16,128]{2,1,0:T(8,128)(2,1)S(1)}, u32[]{:S(2)}, u32[]{:S(2)}) async-start(bf16[16,16,128]{2,1,0:T(8,128)(2,1)} %broadcast_in_dim.35), calls=%async_computation.3 | async-start | bytes 131072 | tf_op jit(solution)/shard_map/all_to_all | solution.py:152
  143.0 10.5 %collective-permute-start.5 = (bf16[16,16384]{1,0:T(8,128)(2,1)}, bf16[16,16384]{1,0:T(8,128)(2,1)}, u32[]{:S(2)}, u32[]{:S(2)}) collective-permute-start(bf16[16,16384]{1,0:T(8,128)(2,1)} %pad_maximum_fusion.1), channel_id=1, source_target_pairs={{0,24},{1,25},{2,26},{3,27},{4,28},{5,29},{6,30},{7,31},{16,40},{1... | collective-permute-start | bytes 1572872 | tf_op jit(solution)/shard_map/ppermute | solution.py:150
  154.5 2.3 %copy-start.3 = (bf16[16,8192]{1,0:T(8,128)(2,1)}, bf16[16,8192]{1,0:T(8,128)(2,1)S(1)}, u32[]{:S(2)}) copy-start(bf16[16,8192]{1,0:T(8,128)(2,1)S(1)} %slice_select_fusion) | copy-start | bytes 786436
  157.2 18.2 %copy-start.10 = (f32[4,4,16,128]{3,2,1,0:T(8,128)S(1)}, f32[4,4,16,128]{3,2,1,0:T(8,128)}, u32[]{:S(2)}) copy-start(f32[4,4,16,128]{3,2,1,0:T(8,128)} %copy-done.9) | copy-start | bytes 393220
  157.2 19.5 %copy-start.4 = (bf16[16,8192]{1,0:T(8,128)(2,1)S(1)}, bf16[16,8192]{1,0:T(8,128)(2,1)}, u32[]{:S(2)}) copy-start(bf16[16,8192]{1,0:T(8,128)(2,1)} %copy-done.3) | copy-start | bytes 786436
  157.2 19.5 %copy-start.2 = (bf16[16,8192]{1,0:T(8,128)(2,1)S(1)}, bf16[16,8192]{1,0:T(8,128)(2,1)}, u32[]{:S(2)}) copy-start(bf16[16,8192]{1,0:T(8,128)(2,1)} %copy-done.1) | copy-start | bytes 786436
  160.3 14.9 %all-to-all-start.4 = ((bf16[16,2,128]{2,1,0:T(2,128)(2,1)}), bf16[16,2,128]{2,1,0:T(2,128)(2,1)S(1)}, u32[]{:S(2)}, u32[]{:S(2)}) async-start(bf16[16,2,128]{2,1,0:T(2,128)(2,1)} %copy.53), calls=%async_computation.4 | async-start | bytes 16384 | tf_op jit(solution)/shard_map/all_to_all | solution.py:169
  167.8 7.7 %collective-permute-start.7 = (bf16[2,16384]{1,0:T(2,128)(2,1)S(1)}, bf16[2,16384]{1,0:T(2,128)(2,1)S(1)}, u32[]{:S(2)}, u32[]{:S(2)}) collective-permute-start(bf16[2,16384]{1,0:T(2,128)(2,1)S(1)} %pad_maximum_fusion.3), channel_id=1, source_target_pairs={{0,8},{8,0},{1,9},{9,1},{2,10},{10,2},{3,11},{11,3},{4,12},{12,4},... | collective-permute-start | bytes 196616 | tf_op jit(solution)/shard_map/ppermute | solution.py:168
  (3 other events, 2.4 us)

commit v2 on v1

v2 whole, which is shorter than its diff:
```python
import functools

import jax
import jax.numpy as jnp
import numpy as np
from jax import lax
from jax.experimental import pallas as pl
from jax.experimental.pallas import tpu as pltpu
from jax.sharding import PartitionSpec as P

QH = 64
KVH = 4
HD = 128
PER = QH // KVH
ALL = ("section", "row", "col")
RC = ("row", "col")
FACTOR = 1.0 / np.sqrt(HD)
bf16 = jnp.bfloat16
f32 = jnp.float32


def angles(positions):
    half = HD // 2
    steps_up = jnp.arange(half).astype(f32)
    inverse = jnp.exp(-jnp.log(f32(500000.0)) * steps_up / half)
    angle = positions.astype(f32)[:, None] * inverse[None, :]
    cosine = jnp.cos(angle)
    sine = jnp.sin(angle)
    return jnp.concatenate([cosine, cosine], 1), jnp.concatenate([-sine, sine], 1)


def attend(qs, k_ref, v_ref, lens, scores, ticks):
    for i, t in enumerate(ticks):
        for g in range(KVH):
            q = qs[t * QH + g * PER : t * QH + (g + 1) * PER, :].astype(bf16)
            k = k_ref[i, :, g * HD : (g + 1) * HD]
            scores[i * QH + g * PER : i * QH + (g + 1) * PER, :] = lax.dot_general(
                q, k, (((1,), (1,)), ((), ())), preferred_element_type=f32
            )
    means, lses = [], []
    lane = lax.broadcasted_iota(jnp.int32, (QH, HD), 1)
    for i, t in enumerate(ticks):
        part = scores[i * QH : (i + 1) * QH, :] * FACTOR
        part = jnp.where(lane < lens[t], part, f32(-1e30))
        top = jnp.max(part, axis=1, keepdims=True)
        weights = jnp.exp(part - top)
        total = jnp.sum(weights, axis=1, keepdims=True)
        probs = (weights / total).astype(bf16)
        lses.append(top + jnp.log(total))
        for g in range(KVH):
            v = v_ref[i, :, g * HD : (g + 1) * HD]
            means.append(jnp.dot(probs[g * PER : (g + 1) * PER], v, preferred_element_type=f32))
    return means, lses


def spread(lse, tick):
    hi = lse.astype(bf16).astype(f32)
    mid = (lse - hi).astype(bf16).astype(f32)
    low = (lse - hi) - mid
    lane = lax.broadcasted_iota(jnp.int32, (PER, HD), 1)
    row = lax.broadcasted_iota(jnp.int32, (PER, HD), 0)
    out = []
    for g in range(KVH):
        total = jnp.zeros((PER, HD), f32)
        for p, part in enumerate((hi, mid, low)):
            there = lane == row + (16 + 48 * (tick // 2) + 16 * p)
            total = total + jnp.where(there, part[g * PER : (g + 1) * PER], 0.0)
        out.append(jnp.sum(total, axis=0, keepdims=True))
    return out


def first_kernel(lens, q_ref, k_ref, v_ref, mean_ref, fed_ref, aux_ref, qs, scores):
    for h in range(QH):
        qs[pl.ds(h, 4, stride=QH), :] = q_ref[:, h * HD : (h + 1) * HD].astype(f32)
    means, lses = attend(qs, k_ref, v_ref, lens, scores, (0, 1, 2))
    for n, mean in enumerate(means):
        mean_ref[n * PER : (n + 1) * PER, :] = mean
        fed_ref[n * PER : (n + 1) * PER, :] = mean.astype(bf16)
    even, odd, late = (spread(lses[t], t) for t in (0, 1, 2))
    for g in range(KVH):
        aux_ref[g : g + 1, :] = even[g] + late[g]
        aux_ref[KVH + g : KVH + g + 1, :] = odd[g]


def second_kernel(lens, pick, q_ref, k_ref, v_ref, row_ref, ent_ref, aux_in, mean_ref, own_ref, tail_ref, head_ref, ask_ref, aux_ref, qs, scores, wide, ents):
    blocks = 2 * QH
    for h in range(QH):
        qs[pl.ds(h, 4, stride=QH), :] = q_ref[:, h * HD : (h + 1) * HD].astype(f32)
    for a in range(blocks):
        wide[a : a + 1, :] = row_ref[:, a * HD : (a + 1) * HD].astype(f32)
        ents[pl.ds(a, 3, stride=blocks), :] = ent_ref[:, a * HD : (a + 1) * HD].astype(f32)
    ask_ref[...] = qs[...].astype(bf16)
    own_ref[...] = wide[...].astype(bf16)
    chosen = pl.multiple_of(pick[0] * blocks + QH, QH)
    tail_ref[...] = ents[pl.ds(chosen, QH), :].astype(bf16)
    for t in range(3):
        head_ref[t * QH : (t + 1) * QH, :] = ents[t * blocks : t * blocks + QH, :].astype(bf16)
    means, lses = attend(qs, k_ref, v_ref, lens, scores, (3,))
    for n, mean in enumerate(means):
        mean_ref[n * PER : (n + 1) * PER, :] = mean
    late = spread(lses[0], 3)
    lane = lax.broadcasted_iota(jnp.int32, (1, HD), 1)
    for r in range(2):
        known = jnp.where(lane == 0, lens[r].astype(f32), 0.0)
        known = known + jnp.where(lane == 1, lens[2 + r].astype(f32), 0.0)
        for g in range(KVH):
            n = r * KVH + g
            row = aux_in[n : n + 1, :] + known
            aux_ref[n : n + 1, :] = row + late[g] if r else row


def third_kernel(flags, fed_ref, head_ref, own_ref, tail_ref, ask_ref, aux_ref, send_ref):
    first = jnp.full((3 * QH, HD), flags[0], jnp.int32) > 0
    fed = jnp.where(first, head_ref[...].astype(f32), fed_ref[...].astype(f32)).astype(bf16)
    own = own_ref[...]
    tail = tail_ref[...]
    pad = jnp.zeros((8, HD), f32)
    sub = lax.broadcasted_iota(jnp.int32, (8, HD), 0)
    for g in range(KVH):
        for r in range(2):
            aux = jnp.where(sub == 0, jnp.broadcast_to(aux_ref[r * KVH + g : r * KVH + g + 1, :], (8, HD)), pad)
            asks = [ask_ref[t * QH + g * PER : t * QH + (g + 1) * PER, :] for t in (r, 2 + r)]
            for c in (2 * g, 2 * g + 1):
                d = 8 * r + c
                if r == 0:
                    send_ref[d, : 2 * QH, :] = own
                    send_ref[d, 2 * QH : 3 * QH, :] = fed[QH : 2 * QH]
                else:
                    send_ref[d, :QH, :] = fed[2 * QH :]
                    send_ref[d, QH : 2 * QH, :] = tail
                    send_ref[d, 2 * QH : 3 * QH, :] = fed[:QH]
                send_ref[d, 3 * QH : 3 * QH + PER, :] = asks[0]
                send_ref[d, 3 * QH + PER : 3 * QH + 2 * PER, :] = asks[1]
                send_ref[d, 3 * QH + 2 * PER :, :] = aux.astype(bf16)


def prepare(queries, keys, values, row, entering, lens, pick, first, shift):
    slots, kept = keys.shape[1], KVH * HD
    held = pl.BlockSpec(memory_space=pltpu.VMEM)
    small = pl.BlockSpec(memory_space=pltpu.SMEM)

    def cost(n):
        return pl.CostEstimate(flops=n, bytes_accessed=n, transcendentals=0)

    mean, fed, aux = pl.pallas_call(
        first_kernel,
        grid=(1,),
        out_shape=(
            jax.ShapeDtypeStruct((3 * QH, HD), f32),
            jax.ShapeDtypeStruct((3 * QH, HD), bf16),
            jax.ShapeDtypeStruct((2 * KVH, HD), f32),
        ),
        in_specs=[small, held, *[pl.BlockSpec((3, slots, kept), lambda i: (0, 0, 0))] * 2],
        out_specs=(held, held, held),
        scratch_shapes=[pltpu.VMEM((4 * QH, HD), f32), pltpu.VMEM((3 * QH, slots), f32)],
        cost_estimate=cost(4 << 20),
        compiler_params=pltpu.CompilerParams(vmem_limit_bytes=8 << 20),
        name="first_part",
    )(lens, queries, keys, values)
    fed = shift(fed)
    late, own, tail, head, ask, aux = pl.pallas_call(
        second_kernel,
        grid=(1,),
        out_shape=(
            jax.ShapeDtypeStruct((QH, HD), f32),
            jax.ShapeDtypeStruct((2 * QH, HD), bf16),
            jax.ShapeDtypeStruct((QH, HD), bf16),
            jax.ShapeDtypeStruct((3 * QH, HD), bf16),
            jax.ShapeDtypeStruct((4 * QH, HD), bf16),
            jax.ShapeDtypeStruct((2 * KVH, HD), f32),
        ),
        in_specs=[small, small, held, *[pl.BlockSpec((1, slots, kept), lambda i: (3, 0, 0))] * 2, held, held, held],
        out_specs=(held,) * 6,
        scratch_shapes=[
            pltpu.VMEM((4 * QH, HD), f32),
            pltpu.VMEM((QH, slots), f32),
            pltpu.VMEM((2 * QH, HD), f32),
            pltpu.VMEM((6 * QH, HD), f32),
        ],
        cost_estimate=cost(16 << 20),
        compiler_params=pltpu.CompilerParams(vmem_limit_bytes=8 << 20),
        name="second_part",
    )(lens, pick, queries, keys, values, row, entering, aux)
    sent = pl.pallas_call(
        third_kernel,
        out_shape=jax.ShapeDtypeStruct((16, 3 * QH + 2 * PER + 8, HD), bf16),
        in_specs=[small, held, held, held, held, held, held],
        out_specs=held,
        cost_estimate=cost(1 << 20),
        compiler_params=pltpu.CompilerParams(vmem_limit_bytes=8 << 20),
        name="third_part",
    )(first, fed, head, own, tail, ask, aux)
    return sent, mean, late


def tick_kernel(tick, *refs):
    combined = tick > 0
    flags, a_ref, b_ref, ask_ref, aux_ref, turn_ref, gain_ref, here_ref, there_ref = refs[:9]
    refs = refs[9:]
    if combined:
        heard_ref, mean_ref, extra_ref = refs[:3]
        refs = refs[3:]
    x_ref, message_ref, scaled = refs
    half = QH * HD
    rows = x_ref.shape[0]
    first = jnp.full((rows, HD), flags[2], jnp.int32) > 0
    lane = lax.broadcasted_iota(jnp.int32, (rows, HD), 1)
    square = jnp.zeros((rows, HD), f32)
    for n in range(2 * QH):
        h = n % QH
        at = slice(h * HD, (h + 1) * HD)
        if n < QH:
            x = a_ref[:, at]
            if combined:
                if h % PER == 0:
                    g = h // PER
                    own = jnp.where(first, 0.0, heard_ref[2 * g].astype(f32))
                    new = heard_ref[2 * g + 1].astype(f32)
                mean = mean_ref[:, at].astype(f32)
                weight = own[:, h % PER : h % PER + 1]
                x = (x.astype(f32) + (mean + weight * (new - mean))).astype(bf16)
        else:
            x = b_ref[:, at]
            if combined:
                x = jnp.where(first, extra_ref[:, at].astype(f32), x.astype(f32)).astype(bf16)
        x_ref[:, n * HD : (n + 1) * HD] = x
        wide = x.astype(f32)
        square = square + wide * wide
        scaled[n // QH, :, at] = (wide * gain_ref[:, n * HD : (n + 1) * HD].astype(f32)).astype(bf16)
    fresh = jnp.zeros((rows, HD), f32)
    step = 2048
    for ref, part in ((here_ref, flags[0]), (there_ref, 1 - flags[0])):
        for k in range(0, half, step):
            fresh = fresh + jnp.dot(scaled[part, :, k : k + step], ref[k : k + step, :], preferred_element_type=f32)
    scale = lax.rsqrt(jnp.sum(square, axis=1, keepdims=True) / (2 * half) + 1e-05)
    fresh = fresh * scale
    key = fresh * turn_ref[0] + pltpu.roll(fresh, HD // 2, 1) * turn_ref[1]
    key = key.astype(bf16).astype(f32)
    score = jnp.zeros((rows, HD), f32)
    for i in range(PER):
        one = jnp.sum(ask_ref[:, i * HD : (i + 1) * HD].astype(f32) * key, axis=1, keepdims=True)
        score = jnp.where(lane == i, one, score)
    aux = aux_ref[:, :HD].astype(f32)
    lse = jnp.zeros((rows, HD), f32)
    for p in range(3):
        lse = lse + pltpu.roll(aux, HD - (16 + 48 * (tick // 2) + 16 * p), 1)
    own = jnp.where(lane < PER, 1.0 / (1.0 + jnp.exp(lse - score * FACTOR)), 0.0)
    is_key = jnp.full((rows, HD), flags[1], jnp.int32) > 0
    message = jnp.where(is_key, own, fresh).astype(bf16)
    for d in range(message_ref.shape[0]):
        message_ref[d] = message


def do_tick(tick, flags, x, got, turn, gain, here, there, heard=None, extra=None):
    rows, half = got.shape[0], QH * HD
    small = pl.BlockSpec(memory_space=pltpu.SMEM)
    held = pl.BlockSpec(memory_space=pltpu.VMEM)

    def block(size, n):
        return pl.BlockSpec((rows, size), lambda i: (0, n))

    k = tick // 2
    specs = [small, block(half, 0), block(half, 1), block(PER * HD, 12 + k), block(8 * HD, 28), held, held, held, held]
    operands = [flags, x, x, got, got, turn, gain, here, there]
    if tick:
        specs += [held, block(half, 0 if tick == 3 else 2), held if tick > 1 else block(half, 1)]
        operands += [heard, got, extra]
    return pl.pallas_call(
        functools.partial(tick_kernel, tick),
        grid=(1,),
        out_shape=(
            jax.ShapeDtypeStruct((rows, 2 * half), bf16),
            jax.ShapeDtypeStruct((rows, rows, HD), bf16),
        ),
        in_specs=specs,
        out_specs=(held, held),
        scratch_shapes=[pltpu.VMEM((2, rows, half), bf16)],
        cost_estimate=pl.CostEstimate(flops=1 << 26, bytes_accessed=6 << 20, transcendentals=0),
        compiler_params=pltpu.CompilerParams(vmem_limit_bytes=20 << 20),
        name=f"tick_{tick}",
    )(*operands)


def pick_kernel(flags, a_ref, b_ref, mine_ref, other_ref):
    rows, width = a_ref.shape
    sub = lax.broadcasted_iota(jnp.int32, (8, rows), 0)
    lane = lax.broadcasted_iota(jnp.int32, (8, rows), 1)
    wanted = jnp.where(sub == 0, flags[0] * 8 + flags[3], (1 - flags[0]) * 8 + flags[3])
    select = jnp.where((lane == wanted) & (sub < 2), 1.0, 0.0).astype(bf16)
    for r, ref in enumerate((a_ref, b_ref)):

        @pl.when(flags[0] == r)
        def _():
            for k in range(0, width, 2048):
                both = jnp.dot(select, ref[:, k : k + 2048], preferred_element_type=f32)
                mine_ref[:, k : k + 2048] = both[0:1].astype(bf16)
                other_ref[:, k : k + 2048] = both[1:2].astype(bf16)


def pick_rows(flags, a, b):
    held = pl.BlockSpec(memory_space=pltpu.VMEM)
    row = jax.ShapeDtypeStruct((1, a.shape[1]), bf16)
    return pl.pallas_call(
        pick_kernel,
        out_shape=(row, row),
        in_specs=[pl.BlockSpec(memory_space=pltpu.SMEM), held, held],
        out_specs=(held, held),
        cost_estimate=pl.CostEstimate(flops=1 << 20, bytes_accessed=2 << 20, transcendentals=0),
        compiler_params=pltpu.CompilerParams(vmem_limit_bytes=8 << 20),
        name="pick_rows",
    )(flags, a, b)


def last_kernel(row_ref, told_ref, early_ref, late_ref, out_ref, tell, mean):
    half = QH * HD
    mean[: 3 * QH, :] = early_ref[...]
    mean[3 * QH :, :] = late_ref[...]
    for c in range(8):
        for r in range(2):
            for k in range(2):
                t = 2 * k + r
                tell[c, t : t + 1, :] = told_ref[8 * r + c, k : k + 1, :].astype(f32)
    for h in range(QH):
        g, i = h // PER, h % PER
        at = slice(h * HD, (h + 1) * HD)
        cached = mean[pl.ds(h, 4, stride=QH), :]
        own = tell[2 * g][:, i : i + 1]
        mixed = cached + own * (tell[2 * g + 1] - cached)
        out_ref[:, at] = (row_ref[:, at].astype(f32) + mixed).astype(bf16)
    out_ref[:, half:] = row_ref[:, half:]


def finish(row, told, early, late):
    held = pl.BlockSpec(memory_space=pltpu.VMEM)
    return pl.pallas_call(
        last_kernel,
        out_shape=jax.ShapeDtypeStruct(row.shape, bf16),
        in_specs=[held] * 4,
        out_specs=held,
        scratch_shapes=[pltpu.VMEM((8, 4, HD), f32), pltpu.VMEM((4 * QH, HD), f32)],
        cost_estimate=pl.CostEstimate(flops=1 << 20, bytes_accessed=1 << 20, transcendentals=0),
        compiler_params=pltpu.CompilerParams(vmem_limit_bytes=8 << 20),
        name="last_part",
    )(row, told, early, late)


def per_device(arriving, entering, gain, kv_weight, queries, cache_keys, cache_values, lengths):
    section_at = lax.axis_index("section")
    row_at = lax.axis_index("row")
    col_at = lax.axis_index("col")
    sections = lax.axis_size("section")
    cols = lax.axis_size("col")
    ticks = queries.shape[1]
    width = arriving.shape[2]
    half = width // 2
    last = section_at == sections - 1
    first = section_at == 0

    def at(s, r, c):
        return ((s % sections) * 2 + r) * cols + c

    def links(pairs):
        return [(at(s, r, c), at(v, w, c)) for s, r, v, w in pairs for c in range(cols)]

    def relay_group(r):
        return [
            [at(s, r, c) for c in range(cols)] + [at(s + 1, 1 - r, c) for c in range(cols)]
            for s in range(sections)
        ]

    w_here = kv_weight[0]
    w_there = lax.ppermute(w_here, "row", [(0, 1), (1, 0)])
    lens = lax.dynamic_slice_in_dim(lengths[:, 0], sections - 1 - section_at, ticks, 0)
    pick = jnp.where(first, 0, jnp.where(last, 1, 2)).astype(jnp.int32)[None]
    sent, early, late = prepare(
        queries[0, :, 0],
        cache_keys[0, :, 0],
        cache_values[0, :, 0],
        arriving[0],
        entering[:, 0],
        lens,
        pick,
        first.astype(jnp.int32)[None],
        lambda fed: lax.ppermute(fed, "section", [(s, s + 1) for s in range(sections - 1)]),
    )
    got = lax.all_to_all(sent, RC, split_axis=0, concat_axis=0, tiled=True)
    got = got.reshape(2 * cols, -1)

    tails = lax.ppermute(got[:, half:width], ALL, links([(sections - 1, 1, 0, 0), (1, 1, 0, 1)]))
    aux_at = width + half + 2 * PER * HD
    turns = [jnp.stack(angles(got[:, aux_at + k].astype(f32))) for k in range(2)]
    flags = jnp.stack([row_at, 1 - col_at % 2, first.astype(jnp.int32), col_at]).astype(jnp.int32)

    rows, messages = [], []
    for tick in range(ticks):
        step = functools.partial(do_tick, tick, flags, got=got, turn=turns[tick // 2], gain=gain, here=w_here, there=w_there)
        if tick == 0:
            x, message = step(got)
        else:
            there = (tick - 1) % 2
            relayed = lax.ppermute(x, ALL, links([(s, there, s + 1, 1 - there) for s in range(sections - 1)]))
            heard = lax.all_to_all(message, ALL, split_axis=0, concat_axis=0, axis_index_groups=relay_group(there), tiled=True)
            x, message = step(relayed, heard=heard, extra=got if tick == 1 else tails)
        rows.append(x)
        messages.append(message[0])

    told, mine, swapped = [], [], []
    for k in range(2):
        here, other = pick_rows(flags, rows[2 * k], rows[2 * k + 1])
        mine.append(here)
        swapped.append(lax.ppermute(other, "row", [(0, 1), (1, 0)]))
        told.append(jnp.where(row_at == 0, messages[2 * k], messages[2 * k + 1]))
    told = lax.all_to_all(jnp.stack(told, 1), RC, split_axis=0, concat_axis=0, tiled=True)
    pairs = [[jnp.where(row_at == r, mine[k], swapped[k]) for r in range(2)] for k in range(2)]
    out = finish(jnp.concatenate(pairs[0] + pairs[1], 0), told, early, late)
    return out[None, :, None]


def solution(mesh):
    placed = (
        P("section", ("row", "col"), None),
        P(None, ("row", "col"), None),
        P("section", None),
        P("section", "row", "col"),
        P("section", None, ("row", "col"), None),
        P("section", None, ("row", "col"), None, None),
        P("section", None, ("row", "col"), None, None),
        P(None, ("row", "col")),
    )
    return jax.shard_map(
        per_device,
        mesh=mesh,
        in_specs=placed,
        out_specs=P("section", None, ("row", "col"), None),
        check_vma=False,
    )
```

time: 181 us -> 149 us (0.82)
  waiting for transfers between devices: 60.1 us -> 38.7 us
  Pallas kernels: 0 us -> 19.1 us
  local copies, waits for them, and re-layouts: 34.4 us -> 17.1 us
  blocking collectives: 0 us -> 13.6 us
  other arithmetic: 18.5 us -> 5.55 us
  matrix products: 10.3 us -> 0 us
    pallas_call x0 -> x10, Pallas kernels: none -> 19.1 us  [the longest x4 12 us: do_tick(): pl.pallas_call(functools.partial(tick_kernel, tick), grid=(1,), out_shape...]
    all_to_all x3 -> x2, waiting for transfers between devices: 16.8 us -> 2.89 us  [per_device(): lax.all_to_all(message, ALL, split_axis=0, concat_axis=0, axis_index_grou...]
    all_to_all x0 -> x1, blocking collectives: none -> 13.6 us  [per_device(): lax.all_to_all(message, ALL, split_axis=0, concat_axis=0, axis_index_grou...]
    concatenate x16 -> x0, local copies, waits for them, and re-layouts: 10.9 us -> none  [the longest x8 10.8 us: block(): aux = jnp.concatenate(aux)]
    dot_general x10 -> x0, matrix products: 10.3 us -> none  [the longest x4 7.98 us: project(): fresh = fresh + jnp.dot(other, w_there, preferred_element_type=f32)]
    ppermute x3, waiting for transfers between devices: 13.8 us -> 6.09 us  [the longest x1 6.08 us: per_device(): lax.ppermute(fed, 'section', [(s, s + 1) for s in range(sections - 1)])]
    ppermute x3, starting transfers between devices: 7.95 us -> 14.1 us  [the longest x2 9.88 us: per_device(): swapped.append(lax.ppermute(other, 'row', [(0, 1), (1, 0)]))]
    another operation x30 -> x0, local copies, waits for them, and re-layouts: 5.73 us -> none  [the longest x16 1.34 us: block(): aux += [parts[t, :, g].reshape(-1) for t in slots]]
  transfers between devices with their start and end apart: 13 -> 12, of which waited for: 7 -> 6; matrix products, arithmetic and copies ran while one was open for 13% -> 5% of each run, Pallas kernels for 0% -> 4%
where the time goes in v2:
time: 149 us; the launch traced here: 148 us
  starting transfers between devices  53.7 us (36%)
  waiting for transfers between devices  38.7 us (26%)
  Pallas kernels  19.1 us (13%)
  local copies, waits for them, and re-layouts  17.1 us (11%)
  blocking collectives  13.6 us (9%)
  other arithmetic  5.55 us (4%)
    all_to_all x1, waiting for transfers between devices, per_device(): got = lax.all_to_all(sent, RC, split_axis=0, concat_axis=0, tiled=True)  21.1 us
    unnamed x47, local copies, waits for them, and re-layouts  16.3 us
    all_to_all x2, starting transfers between devices, per_device(): lax.all_to_all(message, ALL, split_axis=0, concat_axis=0, axis_index_grou...  15.5 us
    all_to_all x1, blocking collectives, per_device(): lax.all_to_all(message, ALL, split_axis=0, concat_axis=0, axis_index_grou...  13.6 us
    pallas_call x4, Pallas kernels, do_tick(): pl.pallas_call(functools.partial(tick_kernel, tick), grid=(1,), out_shape...  12 us
    ppermute x2, starting transfers between devices, per_device(): swapped.append(lax.ppermute(other, 'row', [(0, 1), (1, 0)]))  9.88 us
    all_to_all x1, starting transfers between devices, per_device(): got = lax.all_to_all(sent, RC, split_axis=0, concat_axis=0, tiled=True)  7.34 us
    ppermute x3, starting transfers between devices, per_device(): lax.ppermute(x, ALL, links([(s, there, s + 1, 1 - there) for s in range(s...  6.95 us
  transfers between devices with their start and end apart: 12, of which 6 were waited for; matrix products, arithmetic and copies ran while one was open for 5% of the time, Pallas kernels for 4%

profile of v2, /device:TPU:6, one launch (start us, length us, event | category | flops | bytes accessed | tf_op | source)
XLA Modules:
  0.0 148.1 jit_solution(16454518584551144976)
XLA Ops:
  0.7 1.0 copy-done.2
  1.8 1.0 copy-done.4
  3.7 1.2 first_part.1
  5.5 4.3 %collective-permute-start = (bf16[192,128]{1,0:T(8,128)(2,1)S(1)}, bf16[192,128]{1,0:T(8,128)(2,1)S(1)}, u32[]{:S(2)}, u32[]{:S(2)}) collective-permute-start(bf16[192,128]{1,0:T(8,128)(2,1)S(1)} %get-tuple-element.26), channel_id=1, source_target_pairs={{0,16},{16,32},{32,48},{48,64},{64,80},{80,96},{96,112},{112,128},... | collective-permute-start | bytes 147464 | tf_op jit(solution)/shard_map/ppermute | solution.py:384
  10.8 1.0 copy-done.5
  14.4 1.2 second_part.1
  16.3 6.1 %collective-permute-done.fed_ref = bf16[192,128]{1,0:T(8,128)(2,1)S(1)} collective-permute-done((bf16[192,128]{1,0:T(8,128)(2,1)S(1)}, bf16[192,128]{1,0:T(8,128)(2,1)S(1)}, u32[]{:S(2)}, u32[]{:S(2)}) %collective-permute-start) | collective-permute-done | bytes 49184 | tf_op jit(solution)/shard_map/ppermute | solution.py:384
  22.4 1.0 third_part.1
  23.4 7.3 %all-to-all-start = ((bf16[16,232,128]{2,1,0:T(8,128)(2,1)}), bf16[16,232,128]{2,1,0:T(8,128)(2,1)S(1)}, u32[]{:S(2)}, u32[]{:S(2)}) async-start(bf16[16,232,128]{2,1,0:T(8,128)(2,1)} %third_part.1), calls=%async_computation | async-start | bytes 1900544 | tf_op jit(solution)/shard_map/all_to_all | solution.py:386
  30.8 2.3 %collective-permute-start.1 = (bf16[8192,128]{1,0:T(8,128)(2,1)S(1)}, bf16[8192,128]{1,0:T(8,128)(2,1)}, u32[]{:S(2)}, u32[]{:S(2)}) collective-permute-start(bf16[8192,128]{1,0:T(8,128)(2,1)S(1)} %bitcast.46), channel_id=1, source_target_pairs={{0,8},{8,0},{1,9},{9,1},{2,10},{10,2},{3,11},{11,3},{4,12},{12,4},... | collective-permute-start | bytes 6291464 | tf_op jit(solution)/shard_map/ppermute | solution.py:372
  33.2 21.1 %all-to-all-done = bf16[16,232,128]{2,1,0:T(8,128)(2,1)S(1)} async-done(((bf16[16,232,128]{2,1,0:T(8,128)(2,1)}), bf16[16,232,128]{2,1,0:T(8,128)(2,1)S(1)}, u32[]{:S(2)}, u32[]{:S(2)}) %all-to-all-start) | async-done | bytes 950304 | tf_op jit(solution)/shard_map/all_to_all | solution.py:386
  55.2 1.3 copy.15
  57.0 2.8 %tick_0.1 = (bf16[16,16384]{1,0:T(8,128)(2,1)S(1)}, bf16[16,16,128]{2,1,0:T(8,128)(2,1)S(1)}) custom-call(s32[4]{0:T(128)S(1)} %pad_add_fusion.refs_0_.flags, bf16[16,29696]{1,0:T(8,128)(2,1)S(1)} %bitcast.31, bf16[16,29696]{1,0:T(8,128)(2,1)S(1)} %bitcast.32, bf16[16,29696]{1,0:T(8,128)(2,1)S(1)} %bitcast.33, bf16[16,29696]{1,0:T(8,128)(2,1)S(1)} %bitcast.34, ...), custom_call_target="tpu_custom_call" | custom-call | flops 67108864 | bytes 6291456 | tf_op jit(solution)/shard_map/tick_0/pallas_call | solution.py:268
  59.7 1.3 collective-permute-start.2
  61.1 13.6 %all_to_all.25.refs_9_ = bf16[16,16,128]{2,1,0:T(8,128)(2,1)S(1)} all-to-all(bf16[16,16,128]{2,1,0:T(8,128)(2,1)S(1)} %get-tuple-element.34), channel_id=1, replica_groups={{0,1,2,3,4,5,6,7,24,25,26,27,28,29,30,31},{16,17,18,19,20,21,22,23,40,4..., dimensions={0} | all-to-all | bytes 131072 | tf_op jit(solution)/shard_map/all_to_all | solution.py:402
  74.6 3.0 %tick_1.1 = (bf16[16,16384]{1,0:T(8,128)(2,1)}, bf16[16,16,128]{2,1,0:T(8,128)(2,1)S(1)}) custom-call(s32[4]{0:T(128)S(1)} %pad_add_fusion.refs_0_.flags, bf16[16,16384]{1,0:T(8,128)(2,1)S(1)} %collective-permute-done.2.refs_1_.refs_2_, bf16[16,16384]{1,0:T(8,128)(2,1)S(1)} %collective-permute-done.2.refs_1_.refs_2_, bf16[16,29696]{1,0:T(8,128)(2,1)S(1)} %bitcast.35, ...), custom_call_target="tpu_custom_call" | custom-call | flops 67108864 | bytes 6291456 | tf_op jit(solution)/shard_map/tick_1/pallas_call | solution.py:268
  78.3 1.3 collective-permute-start.4
  81.0 9.7 %all-to-all-start.2 = ((bf16[16,16,128]{2,1,0:T(8,128)(2,1)}), bf16[16,16,128]{2,1,0:T(8,128)(2,1)S(1)}, u32[]{:S(2)}, u32[]{:S(2)}) async-start(bf16[16,16,128]{2,1,0:T(8,128)(2,1)} %copy-done.16), calls=%async_computation.2 | async-start | bytes 131072 | tf_op jit(solution)/shard_map/all_to_all | solution.py:402
  90.7 1.0 copy-done.8
  91.8 2.0 %pick_rows.2 = (bf16[1,16384]{1,0:T(2,128)(2,1)S(1)}, bf16[1,16384]{1,0:T(2,128)(2,1)}) custom-call(s32[4]{0:T(128)S(1)} %pad_add_fusion.refs_0_.flags, bf16[16,16384]{1,0:T(8,128)(2,1)S(1)} %copy-done.8, bf16[16,16384]{1,0:T(8,128)(2,1)} %get-tuple-element.35.b_ref), custom_call_target="tpu_custom_call" | custom-call | flops 1048576 | bytes 2097152 | tf_op jit(solution)/shard_map/pick_rows/pallas_call | solution.py:303
  94.3 1.9 %collective-permute-start.3 = (bf16[1,16384]{1,0:T(2,128)(2,1)}, bf16[1,16384]{1,0:T(2,128)(2,1)}, u32[]{:S(2)}, u32[]{:S(2)}) collective-permute-start(bf16[1,16384]{1,0:T(2,128)(2,1)} %get-tuple-element.37), channel_id=1, source_target_pairs={{0,8},{8,0},{1,9},{9,1},{2,10},{10,2},{3,11},{11,3},{4,12},{12,4},... | collective-permute-start | bytes 98312 | tf_op jit(solution)/shard_map/ppermute | solution.py:411
  97.9 3.1 %tick_2.1 = (bf16[16,16384]{1,0:T(8,128)(2,1)S(1)}, bf16[16,16,128]{2,1,0:T(8,128)(2,1)S(1)}) custom-call(s32[4]{0:T(128)S(1)} %pad_add_fusion.refs_0_.flags, bf16[16,16384]{1,0:T(8,128)(2,1)} %collective-permute-done.4.refs_1_.refs_2_, bf16[16,16384]{1,0:T(8,128)(2,1)} %collective-permute-done.4.refs_1_.refs_2_, bf16[16,29696]{1,0:T(8,128)(2,1)S(1)} %bitcast.40, ...), custom_call_target="tpu_custom_call" | custom-call | flops 67108864 | bytes 6291456 | tf_op jit(solution)/shard_map/tick_2/pallas_call | solution.py:268
  102.5 5.8 %all-to-all-start.3 = ((bf16[16,16,128]{2,1,0:T(8,128)(2,1)}), bf16[16,16,128]{2,1,0:T(8,128)(2,1)S(1)}, u32[]{:S(2)}, u32[]{:S(2)}) async-start(bf16[16,16,128]{2,1,0:T(8,128)(2,1)} %copy-done.17), calls=%async_computation.3 | async-start | bytes 131072 | tf_op jit(solution)/shard_map/all_to_all | solution.py:402
  108.3 4.4 %collective-permute-start.6 = (bf16[16,16384]{1,0:T(8,128)(2,1)}, bf16[16,16384]{1,0:T(8,128)(2,1)}, u32[]{:S(2)}, u32[]{:S(2)}) collective-permute-start(bf16[16,16384]{1,0:T(8,128)(2,1)} %copy-done.9), channel_id=1, source_target_pairs={{0,24},{1,25},{2,26},{3,27},{4,28},{5,29},{6,30},{7,31},{16,40},{1... | collective-permute-start | bytes 1572872 | tf_op jit(solution)/shard_map/ppermute | solution.py:401
  112.7 1.7 %broadcast_select_fusion.3 = (bf16[1,16384]{1,0:T(2,128)(2,1)}, bf16[1,16384]{1,0:T(2,128)(2,1)}) fusion(bf16[1,16384]{1,0:T(2,128)(2,1)} %copy-done.19, bf16[1,16384]{1,0:T(2,128)(2,1)} %collective-permute-done.3, pred[]{:T(512)S(6)} %eq.18, pred[]{:T(512)S(6)} %eq.21), kind=kLoop, calls=%fused_computation.5 | loop fusion | flops 32768 | bytes 131074 | tf_op jit(solution)/shard_map/jit(_where)/select_n | solution.py:414
  114.4 1.9 %all-to-all-done.3.refs_9_ = bf16[16,16,128]{2,1,0:T(8,128)(2,1)S(1)} async-done(((bf16[16,16,128]{2,1,0:T(8,128)(2,1)}), bf16[16,16,128]{2,1,0:T(8,128)(2,1)S(1)}, u32[]{:S(2)}, u32[]{:S(2)}) %all-to-all-start.3) | async-done | bytes 65568 | tf_op jit(solution)/shard_map/all_to_all | solution.py:402
  116.3 2.6 %collective-permute-done.6.refs_1_.refs_2_ = bf16[16,16384]{1,0:T(8,128)(2,1)} collective-permute-done((bf16[16,16384]{1,0:T(8,128)(2,1)}, bf16[16,16384]{1,0:T(8,128)(2,1)}, u32[]{:S(2)}, u32[]{:S(2)}) %collective-permute-start.6) | collective-permute-done | bytes 524320 | tf_op jit(solution)/shard_map/ppermute | solution.py:401
  118.9 3.1 %tick_3.1 = (bf16[16,16384]{1,0:T(8,128)(2,1)S(1)}, bf16[16,16,128]{2,1,0:T(8,128)(2,1)S(1)}) custom-call(s32[4]{0:T(128)S(1)} %pad_add_fusion.refs_0_.flags, bf16[16,16384]{1,0:T(8,128)(2,1)} %collective-permute-done.6.refs_1_.refs_2_, bf16[16,16384]{1,0:T(8,128)(2,1)} %collective-permute-done.6.refs_1_.refs_2_, bf16[16,29696]{1,0:T(8,128)(2,1)S(1)} %bitcast.43, ...), custom_call_target="tpu_custom_call" | custom-call | flops 67108864 | bytes 6291456 | tf_op jit(solution)/shard_map/tick_3/pallas_call | solution.py:268
  123.5 8.0 %collective-permute-start.7 = (bf16[1,16384]{1,0:T(2,128)(2,1)S(1)}, bf16[1,16384]{1,0:T(2,128)(2,1)S(1)}, u32[]{:S(2)}, u32[]{:S(2)}) collective-permute-start(bf16[1,16384]{1,0:T(2,128)(2,1)S(1)} %get-tuple-element.43), channel_id=1, source_target_pairs={{0,8},{8,0},{1,9},{9,1},{2,10},{10,2},{3,11},{11,3},{4,12},{12,4},... | collective-permute-start | bytes 98312 | tf_op jit(solution)/shard_map/ppermute | solution.py:411
  132.1 6.8 %all-to-all-start.4 = ((bf16[16,2,128]{2,1,0:T(2,128)(2,1)}), bf16[16,2,128]{2,1,0:T(2,128)(2,1)S(1)}, u32[]{:S(2)}, u32[]{:S(2)}) async-start(bf16[16,2,128]{2,1,0:T(2,128)(2,1)} %pad_maximum_fusion.3), calls=%async_computation.4 | async-start | bytes 16384 | tf_op jit(solution)/shard_map/all_to_all | solution.py:413
  139.1 1.2 pad_maximum_fusion.row_ref
  140.3 6.1 %all-to-all-done.4.told_ref = bf16[16,2,128]{2,1,0:T(2,128)(2,1)S(1)} async-done(((bf16[16,2,128]{2,1,0:T(2,128)(2,1)}), bf16[16,2,128]{2,1,0:T(2,128)(2,1)S(1)}, u32[]{:S(2)}, u32[]{:S(2)}) %all-to-all-start.4) | async-done | bytes 8224 | tf_op jit(solution)/shard_map/all_to_all | solution.py:413
  (68 shorter events, 17.7 us)
Async XLA Ops:
  0.0 0.7 copy-start
  0.7 1.0 copy-start.2
  1.8 1.0 copy-start.4
  2.8 0.8 copy-start.11
  4.8 0.6 copy-start.14
  5.5 16.9 %collective-permute-start = (bf16[192,128]{1,0:T(8,128)(2,1)S(1)}, bf16[192,128]{1,0:T(8,128)(2,1)S(1)}, u32[]{:S(2)}, u32[]{:S(2)}) collective-permute-start(bf16[192,128]{1,0:T(8,128)(2,1)S(1)} %get-tuple-element.26), channel_id=1, source_target_pairs={{0,16},{16,32},{32,48},{48,64},{64,80},{80,96},{96,112},{112,128},... | collective-permute-start | bytes 147464 | tf_op jit(solution)/shard_map/ppermute | solution.py:384
  9.8 1.0 copy-start.3
  10.8 1.0 copy-start.5
  11.9 0.8 copy-start.12
  12.7 0.9 copy-start.13
  13.6 0.8 copy-start.18
  14.4 16.3 %copy-start.1 = (bf16[1,8192,128]{2,1,0:T(8,128)(2,1)S(1)}, bf16[1,8192,128]{2,1,0:T(8,128)(2,1)}, u32[]{:S(2)}) copy-start(bf16[1,8192,128]{2,1,0:T(8,128)(2,1)} %param.11) | copy-start | bytes 6291460
  23.4 33.5 %copy-start.6 = (bf16[1,16384]{1,0:T(2,128)(2,1)S(1)}, bf16[1,16384]{1,0:T(2,128)(2,1)}, u32[]{:S(2)}) copy-start(bf16[1,16384]{1,0:T(2,128)(2,1)} %refs_6_.7) | copy-start | bytes 98308
  23.4 30.9 %all-to-all-start = ((bf16[16,232,128]{2,1,0:T(8,128)(2,1)}), bf16[16,232,128]{2,1,0:T(8,128)(2,1)S(1)}, u32[]{:S(2)}, u32[]{:S(2)}) async-start(bf16[16,232,128]{2,1,0:T(8,128)(2,1)} %third_part.1), calls=%async_computation | async-start | bytes 1900544 | tf_op jit(solution)/shard_map/all_to_all | solution.py:386
  30.8 26.2 %collective-permute-start.1 = (bf16[8192,128]{1,0:T(8,128)(2,1)S(1)}, bf16[8192,128]{1,0:T(8,128)(2,1)}, u32[]{:S(2)}, u32[]{:S(2)}) collective-permute-start(bf16[8192,128]{1,0:T(8,128)(2,1)S(1)} %bitcast.46), channel_id=1, source_target_pairs={{0,8},{8,0},{1,9},{9,1},{2,10},{10,2},{3,11},{11,3},{4,12},{12,4},... | collective-permute-start | bytes 6291464 | tf_op jit(solution)/shard_map/ppermute | solution.py:372
  54.3 0.9 copy-start.22
  59.7 17.9 %copy-start.7 = (bf16[16,16384]{1,0:T(8,128)(2,1)}, bf16[16,16384]{1,0:T(8,128)(2,1)S(1)}, u32[]{:S(2)}) copy-start(bf16[16,16384]{1,0:T(8,128)(2,1)S(1)} %get-tuple-element.33.a_ref) | copy-start | bytes 1572868
  59.7 14.9 %collective-permute-start.2 = (bf16[16,16384]{1,0:T(8,128)(2,1)S(1)}, bf16[16,16384]{1,0:T(8,128)(2,1)S(1)}, u32[]{:S(2)}, u32[]{:S(2)}) collective-permute-start(bf16[16,16384]{1,0:T(8,128)(2,1)S(1)} %get-tuple-element.33.a_ref), channel_id=1, source_target_pairs={{0,24},{1,25},{2,26},{3,27},{4,28},{5,29},{6,30},{7,31},{16,40},{1... | collective-permute-start | bytes 1572872 | tf_op jit(solution)/shard_map/ppermute | solution.py:401
  77.6 0.6 copy-start.16
  78.3 19.7 %collective-permute-start.4 = (bf16[16,16384]{1,0:T(8,128)(2,1)}, bf16[16,16384]{1,0:T(8,128)(2,1)}, u32[]{:S(2)}, u32[]{:S(2)}) collective-permute-start(bf16[16,16384]{1,0:T(8,128)(2,1)} %get-tuple-element.35.b_ref), channel_id=1, source_target_pairs={{8,16},{9,17},{10,18},{11,19},{12,20},{13,21},{14,22},{15,23},{24,... | collective-permute-start | bytes 1572872 | tf_op jit(solution)/shard_map/ppermute | solution.py:401
  80.3 16.7 %collective-permute-start.5 = (bf16[16,8192]{1,0:T(8,128)(2,1)}, bf16[16,8192]{1,0:T(8,128)(2,1)S(1)}, u32[]{:S(2)}, u32[]{:S(2)}) collective-permute-start(bf16[16,8192]{1,0:T(8,128)(2,1)} %slice.30), channel_id=1, source_target_pairs={{760,0},{761,1},{762,2},{763,3},{764,4},{765,5},{766,6},{767,7},{2... | collective-permute-start | bytes 786440 | tf_op jit(solution)/shard_map/ppermute | solution.py:389
  81.0 16.9 %all-to-all-start.2 = ((bf16[16,16,128]{2,1,0:T(8,128)(2,1)}), bf16[16,16,128]{2,1,0:T(8,128)(2,1)S(1)}, u32[]{:S(2)}, u32[]{:S(2)}) async-start(bf16[16,16,128]{2,1,0:T(8,128)(2,1)} %copy-done.16), calls=%async_computation.2 | async-start | bytes 131072 | tf_op jit(solution)/shard_map/all_to_all | solution.py:402
  90.7 1.0 copy-start.8
  94.3 18.4 %collective-permute-start.3 = (bf16[1,16384]{1,0:T(2,128)(2,1)}, bf16[1,16384]{1,0:T(2,128)(2,1)}, u32[]{:S(2)}, u32[]{:S(2)}) collective-permute-start(bf16[1,16384]{1,0:T(2,128)(2,1)} %get-tuple-element.37), channel_id=1, source_target_pairs={{0,8},{8,0},{1,9},{9,1},{2,10},{10,2},{3,11},{11,3},{4,12},{12,4},... | collective-permute-start | bytes 98312 | tf_op jit(solution)/shard_map/ppermute | solution.py:411
  101.1 0.8 copy-start.9
  102.5 13.8 %all-to-all-start.3 = ((bf16[16,16,128]{2,1,0:T(8,128)(2,1)}), bf16[16,16,128]{2,1,0:T(8,128)(2,1)S(1)}, u32[]{:S(2)}, u32[]{:S(2)}) async-start(bf16[16,16,128]{2,1,0:T(8,128)(2,1)} %copy-done.17), calls=%async_computation.3 | async-start | bytes 131072 | tf_op jit(solution)/shard_map/all_to_all | solution.py:402
  108.3 10.5 %collective-permute-start.6 = (bf16[16,16384]{1,0:T(8,128)(2,1)}, bf16[16,16384]{1,0:T(8,128)(2,1)}, u32[]{:S(2)}, u32[]{:S(2)}) collective-permute-start(bf16[16,16384]{1,0:T(8,128)(2,1)} %copy-done.9), channel_id=1, source_target_pairs={{0,24},{1,25},{2,26},{3,27},{4,28},{5,29},{6,30},{7,31},{16,40},{1... | collective-permute-start | bytes 1572872 | tf_op jit(solution)/shard_map/ppermute | solution.py:401
  114.3 32.0 %copy-start.21 = (f32[64,128]{1,0:T(8,128)S(1)}, f32[64,128]{1,0:T(8,128)}, u32[]{:S(2)}) copy-start(f32[64,128]{1,0:T(8,128)} %copy-done.20) | copy-start | bytes 98308
  116.3 6.4 %copy-start.10 = (bf16[16,16384]{1,0:T(8,128)(2,1)S(1)}, bf16[16,16384]{1,0:T(8,128)(2,1)}, u32[]{:S(2)}) copy-start(bf16[16,16384]{1,0:T(8,128)(2,1)} %copy-done.9) | copy-start | bytes 1572868
  123.5 15.4 %collective-permute-start.7 = (bf16[1,16384]{1,0:T(2,128)(2,1)S(1)}, bf16[1,16384]{1,0:T(2,128)(2,1)S(1)}, u32[]{:S(2)}, u32[]{:S(2)}) collective-permute-start(bf16[1,16384]{1,0:T(2,128)(2,1)S(1)} %get-tuple-element.43), channel_id=1, source_target_pairs={{0,8},{8,0},{1,9},{9,1},{2,10},{10,2},{3,11},{11,3},{4,12},{12,4},... | collective-permute-start | bytes 98312 | tf_op jit(solution)/shard_map/ppermute | solution.py:411
  132.1 14.2 %all-to-all-start.4 = ((bf16[16,2,128]{2,1,0:T(2,128)(2,1)}), bf16[16,2,128]{2,1,0:T(2,128)(2,1)S(1)}, u32[]{:S(2)}, u32[]{:S(2)}) async-start(bf16[16,2,128]{2,1,0:T(2,128)(2,1)} %pad_maximum_fusion.3), calls=%async_computation.4 | async-start | bytes 16384 | tf_op jit(solution)/shard_map/all_to_all | solution.py:413
  146.3 0.9 copy-start.15
  (3 other events, 1.8 us)

commit v3 on v2

--- a/solution.py
+++ b/solution.py
@@ -7,6 +7,7 @@
 from jax.experimental import pallas as pl
 from jax.experimental.pallas import tpu as pltpu
 from jax.sharding import PartitionSpec as P
+
 
 QH = 64
 KVH = 4
@@ -154,7 +155,6 @@
         out_specs=(held, held, held),
         scratch_shapes=[pltpu.VMEM((4 * QH, HD), f32), pltpu.VMEM((3 * QH, slots), f32)],
         cost_estimate=cost(4 << 20),
-        compiler_params=pltpu.CompilerParams(vmem_limit_bytes=8 << 20),
         name="first_part",
     )(lens, queries, keys, values)
     fed = shift(fed)
@@ -178,7 +178,6 @@
             pltpu.VMEM((6 * QH, HD), f32),
         ],
         cost_estimate=cost(16 << 20),
-        compiler_params=pltpu.CompilerParams(vmem_limit_bytes=8 << 20),
         name="second_part",
     )(lens, pick, queries, keys, values, row, entering, aux)
     sent = pl.pallas_call(
@@ -187,7 +186,6 @@
         in_specs=[small, held, held, held, held, held, held],
         out_specs=held,
         cost_estimate=cost(1 << 20),
-        compiler_params=pltpu.CompilerParams(vmem_limit_bytes=8 << 20),
         name="third_part",
     )(first, fed, head, own, tail, ask, aux)
     return sent, mean, late
@@ -200,7 +198,11 @@
     if combined:
         heard_ref, mean_ref, extra_ref = refs[:3]
         refs = refs[3:]
-    x_ref, message_ref, scaled = refs
+    if tick == 3:
+        spoken, refs = refs[:3], refs[3:]
+        x_ref, message_ref, scaled, both = refs
+    else:
+        x_ref, message_ref, scaled = refs
     half = QH * HD
     rows = x_ref.shape[0]
     first = jnp.full((rows, HD), flags[2], jnp.int32) > 0
@@ -218,7 +220,8 @@
                     new = heard_ref[2 * g + 1].astype(f32)
                 mean = mean_ref[:, at].astype(f32)
                 weight = own[:, h % PER : h % PER + 1]
-                x = (x.astype(f32) + (mean + weight * (new - mean))).astype(bf16)
+                x = jnp.where(first, 0.0, x.astype(f32))
+                x = (x + (mean + weight * (new - mean))).astype(bf16)
         else:
             x = b_ref[:, at]
             if combined:
@@ -247,11 +250,18 @@
     own = jnp.where(lane < PER, 1.0 / (1.0 + jnp.exp(lse - score * FACTOR)), 0.0)
     is_key = jnp.full((rows, HD), flags[1], jnp.int32) > 0
     message = jnp.where(is_key, own, fresh).astype(bf16)
-    for d in range(message_ref.shape[0]):
-        message_ref[d] = message
-
-
-def do_tick(tick, flags, x, got, turn, gain, here, there, heard=None, extra=None):
+    if tick < 3:
+        for d in range(message_ref.shape[0]):
+            message_ref[d] = message
+        return
+    even = jnp.full((rows, HD), flags[0], jnp.int32) == 0
+    both[:rows, :] = jnp.where(even, spoken[0][0].astype(f32), spoken[1][0].astype(f32))
+    both[rows:, :] = jnp.where(even, spoken[2][0].astype(f32), message.astype(f32))
+    for j in range(rows):
+        message_ref[j] = both[pl.ds(j, 2, stride=rows), :].astype(bf16)
+
+
+def do_tick(tick, flags, x, got, turn, gain, here, there, heard=None, extra=None, spoken=()):
     rows, half = got.shape[0], QH * HD
     small = pl.BlockSpec(memory_space=pltpu.SMEM)
     held = pl.BlockSpec(memory_space=pltpu.VMEM)
@@ -263,56 +273,58 @@
     specs = [small, block(half, 0), block(half, 1), block(PER * HD, 12 + k), block(8 * HD, 28), held, held, held, held]
     operands = [flags, x, x, got, got, turn, gain, here, there]
     if tick:
-        specs += [held, block(half, 0 if tick == 3 else 2), held if tick > 1 else block(half, 1)]
+        specs += [held, block(half, 0 if tick == 3 else 2), block(half, 1)]
         operands += [heard, got, extra]
+    specs += [pl.BlockSpec((1, rows, HD), lambda i: (0, 0, 0))] * len(spoken)
+    operands += spoken
     return pl.pallas_call(
         functools.partial(tick_kernel, tick),
         grid=(1,),
         out_shape=(
             jax.ShapeDtypeStruct((rows, 2 * half), bf16),
-            jax.ShapeDtypeStruct((rows, rows, HD), bf16),
+            jax.ShapeDtypeStruct((rows, 2 if tick == 3 else rows, HD), bf16),
         ),
         in_specs=specs,
         out_specs=(held, held),
-        scratch_shapes=[pltpu.VMEM((2, rows, half), bf16)],
+        scratch_shapes=[pltpu.VMEM((2, rows, half), bf16)] + [pltpu.VMEM((2 * rows, HD), f32)] * (tick == 3),
         cost_estimate=pl.CostEstimate(flops=1 << 26, bytes_accessed=6 << 20, transcendentals=0),
         compiler_params=pltpu.CompilerParams(vmem_limit_bytes=20 << 20),
-        name=f"tick_{tick}",
     )(*operands)
 
 
-def pick_kernel(flags, a_ref, b_ref, mine_ref, other_ref):
-    rows, width = a_ref.shape
+def pick_kernel(flags, *refs):
+    xs, (mine_ref, other_ref) = refs[:4], refs[4:]
+    rows, width = xs[0].shape
     sub = lax.broadcasted_iota(jnp.int32, (8, rows), 0)
     lane = lax.broadcasted_iota(jnp.int32, (8, rows), 1)
-    wanted = jnp.where(sub == 0, flags[0] * 8 + flags[3], (1 - flags[0]) * 8 + flags[3])
-    select = jnp.where((lane == wanted) & (sub < 2), 1.0, 0.0).astype(bf16)
-    for r, ref in enumerate((a_ref, b_ref)):
+    wanted = jnp.where(sub < 2, flags[0] * 8 + flags[3], (1 - flags[0]) * 8 + flags[3])
+    selects = [jnp.where((lane == wanted) & (sub < 4) & (sub % 2 == k), 1.0, 0.0).astype(bf16) for k in range(2)]
+    for r in range(2):
 
         @pl.when(flags[0] == r)
         def _():
-            for k in range(0, width, 2048):
-                both = jnp.dot(select, ref[:, k : k + 2048], preferred_element_type=f32)
-                mine_ref[:, k : k + 2048] = both[0:1].astype(bf16)
-                other_ref[:, k : k + 2048] = both[1:2].astype(bf16)
-
-
-def pick_rows(flags, a, b):
+            for n in range(0, width, 2048):
+                at = slice(n, n + 2048)
+                found = jnp.dot(selects[0], xs[r][:, at], preferred_element_type=f32)
+                found = found + jnp.dot(selects[1], xs[2 + r][:, at], preferred_element_type=f32)
+                mine_ref[:, at] = found[0:2].astype(bf16)
+                other_ref[:, at] = found[2:4].astype(bf16)
+
+
+def pick_rows(flags, *xs):
     held = pl.BlockSpec(memory_space=pltpu.VMEM)
-    row = jax.ShapeDtypeStruct((1, a.shape[1]), bf16)
+    pair = jax.ShapeDtypeStruct((2, xs[0].shape[1]), bf16)
     return pl.pallas_call(
         pick_kernel,
-        out_shape=(row, row),
-        in_specs=[pl.BlockSpec(memory_space=pltpu.SMEM), held, held],
+        out_shape=(pair, pair),
+        in_specs=[pl.BlockSpec(memory_space=pltpu.SMEM), *[held] * 4],
         out_specs=(held, held),
         cost_estimate=pl.CostEstimate(flops=1 << 20, bytes_accessed=2 << 20, transcendentals=0),
-        compiler_params=pltpu.CompilerParams(vmem_limit_bytes=8 << 20),
         name="pick_rows",
-    )(flags, a, b)
-
-
-def last_kernel(row_ref, told_ref, early_ref, late_ref, out_ref, tell, mean):
-    half = QH * HD
+    )(flags, *xs)
+
+
+def last_kernel(flags, mine_ref, swap_ref, told_ref, early_ref, late_ref, out_ref, tell, mean):
     mean[: 3 * QH, :] = early_ref[...]
     mean[3 * QH :, :] = late_ref[...]
     for c in range(8):
@@ -320,31 +332,37 @@
             for k in range(2):
                 t = 2 * k + r
                 tell[c, t : t + 1, :] = told_ref[8 * r + c, k : k + 1, :].astype(f32)
-    for h in range(QH):
-        g, i = h // PER, h % PER
-        at = slice(h * HD, (h + 1) * HD)
-        cached = mean[pl.ds(h, 4, stride=QH), :]
-        own = tell[2 * g][:, i : i + 1]
-        mixed = cached + own * (tell[2 * g + 1] - cached)
-        out_ref[:, at] = (row_ref[:, at].astype(f32) + mixed).astype(bf16)
-    out_ref[:, half:] = row_ref[:, half:]
-
-
-def finish(row, told, early, late):
+    even = jnp.full((2, HD), flags[0], jnp.int32) == 0
+    for n in range(2 * QH):
+        at = slice(n * HD, (n + 1) * HD)
+        mine = mine_ref[:, at].astype(f32)
+        swap = swap_ref[:, at].astype(f32)
+        a = jnp.where(even, mine, swap)
+        b = jnp.where(even, swap, mine)
+        x = jnp.concatenate([a[0:1], b[0:1], a[1:2], b[1:2]], axis=0)
+        if n < QH:
+            g, i = n // PER, n % PER
+            cached = mean[pl.ds(n, 4, stride=QH), :]
+            own = tell[2 * g][:, i : i + 1]
+            x = x + (cached + own * (tell[2 * g + 1] - cached))
+        out_ref[:, at] = x.astype(bf16)
+
+
+def finish(flags, mine, swapped, told, early, late):
     held = pl.BlockSpec(memory_space=pltpu.VMEM)
     return pl.pallas_call(
         last_kernel,
-        out_shape=jax.ShapeDtypeStruct(row.shape, bf16),
-        in_specs=[held] * 4,
+        out_shape=jax.ShapeDtypeStruct((4, mine.shape[1]), bf16),
+        in_specs=[pl.BlockSpec(memory_space=pltpu.SMEM), *[held] * 5],
         out_specs=held,
         scratch_shapes=[pltpu.VMEM((8, 4, HD), f32), pltpu.VMEM((4 * QH, HD), f32)],
         cost_estimate=pl.CostEstimate(flops=1 << 20, bytes_accessed=1 << 20, transcendentals=0),
         compiler_params=pltpu.CompilerParams(vmem_limit_bytes=8 << 20),
         name="last_part",
-    )(row, told, early, late)
-
-
-def per_device(arriving, entering, gain, kv_weight, queries, cache_keys, cache_values, lengths):
+    )(flags, mine, swapped, told, early, late)
+
+
+def inner(arriving, entering, gain, kv_weight, queries, cache_keys, cache_values, lengths):
     section_at = lax.axis_index("section")
     row_at = lax.axis_index("row")
     col_at = lax.axis_index("col")
@@ -386,7 +404,6 @@
     got = lax.all_to_all(sent, RC, split_axis=0, concat_axis=0, tiled=True)
     got = got.reshape(2 * cols, -1)
 
-    tails = lax.ppermute(got[:, half:width], ALL, links([(sections - 1, 1, 0, 0), (1, 1, 0, 1)]))
     aux_at = width + half + 2 * PER * HD
     turns = [jnp.stack(angles(got[:, aux_at + k].astype(f32))) for k in range(2)]
     flags = jnp.stack([row_at, 1 - col_at % 2, first.astype(jnp.int32), col_at]).astype(jnp.int32)
@@ -398,21 +415,21 @@
             x, message = step(got)
         else:
             there = (tick - 1) % 2
-            relayed = lax.ppermute(x, ALL, links([(s, there, s + 1, 1 - there) for s in range(sections - 1)]))
+            pairs = [(s, there, s + 1, 1 - there) for s in range(sections - 1)]
+            if tick == 1:
+                pairs += [(sections - 1, 1, 0, 0), (1, 1, 0, 1)]
+            relayed = lax.ppermute(x, ALL, links(pairs))
             heard = lax.all_to_all(message, ALL, split_axis=0, concat_axis=0, axis_index_groups=relay_group(there), tiled=True)
-            x, message = step(relayed, heard=heard, extra=got if tick == 1 else tails)
+            tails = relayed if tick == 1 else tails
+            extra = got if tick == 1 else tails
+            x, message = step(relayed, heard=heard, extra=extra, spoken=messages if tick == 3 else [])
         rows.append(x)
-        messages.append(message[0])
-
-    told, mine, swapped = [], [], []
-    for k in range(2):
-        here, other = pick_rows(flags, rows[2 * k], rows[2 * k + 1])
-        mine.append(here)
-        swapped.append(lax.ppermute(other, "row", [(0, 1), (1, 0)]))
-        told.append(jnp.where(row_at == 0, messages[2 * k], messages[2 * k + 1]))
-    told = lax.all_to_all(jnp.stack(told, 1), RC, split_axis=0, concat_axis=0, tiled=True)
-    pairs = [[jnp.where(row_at == r, mine[k], swapped[k]) for r in range(2)] for k in range(2)]
-    out = finish(jnp.concatenate(pairs[0] + pairs[1], 0), told, early, late)
+        messages.append(message)
+
+    told = lax.all_to_all(messages[3], RC, split_axis=0, concat_axis=0, tiled=True)
+    mine, other = pick_rows(flags, *rows)
+    swapped = lax.ppermute(other, "row", [(0, 1), (1, 0)])
+    out = finish(flags, mine, swapped, told, early, late)
     return out[None, :, None]
 
 
@@ -428,7 +445,7 @@
         P(None, ("row", "col")),
     )
     return jax.shard_map(
-        per_device,
+        inner,
         mesh=mesh,
         in_specs=placed,
         out_specs=P("section", None, ("row", "col"), None),

time: 149 us -> 138 us (0.926)
  blocking collectives: 13.6 us -> 36 us
  starting transfers between devices: 53.7 us -> 31.4 us
  local copies, waits for them, and re-layouts: 17.1 us -> 6.84 us
  other arithmetic: 5.55 us -> 0.58 us
  Pallas kernels: 19.1 us -> 23.7 us
    all_to_all x1 -> x3, blocking collectives: 13.6 us -> 36 us  [the longest x2 24.1 us: inner(): lax.all_to_all(message, ALL, split_axis=0, concat_axis=0, axis_index_grou...]
    all_to_all x4 -> x2, starting transfers between devices: 29.6 us -> 15.9 us  [the longest x1 8.6 us: inner(): lax.all_to_all(message, ALL, split_axis=0, concat_axis=0, axis_index_grou...]
    unnamed x47 -> x33, local copies, waits for them, and re-layouts: 16.3 us -> 6.26 us
    ppermute x8 -> x6, starting transfers between devices: 24.1 us -> 15.5 us  [the longest x1 4.94 us: inner(): swapped = lax.ppermute(other, 'row', [(0, 1), (1, 0)])]
    select_n x4 -> x0, other arithmetic: 3.17 us -> none  [the longest x2 1.81 us: per_device(): jnp.where(row_at == r, mine[k], swapped[k])]
    all_to_all x4 -> x2, waiting for transfers between devices: 30 us -> 28.3 us  [the longest x1 21.1 us: inner(): got = lax.all_to_all(sent, RC, split_axis=0, concat_axis=0, tiled=True)]
    ppermute x8 -> x6, waiting for transfers between devices: 8.69 us -> 10.3 us  [the longest x1 10.3 us: inner(): lax.ppermute(fed, 'section', [(s, s + 1) for s in range(sections - 1)])]
    pallas_call x3 -> x2, Pallas kernels: 3.61 us -> 4.11 us  [the longest x1 2.62 us: pick_rows(): pl.pallas_call(pick_kernel, out_shape=(pair, pair), in_specs=[pl.BlockSpe...]
  transfers between devices with their start and end apart: 12 -> 8, of which waited for: 6 -> 3; matrix products, arithmetic and copies ran while one was open for 5% -> 1% of each run, Pallas kernels for 4% -> 2%
where the time goes in v3:
time: 138 us; the launch traced here: 137 us
  waiting for transfers between devices  38.6 us (28%)
  blocking collectives  36 us (26%)
  starting transfers between devices  31.4 us (23%)
  Pallas kernels  23.7 us (17%)
  local copies, waits for them, and re-layouts  6.84 us (5%)
    all_to_all x2, blocking collectives, inner(): lax.all_to_all(message, ALL, split_axis=0, concat_axis=0, axis_index_grou...  24.1 us
    all_to_all x1, waiting for transfers between devices, inner(): got = lax.all_to_all(sent, RC, split_axis=0, concat_axis=0, tiled=True)  21.1 us
    pallas_call x4, Pallas kernels, do_tick(): pl.pallas_call(functools.partial(tick_kernel, tick), grid=(1,), out_shape...  12.7 us
    all_to_all x1, blocking collectives, inner(): lax.all_to_all(messages[3], RC, split_axis=0, concat_axis=0, tiled=True)  11.8 us
    ppermute x1, waiting for transfers between devices, inner(): lax.ppermute(fed, 'section', [(s, s + 1) for s in range(sections - 1)])  10.3 us
    all_to_all x1, starting transfers between devices, inner(): lax.all_to_all(message, ALL, split_axis=0, concat_axis=0, axis_index_grou...  8.6 us
    all_to_all x1, starting transfers between devices, inner(): got = lax.all_to_all(sent, RC, split_axis=0, concat_axis=0, tiled=True)  7.34 us
    all_to_all x1, waiting for transfers between devices, inner(): lax.all_to_all(message, ALL, split_axis=0, concat_axis=0, axis_index_grou...  7.23 us
  transfers between devices with their start and end apart: 8, of which 3 were waited for; matrix products, arithmetic and copies ran while one was open for 1% of the time, Pallas kernels for 2%

profile of v3, /device:TPU:6, one launch (start us, length us, event | category | flops | bytes accessed | tf_op | source)
XLA Modules:
  0.0 137.3 jit_solution(15227195456373311976)
XLA Ops:
  0.0 0.7 copy-done
  0.7 0.6 dynamic-slice_bitcast_fusion.lens
  1.2 2.4 %first_part.1 = (f32[192,128]{1,0:T(8,128)}, bf16[192,128]{1,0:T(8,128)(2,1)}, f32[8,128]{1,0:T(8,128)}) custom-call(s32[4]{0:T(128)} %dynamic-slice_bitcast_fusion.lens, bf16[4,8192]{1,0:T(4,128)(2,1)} %bitcast.51, bf16[4,128,512]{2,1,0:T(8,128)(2,1)} %bitcast.47, bf16[4,128,512]{2,1,0:T(8,128)(2,1)} %bitcast.49), custom_call_target="tpu_custom_call" | custom-call | flops 4194304 | bytes 4194304 | tf_op jit(solution)/shard_map/first_part/pallas_call | solution.py:146
  3.7 4.3 %collective-permute-start = (bf16[192,128]{1,0:T(8,128)(2,1)}, bf16[192,128]{1,0:T(8,128)(2,1)S(1)}, u32[]{:S(2)}, u32[]{:S(2)}) collective-permute-start(bf16[192,128]{1,0:T(8,128)(2,1)} %get-tuple-element.24), channel_id=1, source_target_pairs={{0,16},{16,32},{32,48},{48,64},{64,80},{80,96},{96,112},{112,128},... | collective-permute-start | bytes 147464 | tf_op jit(solution)/shard_map/ppermute | solution.py:402
  8.0 2.5 %second_part.1 = (f32[64,128]{1,0:T(8,128)}, bf16[128,128]{1,0:T(8,128)(2,1)}, bf16[64,128]{1,0:T(8,128)(2,1)}, bf16[192,128]{1,0:T(8,128)(2,1)}, bf16[256,128]{1,0:T(8,128)(2,1)}, /*index=5*/f32[8,128]{1,0:T(8,128)}) custom-call(s32[4]{0:T(128)} %dynamic-slice_bitcast_fusion.lens, s32[1]{0:T(128)} %bitcast.8.pick, bf16[4,8192]{1,0:T(4,128)(2,1)} %bitcast.52, ...), custom_call_target="tpu_custom_call" | custom-call | flops 16777216 | bytes 16777216 | tf_op jit(solution)/shard_map/second_part/pallas_call | solution.py:161
  10.5 10.3 %collective-permute-done.fed_ref = bf16[192,128]{1,0:T(8,128)(2,1)S(1)} collective-permute-done((bf16[192,128]{1,0:T(8,128)(2,1)}, bf16[192,128]{1,0:T(8,128)(2,1)S(1)}, u32[]{:S(2)}, u32[]{:S(2)}) %collective-permute-start) | collective-permute-done | bytes 49184 | tf_op jit(solution)/shard_map/ppermute | solution.py:402
  20.8 0.6 copy-done.15
  21.4 2.0 %third_part.1 = bf16[16,232,128]{2,1,0:T(8,128)(2,1)} custom-call(s32[1]{0:T(128)} %bitcast.2.flags, bf16[192,128]{1,0:T(8,128)(2,1)} %copy-done.15, bf16[192,128]{1,0:T(8,128)(2,1)} %get-tuple-element.26.head_ref, bf16[128,128]{1,0:T(8,128)(2,1)} %get-tuple-element.27.own_ref, bf16[64,128]{1,0:T(8,128)(2,1)} %get-tuple-element.28.tail_ref, ...), custom_call_target="tpu_custom_call" | custom-call | flops 1048576 | bytes 1048576 | tf_op jit(solution)/shard_map/third_part/pallas_call | solution.py:183
  23.4 7.3 %all-to-all-start = ((bf16[16,232,128]{2,1,0:T(8,128)(2,1)}), bf16[16,232,128]{2,1,0:T(8,128)(2,1)S(1)}, u32[]{:S(2)}, u32[]{:S(2)}) async-start(bf16[16,232,128]{2,1,0:T(8,128)(2,1)} %third_part.1), calls=%async_computation | async-start | bytes 1900544 | tf_op jit(solution)/shard_map/all_to_all | solution.py:404
  30.8 2.3 %collective-permute-start.1 = (bf16[8192,128]{1,0:T(8,128)(2,1)S(1)}, bf16[8192,128]{1,0:T(8,128)(2,1)}, u32[]{:S(2)}, u32[]{:S(2)}) collective-permute-start(bf16[8192,128]{1,0:T(8,128)(2,1)S(1)} %bitcast.41), channel_id=1, source_target_pairs={{0,8},{8,0},{1,9},{9,1},{2,10},{10,2},{3,11},{11,3},{4,12},{12,4},... | collective-permute-start | bytes 6291464 | tf_op jit(solution)/shard_map/ppermute | solution.py:390
  33.2 21.1 %all-to-all-done = bf16[16,232,128]{2,1,0:T(8,128)(2,1)S(1)} async-done(((bf16[16,232,128]{2,1,0:T(8,128)(2,1)}), bf16[16,232,128]{2,1,0:T(8,128)(2,1)S(1)}, u32[]{:S(2)}, u32[]{:S(2)}) %all-to-all-start) | async-done | bytes 950304 | tf_op jit(solution)/shard_map/all_to_all | solution.py:404
  54.2 1.0 copy-done.14
  55.2 1.3 copy.11
  56.5 0.2 convert_reduce_fusion
  57.0 2.8 %shard_map.82 = (bf16[16,16384]{1,0:T(8,128)(2,1)S(1)}, bf16[16,16,128]{2,1,0:T(8,128)(2,1)S(1)}) custom-call(s32[4]{0:T(128)S(1)} %pad_add_fusion.refs_0_.flags, bf16[16,29696]{1,0:T(8,128)(2,1)S(1)} %bitcast.27, bf16[16,29696]{1,0:T(8,128)(2,1)S(1)} %bitcast.28, bf16[16,29696]{1,0:T(8,128)(2,1)S(1)} %bitcast.29, bf16[16,29696]{1,0:T(8,128)(2,1)S(1)} %bitcast.30, ...), custom_call_target="tpu_custom_call" | custom-call | flops 67108864 | bytes 6291456 | tf_op jit(solution)/shard_map/pallas_call | solution.py:280
  59.7 1.3 collective-permute-start.2
  61.1 13.6 %all_to_all.25.refs_9_ = bf16[16,16,128]{2,1,0:T(8,128)(2,1)S(1)} all-to-all(bf16[16,16,128]{2,1,0:T(8,128)(2,1)S(1)} %get-tuple-element.32.refs_12_), channel_id=1, replica_groups={{0,1,2,3,4,5,6,7,24,25,26,27,28,29,30,31},{16,17,18,19,20,21,22,23,40,4..., dimensions={0} | all-to-all | bytes 131072 | tf_op jit(solution)/shard_map/all_to_all | solution.py:422
  74.7 3.8 %shard_map.83 = (bf16[16,16384]{1,0:T(8,128)(2,1)}, bf16[16,16,128]{2,1,0:T(8,128)(2,1)}) custom-call(s32[4]{0:T(128)S(1)} %pad_add_fusion.refs_0_.flags, bf16[16,16384]{1,0:T(8,128)(2,1)S(1)} %collective-permute-done.2.refs_1_.refs_2_.refs_11_, bf16[16,16384]{1,0:T(8,128)(2,1)S(1)} %collective-permute-done.2.refs_1_.refs_2_.refs_11_, ...), custom_call_target="tpu_custom_call" | custom-call | flops 67108864 | bytes 6291456 | tf_op jit(solution)/shard_map/pallas_call | solution.py:280
  78.4 1.3 collective-permute-start.3
  79.7 8.6 %all-to-all-start.2 = ((bf16[16,16,128]{2,1,0:T(8,128)(2,1)}), bf16[16,16,128]{2,1,0:T(8,128)(2,1)S(1)}, u32[]{:S(2)}, u32[]{:S(2)}) async-start(bf16[16,16,128]{2,1,0:T(8,128)(2,1)} %get-tuple-element.34.refs_13_), calls=%async_computation.2 | async-start | bytes 131072 | tf_op jit(solution)/shard_map/all_to_all | solution.py:422
  88.4 7.2 %all-to-all-done.2.refs_9_ = bf16[16,16,128]{2,1,0:T(8,128)(2,1)S(1)} async-done(((bf16[16,16,128]{2,1,0:T(8,128)(2,1)}), bf16[16,16,128]{2,1,0:T(8,128)(2,1)S(1)}, u32[]{:S(2)}, u32[]{:S(2)}) %all-to-all-start.2) | async-done | bytes 65568 | tf_op jit(solution)/shard_map/all_to_all | solution.py:422
  95.6 1.0 copy-done.3
  96.7 3.2 %shard_map.84 = (bf16[16,16384]{1,0:T(8,128)(2,1)S(1)}, bf16[16,16,128]{2,1,0:T(8,128)(2,1)S(1)}) custom-call(s32[4]{0:T(128)S(1)} %pad_add_fusion.refs_0_.flags, bf16[16,16384]{1,0:T(8,128)(2,1)} %collective-permute-done.3.refs_1_.refs_2_, bf16[16,16384]{1,0:T(8,128)(2,1)} %collective-permute-done.3.refs_1_.refs_2_, bf16[16,29696]{1,0:T(8,128)(2,1)S(1)} %bitcast.35, ...), custom_call_target="tpu_custom_call" | custom-call | flops 67108864 | bytes 6291456 | tf_op jit(solution)/shard_map/pallas_call | solution.py:280
  99.9 1.3 collective-permute-start.4
  101.2 10.6 %all_to_all.26.refs_9_ = bf16[16,16,128]{2,1,0:T(8,128)(2,1)S(1)} all-to-all(bf16[16,16,128]{2,1,0:T(8,128)(2,1)S(1)} %get-tuple-element.36.refs_14_), channel_id=1, replica_groups={{0,1,2,3,4,5,6,7,24,25,26,27,28,29,30,31},{16,17,18,19,20,21,22,23,40,4..., dimensions={0} | all-to-all | bytes 131072 | tf_op jit(solution)/shard_map/all_to_all | solution.py:422
  111.8 3.0 %shard_map.85 = (bf16[16,16384]{1,0:T(8,128)(2,1)S(1)}, bf16[16,2,128]{2,1,0:T(2,128)(2,1)S(1)}) custom-call(s32[4]{0:T(128)S(1)} %pad_add_fusion.refs_0_.flags, bf16[16,16384]{1,0:T(8,128)(2,1)S(1)} %collective-permute-done.4.refs_1_.refs_2_, bf16[16,16384]{1,0:T(8,128)(2,1)S(1)} %collective-permute-done.4.refs_1_.refs_2_, bf16[16,29696]{1,0:T(8,128)(2,1)S(1)} %bitcast.38, ...), custom_call_target="tpu_custom_call" | custom-call | flops 67108864 | bytes 6291456 | tf_op jit(solution)/shard_map/pallas_call | solution.py:280
  114.8 0.8 copy-done.8
  115.6 2.6 %pick_rows.1 = (bf16[2,16384]{1,0:T(2,128)(2,1)}, bf16[2,16384]{1,0:T(2,128)(2,1)}) custom-call(s32[4]{0:T(128)} %copy-done.12, bf16[16,16384]{1,0:T(8,128)(2,1)} %copy-done.6, bf16[16,16384]{1,0:T(8,128)(2,1)} %get-tuple-element.33.refs_1_, bf16[16,16384]{1,0:T(8,128)(2,1)} %copy-done.7, bf16[16,16384]{1,0:T(8,128)(2,1)} %copy-done.8), custom_call_target="tpu_custom_call" | custom-call | flops 1048576 | bytes 2097152 | tf_op jit(solution)/shard_map/pick_rows/pallas_call | solution.py:317
  118.2 4.9 %collective-permute-start.5 = (bf16[2,16384]{1,0:T(2,128)(2,1)}, bf16[2,16384]{1,0:T(2,128)(2,1)S(1)}, u32[]{:S(2)}, u32[]{:S(2)}) collective-permute-start(bf16[2,16384]{1,0:T(2,128)(2,1)} %get-tuple-element.39), channel_id=1, source_target_pairs={{0,8},{8,0},{1,9},{9,1},{2,10},{10,2},{3,11},{11,3},{4,12},{12,4},... | collective-permute-start | bytes 196616 | tf_op jit(solution)/shard_map/ppermute | solution.py:431
  123.2 11.8 %all_to_all.27.told_ref = bf16[16,2,128]{2,1,0:T(2,128)(2,1)S(1)} all-to-all(bf16[16,2,128]{2,1,0:T(2,128)(2,1)S(1)} %get-tuple-element.40), channel_id=1, replica_groups=mesh['section'=48,'row'=2,'col'=8] {'row','col'}, dimensions={0} | all-to-all | bytes 16384 | tf_op jit(solution)/shard_map/all_to_all | solution.py:429
  135.0 0.8 copy-done.10
  135.9 1.5 %last_part.1 = bf16[4,16384]{1,0:T(4,128)(2,1)} custom-call(s32[4]{0:T(128)S(1)} %copy-done.13, bf16[2,16384]{1,0:T(2,128)(2,1)S(1)} %copy-done.10, bf16[2,16384]{1,0:T(2,128)(2,1)S(1)} %collective-permute-done.5.swap_ref, bf16[16,2,128]{2,1,0:T(2,128)(2,1)S(1)} %all_to_all.27.told_ref, f32[192,128]{1,0:T(8,128)S(1)} %copy-done.9, f32[64,128]{1,0:T(8,128)S(1)} %copy-done.11), custom_call_target="tpu_custom_call" | custom-call | flops 1048576 | bytes 1048576 | tf_op jit(solution)/shard_map/last_part/pallas_call | solution.py:353
  (38 shorter events, 0.5 us)
Async XLA Ops:
  0.0 0.7 copy-start
  3.7 17.1 %collective-permute-start = (bf16[192,128]{1,0:T(8,128)(2,1)}, bf16[192,128]{1,0:T(8,128)(2,1)S(1)}, u32[]{:S(2)}, u32[]{:S(2)}) collective-permute-start(bf16[192,128]{1,0:T(8,128)(2,1)} %get-tuple-element.24), channel_id=1, source_target_pairs={{0,16},{16,32},{32,48},{48,64},{64,80},{80,96},{96,112},{112,128},... | collective-permute-start | bytes 147464 | tf_op jit(solution)/shard_map/ppermute | solution.py:402
  8.0 22.8 %copy-start.1 = (bf16[1,8192,128]{2,1,0:T(8,128)(2,1)S(1)}, bf16[1,8192,128]{2,1,0:T(8,128)(2,1)}, u32[]{:S(2)}) copy-start(bf16[1,8192,128]{2,1,0:T(8,128)(2,1)} %param.11) | copy-start | bytes 6291460
  20.8 0.6 copy-start.15
  23.4 33.6 %copy-start.5 = (bf16[1,16384]{1,0:T(2,128)(2,1)S(1)}, bf16[1,16384]{1,0:T(2,128)(2,1)}, u32[]{:S(2)}) copy-start(bf16[1,16384]{1,0:T(2,128)(2,1)} %refs_6_.7) | copy-start | bytes 98308
  23.4 30.9 %all-to-all-start = ((bf16[16,232,128]{2,1,0:T(8,128)(2,1)}), bf16[16,232,128]{2,1,0:T(8,128)(2,1)S(1)}, u32[]{:S(2)}, u32[]{:S(2)}) async-start(bf16[16,232,128]{2,1,0:T(8,128)(2,1)} %third_part.1), calls=%async_computation | async-start | bytes 1900544 | tf_op jit(solution)/shard_map/all_to_all | solution.py:404
  30.8 26.2 %collective-permute-start.1 = (bf16[8192,128]{1,0:T(8,128)(2,1)S(1)}, bf16[8192,128]{1,0:T(8,128)(2,1)}, u32[]{:S(2)}, u32[]{:S(2)}) collective-permute-start(bf16[8192,128]{1,0:T(8,128)(2,1)S(1)} %bitcast.41), channel_id=1, source_target_pairs={{0,8},{8,0},{1,9},{9,1},{2,10},{10,2},{3,11},{11,3},{4,12},{12,4},... | collective-permute-start | bytes 6291464 | tf_op jit(solution)/shard_map/ppermute | solution.py:390
  33.2 78.6 %copy-start.12 = (s32[4]{0:T(128)}, s32[4]{0:T(128)S(1)}, u32[]{:S(2)}) copy-start(s32[4]{0:T(128)S(1)} %pad_add_fusion.refs_0_.flags) | copy-start | bytes 52
  54.2 1.0 copy-start.14
  59.7 18.7 %copy-start.6 = (bf16[16,16384]{1,0:T(8,128)(2,1)}, bf16[16,16384]{1,0:T(8,128)(2,1)S(1)}, u32[]{:S(2)}) copy-start(bf16[16,16384]{1,0:T(8,128)(2,1)S(1)} %get-tuple-element.31.refs_0_) | copy-start | bytes 1572868
  59.7 14.9 %collective-permute-start.2 = (bf16[16,16384]{1,0:T(8,128)(2,1)S(1)}, bf16[16,16384]{1,0:T(8,128)(2,1)S(1)}, u32[]{:S(2)}, u32[]{:S(2)}) collective-permute-start(bf16[16,16384]{1,0:T(8,128)(2,1)S(1)} %get-tuple-element.31.refs_0_), channel_id=1, source_target_pairs={{0,24},{1,25},{2,26},{3,27},{4,28},{5,29},{6,30},{7,31},{16,40},{1... | collective-permute-start | bytes 1572872 | tf_op jit(solution)/shard_map/ppermute | solution.py:421
  74.7 3.8 %copy-start.2 = (bf16[16,16384]{1,0:T(8,128)(2,1)}, bf16[16,16384]{1,0:T(8,128)(2,1)S(1)}, u32[]{:S(2)}) copy-start(bf16[16,16384]{1,0:T(8,128)(2,1)S(1)} %collective-permute-done.2.refs_1_.refs_2_.refs_11_) | copy-start | bytes 1572868
  78.4 17.2 %collective-permute-start.3 = (bf16[16,16384]{1,0:T(8,128)(2,1)}, bf16[16,16384]{1,0:T(8,128)(2,1)}, u32[]{:S(2)}, u32[]{:S(2)}) collective-permute-start(bf16[16,16384]{1,0:T(8,128)(2,1)} %get-tuple-element.33.refs_1_), channel_id=1, source_target_pairs={{8,16},{9,17},{10,18},{11,19},{12,20},{13,21},{14,22},{15,23},{24,... | collective-permute-start | bytes 1572872 | tf_op jit(solution)/shard_map/ppermute | solution.py:421
  79.7 15.9 %all-to-all-start.2 = ((bf16[16,16,128]{2,1,0:T(8,128)(2,1)}), bf16[16,16,128]{2,1,0:T(8,128)(2,1)S(1)}, u32[]{:S(2)}, u32[]{:S(2)}) async-start(bf16[16,16,128]{2,1,0:T(8,128)(2,1)} %get-tuple-element.34.refs_13_), calls=%async_computation.2 | async-start | bytes 131072 | tf_op jit(solution)/shard_map/all_to_all | solution.py:422
  95.6 1.0 copy-start.3
  96.7 15.1 %copy-start.4 = (bf16[16,16384]{1,0:T(8,128)(2,1)S(1)}, bf16[16,16384]{1,0:T(8,128)(2,1)}, u32[]{:S(2)}) copy-start(bf16[16,16384]{1,0:T(8,128)(2,1)} %copy-done.2) | copy-start | bytes 1572868
  99.9 1.3 copy-start.7
  99.9 11.9 %collective-permute-start.4 = (bf16[16,16384]{1,0:T(8,128)(2,1)S(1)}, bf16[16,16384]{1,0:T(8,128)(2,1)S(1)}, u32[]{:S(2)}, u32[]{:S(2)}) collective-permute-start(bf16[16,16384]{1,0:T(8,128)(2,1)S(1)} %get-tuple-element.35.refs_2_), channel_id=1, source_target_pairs={{0,24},{1,25},{2,26},{3,27},{4,28},{5,29},{6,30},{7,31},{16,40},{1... | collective-permute-start | bytes 1572872 | tf_op jit(solution)/shard_map/ppermute | solution.py:421
  114.8 0.8 copy-start.8
  115.6 19.4 %copy-start.9 = (f32[192,128]{1,0:T(8,128)S(1)}, f32[192,128]{1,0:T(8,128)}, u32[]{:S(2)}) copy-start(f32[192,128]{1,0:T(8,128)} %get-tuple-element.41.early_ref) | copy-start | bytes 294916
  115.6 19.4 %copy-start.11 = (f32[64,128]{1,0:T(8,128)S(1)}, f32[64,128]{1,0:T(8,128)}, u32[]{:S(2)}) copy-start(f32[64,128]{1,0:T(8,128)} %get-tuple-element.42.late_ref) | copy-start | bytes 98308
  115.6 19.4 %copy-start.13 = (s32[4]{0:T(128)S(1)}, s32[4]{0:T(128)}, u32[]{:S(2)}) copy-start(s32[4]{0:T(128)} %copy-done.12) | copy-start | bytes 52
  118.2 16.8 %collective-permute-start.5 = (bf16[2,16384]{1,0:T(2,128)(2,1)}, bf16[2,16384]{1,0:T(2,128)(2,1)S(1)}, u32[]{:S(2)}, u32[]{:S(2)}) collective-permute-start(bf16[2,16384]{1,0:T(2,128)(2,1)} %get-tuple-element.39), channel_id=1, source_target_pairs={{0,8},{8,0},{1,9},{9,1},{2,10},{10,2},{3,11},{11,3},{4,12},{12,4},... | collective-permute-start | bytes 196616 | tf_op jit(solution)/shard_map/ppermute | solution.py:431
  135.0 0.8 copy-start.10

commit v4 on v3

--- a/solution.py
+++ b/solution.py
@@ -70,7 +70,8 @@
     return out
 
 
-def first_kernel(lens, q_ref, k_ref, v_ref, mean_ref, fed_ref, aux_ref, qs, scores):
+def first_kernel(base, lengths, q_ref, k_ref, v_ref, mean_ref, fed_ref, aux_ref, qs, scores):
+    lens = [lengths[base[0] + t] for t in range(4)]
     for h in range(QH):
         qs[pl.ds(h, 4, stride=QH), :] = q_ref[:, h * HD : (h + 1) * HD].astype(f32)
     means, lses = attend(qs, k_ref, v_ref, lens, scores, (0, 1, 2))
@@ -83,8 +84,9 @@
         aux_ref[KVH + g : KVH + g + 1, :] = odd[g]
 
 
-def second_kernel(lens, pick, q_ref, k_ref, v_ref, row_ref, ent_ref, aux_in, mean_ref, own_ref, tail_ref, head_ref, ask_ref, aux_ref, qs, scores, wide, ents):
+def second_kernel(base, lengths, pick, q_ref, k_ref, v_ref, row_ref, ent_ref, aux_in, mean_ref, own_ref, tail_ref, head_ref, ask_ref, aux_ref, qs, scores, wide, ents):
     blocks = 2 * QH
+    lens = [lengths[base[0] + t] for t in range(4)]
     for h in range(QH):
         qs[pl.ds(h, 4, stride=QH), :] = q_ref[:, h * HD : (h + 1) * HD].astype(f32)
     for a in range(blocks):
@@ -135,7 +137,7 @@
                 send_ref[d, 3 * QH + 2 * PER :, :] = aux.astype(bf16)
 
 
-def prepare(queries, keys, values, row, entering, lens, pick, first, shift):
+def prepare(queries, keys, values, row, entering, base, lengths, pick, first, shift):
     slots, kept = keys.shape[1], KVH * HD
     held = pl.BlockSpec(memory_space=pltpu.VMEM)
     small = pl.BlockSpec(memory_space=pltpu.SMEM)
@@ -151,12 +153,12 @@
             jax.ShapeDtypeStruct((3 * QH, HD), bf16),
             jax.ShapeDtypeStruct((2 * KVH, HD), f32),
         ),
-        in_specs=[small, held, *[pl.BlockSpec((3, slots, kept), lambda i: (0, 0, 0))] * 2],
+        in_specs=[small, small, held, *[pl.BlockSpec((3, slots, kept), lambda i: (0, 0, 0))] * 2],
         out_specs=(held, held, held),
         scratch_shapes=[pltpu.VMEM((4 * QH, HD), f32), pltpu.VMEM((3 * QH, slots), f32)],
         cost_estimate=cost(4 << 20),
         name="first_part",
-    )(lens, queries, keys, values)
+    )(base, lengths, queries, keys, values)
     fed = shift(fed)
     late, own, tail, head, ask, aux = pl.pallas_call(
         second_kernel,
@@ -169,7 +171,7 @@
             jax.ShapeDtypeStruct((4 * QH, HD), bf16),
             jax.ShapeDtypeStruct((2 * KVH, HD), f32),
         ),
-        in_specs=[small, small, held, *[pl.BlockSpec((1, slots, kept), lambda i: (3, 0, 0))] * 2, held, held, held],
+        in_specs=[small, small, small, held, *[pl.BlockSpec((1, slots, kept), lambda i: (3, 0, 0))] * 2, held, held, held],
         out_specs=(held,) * 6,
         scratch_shapes=[
             pltpu.VMEM((4 * QH, HD), f32),
@@ -179,7 +181,7 @@
         ],
         cost_estimate=cost(16 << 20),
         name="second_part",
-    )(lens, pick, queries, keys, values, row, entering, aux)
+    )(base, lengths, pick, queries, keys, values, row, entering, aux)
     sent = pl.pallas_call(
         third_kernel,
         out_shape=jax.ShapeDtypeStruct((16, 3 * QH + 2 * PER + 8, HD), bf16),
@@ -200,9 +202,11 @@
         refs = refs[3:]
     if tick == 3:
         spoken, refs = refs[:3], refs[3:]
-        x_ref, message_ref, scaled, both = refs
+        x_ref, message_ref, scaled, held_there, arrived, both = refs
     else:
-        x_ref, message_ref, scaled = refs
+        x_ref, message_ref, scaled, held_there, arrived = refs
+    bring = pltpu.make_async_copy(there_ref, held_there, arrived)
+    bring.start()
     half = QH * HD
     rows = x_ref.shape[0]
     first = jnp.full((rows, HD), flags[2], jnp.int32) > 0
@@ -232,12 +236,15 @@
         scaled[n // QH, :, at] = (wide * gain_ref[:, n * HD : (n + 1) * HD].astype(f32)).astype(bf16)
     fresh = jnp.zeros((rows, HD), f32)
     step = 2048
-    for ref, part in ((here_ref, flags[0]), (there_ref, 1 - flags[0])):
+    for ref, part in ((here_ref, flags[0]), (held_there, 1 - flags[0])):
+        if ref is held_there:
+            bring.wait()
         for k in range(0, half, step):
             fresh = fresh + jnp.dot(scaled[part, :, k : k + step], ref[k : k + step, :], preferred_element_type=f32)
     scale = lax.rsqrt(jnp.sum(square, axis=1, keepdims=True) / (2 * half) + 1e-05)
     fresh = fresh * scale
-    key = fresh * turn_ref[0] + pltpu.roll(fresh, HD // 2, 1) * turn_ref[1]
+    k = tick // 2
+    key = fresh * turn_ref[2 * k] + pltpu.roll(fresh, HD // 2, 1) * turn_ref[2 * k + 1]
     key = key.astype(bf16).astype(f32)
     score = jnp.zeros((rows, HD), f32)
     for i in range(PER):
@@ -270,7 +277,7 @@
         return pl.BlockSpec((rows, size), lambda i: (0, n))
 
     k = tick // 2
-    specs = [small, block(half, 0), block(half, 1), block(PER * HD, 12 + k), block(8 * HD, 28), held, held, held, held]
+    specs = [small, block(half, 0), block(half, 1), block(PER * HD, 12 + k), block(8 * HD, 28), held, held, held, pl.BlockSpec(memory_space=pl.ANY)]
     operands = [flags, x, x, got, got, turn, gain, here, there]
     if tick:
         specs += [held, block(half, 0 if tick == 3 else 2), block(half, 1)]
@@ -286,7 +293,12 @@
         ),
         in_specs=specs,
         out_specs=(held, held),
-        scratch_shapes=[pltpu.VMEM((2, rows, half), bf16)] + [pltpu.VMEM((2 * rows, HD), f32)] * (tick == 3),
+        scratch_shapes=[
+            pltpu.VMEM((2, rows, half), bf16),
+            pltpu.VMEM(there.shape, bf16),
+            pltpu.SemaphoreType.DMA,
+            *[pltpu.VMEM((2 * rows, HD), f32)] * (tick == 3),
+        ],
         cost_estimate=pl.CostEstimate(flops=1 << 26, bytes_accessed=6 << 20, transcendentals=0),
         compiler_params=pltpu.CompilerParams(vmem_limit_bytes=20 << 20),
     )(*operands)
@@ -388,7 +400,6 @@
 
     w_here = kv_weight[0]
     w_there = lax.ppermute(w_here, "row", [(0, 1), (1, 0)])
-    lens = lax.dynamic_slice_in_dim(lengths[:, 0], sections - 1 - section_at, ticks, 0)
     pick = jnp.where(first, 0, jnp.where(last, 1, 2)).astype(jnp.int32)[None]
     sent, early, late = prepare(
         queries[0, :, 0],
@@ -396,7 +407,8 @@
         cache_values[0, :, 0],
         arriving[0],
         entering[:, 0],
-        lens,
+        (sections - 1 - section_at).astype(jnp.int32)[None],
+        lengths[:, 0],
         pick,
         first.astype(jnp.int32)[None],
         lambda fed: lax.ppermute(fed, "section", [(s, s + 1) for s in range(sections - 1)]),
@@ -405,22 +417,21 @@
     got = got.reshape(2 * cols, -1)
 
     aux_at = width + half + 2 * PER * HD
-    turns = [jnp.stack(angles(got[:, aux_at + k].astype(f32))) for k in range(2)]
+    turns = jnp.stack([t for k in range(2) for t in angles(got[:, aux_at + k].astype(f32))])
     flags = jnp.stack([row_at, 1 - col_at % 2, first.astype(jnp.int32), col_at]).astype(jnp.int32)
 
     rows, messages = [], []
     for tick in range(ticks):
-        step = functools.partial(do_tick, tick, flags, got=got, turn=turns[tick // 2], gain=gain, here=w_here, there=w_there)
+        step = functools.partial(do_tick, tick, flags, got=got, turn=turns, gain=gain, here=w_here, there=w_there)
         if tick == 0:
             x, message = step(got)
         else:
             there = (tick - 1) % 2
             pairs = [(s, there, s + 1, 1 - there) for s in range(sections - 1)]
-            if tick == 1:
-                pairs += [(sections - 1, 1, 0, 0), (1, 1, 0, 1)]
             relayed = lax.ppermute(x, ALL, links(pairs))
             heard = lax.all_to_all(message, ALL, split_axis=0, concat_axis=0, axis_index_groups=relay_group(there), tiled=True)
-            tails = relayed if tick == 1 else tails
+            if tick == 1:
+                tails = lax.ppermute(x, ALL, links([(sections - 1, 1, 0, 0), (1, 1, 0, 1)]))
             extra = got if tick == 1 else tails
             x, message = step(relayed, heard=heard, extra=extra, spoken=messages if tick == 3 else [])
         rows.append(x)

time: 138 us -> 141 us (1.022)
  blocking collectives: 36 us -> 22.3 us
  starting transfers between devices: 31.4 us -> 39.6 us
  waiting for transfers between devices: 38.6 us -> 45.1 us
  Pallas kernels: 23.7 us -> 27.5 us
  local copies, waits for them, and re-layouts: 6.84 us -> 4.54 us
    all_to_all x2 -> x1, blocking collectives: 24.1 us -> 10.5 us  [inner(): lax.all_to_all(message, ALL, split_axis=0, concat_axis=0, axis_index_grou...]
    all_to_all x1 -> x2, waiting for transfers between devices: 7.23 us -> 13.7 us  [inner(): lax.all_to_all(message, ALL, split_axis=0, concat_axis=0, axis_index_grou...]
    all_to_all x1 -> x2, starting transfers between devices: 8.6 us -> 14.4 us  [inner(): lax.all_to_all(message, ALL, split_axis=0, concat_axis=0, axis_index_grou...]
    pallas_call x4, Pallas kernels: 12.7 us -> 16.4 us  [do_tick(): pl.pallas_call(functools.partial(tick_kernel, tick), grid=(1,), out_shape...]
    unnamed x33 -> x23, local copies, waits for them, and re-layouts: 6.26 us -> 4.54 us
    ppermute x0 -> x1, starting transfers between devices: none -> 1.46 us  [inner(): tails = lax.ppermute(x, ALL, links([(sections - 1, 1, 0, 0), (1, 1, 0, 1)]))]
  transfers between devices with their start and end apart: 8 -> 10, of which waited for: 3 -> 4; matrix products, arithmetic and copies ran while one was open for 1% -> 1% of each run, Pallas kernels for 2% -> 5%
where the time goes in v4:
time: 141 us; the launch traced here: 140 us
  waiting for transfers between devices  45.1 us (32%)
  starting transfers between devices  39.6 us (28%)
  Pallas kernels  27.5 us (20%)
  blocking collectives  22.3 us (16%)
  local copies, waits for them, and re-layouts  4.54 us (3%)
    all_to_all x1, waiting for transfers between devices, inner(): got = lax.all_to_all(sent, RC, split_axis=0, concat_axis=0, tiled=True)  21.1 us
    pallas_call x4, Pallas kernels, do_tick(): pl.pallas_call(functools.partial(tick_kernel, tick), grid=(1,), out_shape...  16.4 us
    all_to_all x2, starting transfers between devices, inner(): lax.all_to_all(message, ALL, split_axis=0, concat_axis=0, axis_index_grou...  14.4 us
    all_to_all x2, waiting for transfers between devices, inner(): lax.all_to_all(message, ALL, split_axis=0, concat_axis=0, axis_index_grou...  13.7 us
    all_to_all x1, blocking collectives, inner(): lax.all_to_all(messages[3], RC, split_axis=0, concat_axis=0, tiled=True)  11.8 us
    all_to_all x1, blocking collectives, inner(): lax.all_to_all(message, ALL, split_axis=0, concat_axis=0, axis_index_grou...  10.5 us
    ppermute x1, waiting for transfers between devices, inner(): lax.ppermute(fed, 'section', [(s, s + 1) for s in range(sections - 1)])  10.3 us
    all_to_all x1, starting transfers between devices, inner(): got = lax.all_to_all(sent, RC, split_axis=0, concat_axis=0, tiled=True)  7.34 us
  transfers between devices with their start and end apart: 10, of which 4 were waited for; matrix products, arithmetic and copies ran while one was open for 1% of the time, Pallas kernels for 5%

profile of v4, /device:TPU:6, one launch (start us, length us, event | category | flops | bytes accessed | tf_op | source)
XLA Modules:
  0.0 139.8 jit_solution(3225170976619956927)
XLA Ops:
  0.0 2.4 %first_part.1 = (f32[192,128]{1,0:T(8,128)}, bf16[192,128]{1,0:T(8,128)(2,1)}, f32[8,128]{1,0:T(8,128)}) custom-call(s32[1]{0:T(128)} %bitcast.4.base, s32[51]{0:T(128)} %bitcast.55, bf16[4,8192]{1,0:T(4,128)(2,1)} %bitcast.51, bf16[4,128,512]{2,1,0:T(8,128)(2,1)} %bitcast.47, bf16[4,128,512]{2,1,0:T(8,128)(2,1)} %bitcast.49), custom_call_target="tpu_custom_call" | custom-call | flops 4194304 | bytes 4194304 | tf_op jit(solution)/shard_map/first_part/pallas_call | solution.py:148
  2.4 4.3 %collective-permute-start = (bf16[192,128]{1,0:T(8,128)(2,1)}, bf16[192,128]{1,0:T(8,128)(2,1)S(1)}, u32[]{:S(2)}, u32[]{:S(2)}) collective-permute-start(bf16[192,128]{1,0:T(8,128)(2,1)} %get-tuple-element.24), channel_id=1, source_target_pairs={{0,16},{16,32},{32,48},{48,64},{64,80},{80,96},{96,112},{112,128},... | collective-permute-start | bytes 147464 | tf_op jit(solution)/shard_map/ppermute | solution.py:414
  6.7 2.5 %second_part.1 = (f32[64,128]{1,0:T(8,128)}, bf16[128,128]{1,0:T(8,128)(2,1)}, bf16[64,128]{1,0:T(8,128)(2,1)}, bf16[192,128]{1,0:T(8,128)(2,1)}, bf16[256,128]{1,0:T(8,128)(2,1)}, /*index=5*/f32[8,128]{1,0:T(8,128)}) custom-call(s32[1]{0:T(128)} %bitcast.4.base, s32[51]{0:T(128)} %bitcast.56, s32[1]{0:T(128)} %bitcast.9.pick, bf16[4,8192]{1,0:T(4,128)(2,1)} %bitcast.52, ...), custom_call_target="tpu_custom_call" | custom-call | flops 16777216 | bytes 16777216 | tf_op jit(solution)/shard_map/second_part/pallas_call | solution.py:163
  9.2 10.3 %collective-permute-done.fed_ref = bf16[192,128]{1,0:T(8,128)(2,1)S(1)} collective-permute-done((bf16[192,128]{1,0:T(8,128)(2,1)}, bf16[192,128]{1,0:T(8,128)(2,1)S(1)}, u32[]{:S(2)}, u32[]{:S(2)}) %collective-permute-start) | collective-permute-done | bytes 49184 | tf_op jit(solution)/shard_map/ppermute | solution.py:414
  19.6 0.6 copy-done.10
  20.2 2.0 %third_part.1 = bf16[16,232,128]{2,1,0:T(8,128)(2,1)} custom-call(s32[1]{0:T(128)} %bitcast.2.flags, bf16[192,128]{1,0:T(8,128)(2,1)} %copy-done.10, bf16[192,128]{1,0:T(8,128)(2,1)} %get-tuple-element.26.head_ref, bf16[128,128]{1,0:T(8,128)(2,1)} %get-tuple-element.27.own_ref, bf16[64,128]{1,0:T(8,128)(2,1)} %get-tuple-element.28.tail_ref, ...), custom_call_target="tpu_custom_call" | custom-call | flops 1048576 | bytes 1048576 | tf_op jit(solution)/shard_map/third_part/pallas_call | solution.py:185
  22.2 7.3 %all-to-all-start = ((bf16[16,232,128]{2,1,0:T(8,128)(2,1)}), bf16[16,232,128]{2,1,0:T(8,128)(2,1)S(1)}, u32[]{:S(2)}, u32[]{:S(2)}) async-start(bf16[16,232,128]{2,1,0:T(8,128)(2,1)} %third_part.1), calls=%async_computation | async-start | bytes 1900544 | tf_op jit(solution)/shard_map/all_to_all | solution.py:416
  29.5 2.3 %collective-permute-start.1 = (bf16[8192,128]{1,0:T(8,128)(2,1)S(1)}, bf16[8192,128]{1,0:T(8,128)(2,1)}, u32[]{:S(2)}, u32[]{:S(2)}) collective-permute-start(bf16[8192,128]{1,0:T(8,128)(2,1)S(1)} %bitcast.41), channel_id=1, source_target_pairs={{0,8},{8,0},{1,9},{9,1},{2,10},{10,2},{3,11},{11,3},{4,12},{12,4},... | collective-permute-start | bytes 6291464 | tf_op jit(solution)/shard_map/ppermute | solution.py:402
  31.9 21.1 %all-to-all-done = bf16[16,232,128]{2,1,0:T(8,128)(2,1)S(1)} async-done(((bf16[16,232,128]{2,1,0:T(8,128)(2,1)}), bf16[16,232,128]{2,1,0:T(8,128)(2,1)S(1)}, u32[]{:S(2)}, u32[]{:S(2)}) %all-to-all-start) | async-done | bytes 950304 | tf_op jit(solution)/shard_map/all_to_all | solution.py:416
  53.0 0.9 copy-done.9
  54.0 1.3 copy.11
  55.3 0.2 convert_reduce_fusion.1
  55.5 0.1 multiply_cosine_fusion.1
  55.8 3.9 %shard_map.82 = (bf16[16,16384]{1,0:T(8,128)(2,1)}, bf16[16,16,128]{2,1,0:T(8,128)(2,1)}) custom-call(s32[4]{0:T(128)S(1)} %pad_add_fusion.refs_0_.flags, bf16[16,29696]{1,0:T(8,128)(2,1)S(1)} %bitcast.27, bf16[16,29696]{1,0:T(8,128)(2,1)S(1)} %bitcast.28, bf16[16,29696]{1,0:T(8,128)(2,1)S(1)} %bitcast.29, bf16[16,29696]{1,0:T(8,128)(2,1)S(1)} %bitcast.30, ...), custom_call_target="tpu_custom_call" | custom-call | flops 67108864 | bytes 6291456 | tf_op jit(solution)/shard_map/pallas_call | solution.py:287
  59.7 2.1 %collective-permute-start.2 = (bf16[16,16384]{1,0:T(8,128)(2,1)}, bf16[16,16384]{1,0:T(8,128)(2,1)}, u32[]{:S(2)}, u32[]{:S(2)}) collective-permute-start(bf16[16,16384]{1,0:T(8,128)(2,1)} %get-tuple-element.31.refs_0_), channel_id=1, source_target_pairs={{0,24},{1,25},{2,26},{3,27},{4,28},{5,29},{6,30},{7,31},{16,40},{1... | collective-permute-start | bytes 1572872 | tf_op jit(solution)/shard_map/ppermute | solution.py:431
  61.8 5.8 %all-to-all-start.1 = ((bf16[16,16,128]{2,1,0:T(8,128)(2,1)}), bf16[16,16,128]{2,1,0:T(8,128)(2,1)S(1)}, u32[]{:S(2)}, u32[]{:S(2)}) async-start(bf16[16,16,128]{2,1,0:T(8,128)(2,1)} %get-tuple-element.32.refs_12_), calls=%async_computation.1 | async-start | bytes 131072 | tf_op jit(solution)/shard_map/all_to_all | solution.py:432
  67.6 1.5 %collective-permute-start.4 = (bf16[16,16384]{1,0:T(8,128)(2,1)}, bf16[16,16384]{1,0:T(8,128)(2,1)}, u32[]{:S(2)}, u32[]{:S(2)}) collective-permute-start(bf16[16,16384]{1,0:T(8,128)(2,1)} %get-tuple-element.31.refs_0_), channel_id=1, source_target_pairs={{760,0},{761,1},{762,2},{763,3},{764,4},{765,5},{766,6},{767,7},{2... | collective-permute-start | bytes 1572872 | tf_op jit(solution)/shard_map/ppermute | solution.py:434
  69.0 6.5 %all-to-all-done.1.refs_9_ = bf16[16,16,128]{2,1,0:T(8,128)(2,1)S(1)} async-done(((bf16[16,16,128]{2,1,0:T(8,128)(2,1)}), bf16[16,16,128]{2,1,0:T(8,128)(2,1)S(1)}, u32[]{:S(2)}, u32[]{:S(2)}) %all-to-all-start.1) | async-done | bytes 65568 | tf_op jit(solution)/shard_map/all_to_all | solution.py:432
  75.5 4.6 %shard_map.83 = (bf16[16,16384]{1,0:T(8,128)(2,1)}, bf16[16,16,128]{2,1,0:T(8,128)(2,1)}) custom-call(s32[4]{0:T(128)S(1)} %pad_add_fusion.refs_0_.flags, bf16[16,16384]{1,0:T(8,128)(2,1)} %collective-permute-done.2.refs_1_.refs_2_, bf16[16,16384]{1,0:T(8,128)(2,1)} %collective-permute-done.2.refs_1_.refs_2_, bf16[16,29696]{1,0:T(8,128)(2,1)S(1)} %bitcast.31, ...), custom_call_target="tpu_custom_call" | custom-call | flops 67108864 | bytes 6291456 | tf_op jit(solution)/shard_map/pallas_call | solution.py:287
  80.1 1.3 collective-permute-start.3
  81.4 8.6 %all-to-all-start.2 = ((bf16[16,16,128]{2,1,0:T(8,128)(2,1)}), bf16[16,16,128]{2,1,0:T(8,128)(2,1)S(1)}, u32[]{:S(2)}, u32[]{:S(2)}) async-start(bf16[16,16,128]{2,1,0:T(8,128)(2,1)} %get-tuple-element.34.refs_13_), calls=%async_computation.2 | async-start | bytes 131072 | tf_op jit(solution)/shard_map/all_to_all | solution.py:432
  90.0 7.2 %all-to-all-done.2.refs_9_ = bf16[16,16,128]{2,1,0:T(8,128)(2,1)S(1)} async-done(((bf16[16,16,128]{2,1,0:T(8,128)(2,1)}), bf16[16,16,128]{2,1,0:T(8,128)(2,1)S(1)}, u32[]{:S(2)}, u32[]{:S(2)}) %all-to-all-start.2) | async-done | bytes 65568 | tf_op jit(solution)/shard_map/all_to_all | solution.py:432
  97.2 4.0 %shard_map.84 = (bf16[16,16384]{1,0:T(8,128)(2,1)S(1)}, bf16[16,16,128]{2,1,0:T(8,128)(2,1)S(1)}) custom-call(s32[4]{0:T(128)S(1)} %pad_add_fusion.refs_0_.flags, bf16[16,16384]{1,0:T(8,128)(2,1)} %collective-permute-done.3.refs_1_.refs_2_, bf16[16,16384]{1,0:T(8,128)(2,1)} %collective-permute-done.3.refs_1_.refs_2_, bf16[16,29696]{1,0:T(8,128)(2,1)S(1)} %bitcast.35, ...), custom_call_target="tpu_custom_call" | custom-call | flops 67108864 | bytes 6291456 | tf_op jit(solution)/shard_map/pallas_call | solution.py:287
  101.3 1.3 collective-permute-start.5
  102.6 10.5 %all_to_all.25.refs_9_ = bf16[16,16,128]{2,1,0:T(8,128)(2,1)S(1)} all-to-all(bf16[16,16,128]{2,1,0:T(8,128)(2,1)S(1)} %get-tuple-element.36.refs_14_), channel_id=1, replica_groups={{0,1,2,3,4,5,6,7,24,25,26,27,28,29,30,31},{16,17,18,19,20,21,22,23,40,4..., dimensions={0} | all-to-all | bytes 131072 | tf_op jit(solution)/shard_map/all_to_all | solution.py:432
  113.1 3.9 %shard_map.85 = (bf16[16,16384]{1,0:T(8,128)(2,1)S(1)}, bf16[16,2,128]{2,1,0:T(2,128)(2,1)S(1)}) custom-call(s32[4]{0:T(128)S(1)} %pad_add_fusion.refs_0_.flags, bf16[16,16384]{1,0:T(8,128)(2,1)S(1)} %collective-permute-done.5.refs_1_.refs_2_, bf16[16,16384]{1,0:T(8,128)(2,1)S(1)} %collective-permute-done.5.refs_1_.refs_2_, bf16[16,29696]{1,0:T(8,128)(2,1)S(1)} %bitcast.38, ...), custom_call_target="tpu_custom_call" | custom-call | flops 67108864 | bytes 6291456 | tf_op jit(solution)/shard_map/pallas_call | solution.py:287
  117.1 0.8 copy-done.3
  117.9 2.6 %pick_rows.1 = (bf16[2,16384]{1,0:T(2,128)(2,1)}, bf16[2,16384]{1,0:T(2,128)(2,1)}) custom-call(s32[4]{0:T(128)} %copy-done.7, bf16[16,16384]{1,0:T(8,128)(2,1)} %get-tuple-element.31.refs_0_, bf16[16,16384]{1,0:T(8,128)(2,1)} %get-tuple-element.33.refs_1_, bf16[16,16384]{1,0:T(8,128)(2,1)} %copy-done.2, bf16[16,16384]{1,0:T(8,128)(2,1)} %copy-done.3), custom_call_target="tpu_custom_call" | custom-call | flops 1048576 | bytes 2097152 | tf_op jit(solution)/shard_map/pick_rows/pallas_call | solution.py:329
  120.5 5.1 %collective-permute-start.6 = (bf16[2,16384]{1,0:T(2,128)(2,1)}, bf16[2,16384]{1,0:T(2,128)(2,1)S(1)}, u32[]{:S(2)}, u32[]{:S(2)}) collective-permute-start(bf16[2,16384]{1,0:T(2,128)(2,1)} %get-tuple-element.39), channel_id=1, source_target_pairs={{0,8},{8,0},{1,9},{9,1},{2,10},{10,2},{3,11},{11,3},{4,12},{12,4},... | collective-permute-start | bytes 196616 | tf_op jit(solution)/shard_map/ppermute | solution.py:442
  125.7 11.8 %all_to_all.26.told_ref = bf16[16,2,128]{2,1,0:T(2,128)(2,1)S(1)} all-to-all(bf16[16,2,128]{2,1,0:T(2,128)(2,1)S(1)} %get-tuple-element.40), channel_id=1, replica_groups=mesh['section'=48,'row'=2,'col'=8] {'row','col'}, dimensions={0} | all-to-all | bytes 16384 | tf_op jit(solution)/shard_map/all_to_all | solution.py:440
  137.5 0.8 copy-done.5
  138.4 1.5 %last_part.1 = bf16[4,16384]{1,0:T(4,128)(2,1)} custom-call(s32[4]{0:T(128)S(1)} %copy-done.8, bf16[2,16384]{1,0:T(2,128)(2,1)S(1)} %copy-done.5, bf16[2,16384]{1,0:T(2,128)(2,1)S(1)} %collective-permute-done.6.swap_ref, bf16[16,2,128]{2,1,0:T(2,128)(2,1)S(1)} %all_to_all.26.told_ref, f32[192,128]{1,0:T(8,128)S(1)} %copy-done.4, f32[64,128]{1,0:T(8,128)S(1)} %copy-done.6), custom_call_target="tpu_custom_call" | custom-call | flops 1048576 | bytes 1048576 | tf_op jit(solution)/shard_map/last_part/pallas_call | solution.py:365
  (29 shorter events, 0.3 us)
Async XLA Ops:
  2.4 17.1 %collective-permute-start = (bf16[192,128]{1,0:T(8,128)(2,1)}, bf16[192,128]{1,0:T(8,128)(2,1)S(1)}, u32[]{:S(2)}, u32[]{:S(2)}) collective-permute-start(bf16[192,128]{1,0:T(8,128)(2,1)} %get-tuple-element.24), channel_id=1, source_target_pairs={{0,16},{16,32},{32,48},{48,64},{64,80},{80,96},{96,112},{112,128},... | collective-permute-start | bytes 147464 | tf_op jit(solution)/shard_map/ppermute | solution.py:414
  6.7 22.8 %copy-start = (bf16[1,8192,128]{2,1,0:T(8,128)(2,1)S(1)}, bf16[1,8192,128]{2,1,0:T(8,128)(2,1)}, u32[]{:S(2)}) copy-start(bf16[1,8192,128]{2,1,0:T(8,128)(2,1)} %param.11) | copy-start | bytes 6291460
  19.6 0.6 copy-start.10
  22.2 33.6 %copy-start.1 = (bf16[1,16384]{1,0:T(2,128)(2,1)S(1)}, bf16[1,16384]{1,0:T(2,128)(2,1)}, u32[]{:S(2)}) copy-start(bf16[1,16384]{1,0:T(2,128)(2,1)} %refs_6_.7) | copy-start | bytes 98308
  22.2 30.9 %all-to-all-start = ((bf16[16,232,128]{2,1,0:T(8,128)(2,1)}), bf16[16,232,128]{2,1,0:T(8,128)(2,1)S(1)}, u32[]{:S(2)}, u32[]{:S(2)}) async-start(bf16[16,232,128]{2,1,0:T(8,128)(2,1)} %third_part.1), calls=%async_computation | async-start | bytes 1900544 | tf_op jit(solution)/shard_map/all_to_all | solution.py:416
  29.5 26.3 %collective-permute-start.1 = (bf16[8192,128]{1,0:T(8,128)(2,1)S(1)}, bf16[8192,128]{1,0:T(8,128)(2,1)}, u32[]{:S(2)}, u32[]{:S(2)}) collective-permute-start(bf16[8192,128]{1,0:T(8,128)(2,1)S(1)} %bitcast.41), channel_id=1, source_target_pairs={{0,8},{8,0},{1,9},{9,1},{2,10},{10,2},{3,11},{11,3},{4,12},{12,4},... | collective-permute-start | bytes 6291464 | tf_op jit(solution)/shard_map/ppermute | solution.py:402
  31.9 81.2 %copy-start.7 = (s32[4]{0:T(128)}, s32[4]{0:T(128)S(1)}, u32[]{:S(2)}) copy-start(s32[4]{0:T(128)S(1)} %pad_add_fusion.refs_0_.flags) | copy-start | bytes 52
  53.0 0.9 copy-start.9
  59.7 15.9 %collective-permute-start.2 = (bf16[16,16384]{1,0:T(8,128)(2,1)}, bf16[16,16384]{1,0:T(8,128)(2,1)}, u32[]{:S(2)}, u32[]{:S(2)}) collective-permute-start(bf16[16,16384]{1,0:T(8,128)(2,1)} %get-tuple-element.31.refs_0_), channel_id=1, source_target_pairs={{0,24},{1,25},{2,26},{3,27},{4,28},{5,29},{6,30},{7,31},{16,40},{1... | collective-permute-start | bytes 1572872 | tf_op jit(solution)/shard_map/ppermute | solution.py:431
  61.8 13.8 %all-to-all-start.1 = ((bf16[16,16,128]{2,1,0:T(8,128)(2,1)}), bf16[16,16,128]{2,1,0:T(8,128)(2,1)S(1)}, u32[]{:S(2)}, u32[]{:S(2)}) async-start(bf16[16,16,128]{2,1,0:T(8,128)(2,1)} %get-tuple-element.32.refs_12_), calls=%async_computation.1 | async-start | bytes 131072 | tf_op jit(solution)/shard_map/all_to_all | solution.py:432
  67.6 22.4 %collective-permute-start.4 = (bf16[16,16384]{1,0:T(8,128)(2,1)}, bf16[16,16384]{1,0:T(8,128)(2,1)}, u32[]{:S(2)}, u32[]{:S(2)}) collective-permute-start(bf16[16,16384]{1,0:T(8,128)(2,1)} %get-tuple-element.31.refs_0_), channel_id=1, source_target_pairs={{760,0},{761,1},{762,2},{763,3},{764,4},{765,5},{766,6},{767,7},{2... | collective-permute-start | bytes 1572872 | tf_op jit(solution)/shard_map/ppermute | solution.py:434
  80.1 17.1 %collective-permute-start.3 = (bf16[16,16384]{1,0:T(8,128)(2,1)}, bf16[16,16384]{1,0:T(8,128)(2,1)}, u32[]{:S(2)}, u32[]{:S(2)}) collective-permute-start(bf16[16,16384]{1,0:T(8,128)(2,1)} %get-tuple-element.33.refs_1_), channel_id=1, source_target_pairs={{8,16},{9,17},{10,18},{11,19},{12,20},{13,21},{14,22},{15,23},{24,... | collective-permute-start | bytes 1572872 | tf_op jit(solution)/shard_map/ppermute | solution.py:431
  81.4 15.8 %all-to-all-start.2 = ((bf16[16,16,128]{2,1,0:T(8,128)(2,1)}), bf16[16,16,128]{2,1,0:T(8,128)(2,1)S(1)}, u32[]{:S(2)}, u32[]{:S(2)}) async-start(bf16[16,16,128]{2,1,0:T(8,128)(2,1)} %get-tuple-element.34.refs_13_), calls=%async_computation.2 | async-start | bytes 131072 | tf_op jit(solution)/shard_map/all_to_all | solution.py:432
  101.3 1.3 copy-start.2
  101.3 11.9 %collective-permute-start.5 = (bf16[16,16384]{1,0:T(8,128)(2,1)S(1)}, bf16[16,16384]{1,0:T(8,128)(2,1)S(1)}, u32[]{:S(2)}, u32[]{:S(2)}) collective-permute-start(bf16[16,16384]{1,0:T(8,128)(2,1)S(1)} %get-tuple-element.35.refs_2_), channel_id=1, source_target_pairs={{0,24},{1,25},{2,26},{3,27},{4,28},{5,29},{6,30},{7,31},{16,40},{1... | collective-permute-start | bytes 1572872 | tf_op jit(solution)/shard_map/ppermute | solution.py:431
  117.1 0.8 copy-start.3
  117.9 19.6 %copy-start.4 = (f32[192,128]{1,0:T(8,128)S(1)}, f32[192,128]{1,0:T(8,128)}, u32[]{:S(2)}) copy-start(f32[192,128]{1,0:T(8,128)} %get-tuple-element.41.early_ref) | copy-start | bytes 294916
  117.9 19.6 %copy-start.6 = (f32[64,128]{1,0:T(8,128)S(1)}, f32[64,128]{1,0:T(8,128)}, u32[]{:S(2)}) copy-start(f32[64,128]{1,0:T(8,128)} %get-tuple-element.42.late_ref) | copy-start | bytes 98308
  117.9 19.6 %copy-start.8 = (s32[4]{0:T(128)S(1)}, s32[4]{0:T(128)}, u32[]{:S(2)}) copy-start(s32[4]{0:T(128)} %copy-done.7) | copy-start | bytes 52
  120.5 16.9 %collective-permute-start.6 = (bf16[2,16384]{1,0:T(2,128)(2,1)}, bf16[2,16384]{1,0:T(2,128)(2,1)S(1)}, u32[]{:S(2)}, u32[]{:S(2)}) collective-permute-start(bf16[2,16384]{1,0:T(2,128)(2,1)} %get-tuple-element.39), channel_id=1, source_target_pairs={{0,8},{8,0},{1,9},{9,1},{2,10},{10,2},{3,11},{11,3},{4,12},{12,4},... | collective-permute-start | bytes 196616 | tf_op jit(solution)/shard_map/ppermute | solution.py:442
  137.5 0.8 copy-start.5

commit v5 on v4

--- a/solution.py
+++ b/solution.py
@@ -201,12 +201,10 @@
         heard_ref, mean_ref, extra_ref = refs[:3]
         refs = refs[3:]
     if tick == 3:
-        spoken, refs = refs[:3], refs[3:]
-        x_ref, message_ref, scaled, held_there, arrived, both = refs
+        spoken, found, refs = refs[:3], refs[3:6], refs[6:]
+        x_ref, message_ref, pick_ref, scaled, exact, both = refs
     else:
-        x_ref, message_ref, scaled, held_there, arrived = refs
-    bring = pltpu.make_async_copy(there_ref, held_there, arrived)
-    bring.start()
+        x_ref, message_ref, pick_ref, scaled, exact = refs
     half = QH * HD
     rows = x_ref.shape[0]
     first = jnp.full((rows, HD), flags[2], jnp.int32) > 0
@@ -232,13 +230,12 @@
                 x = jnp.where(first, extra_ref[:, at].astype(f32), x.astype(f32)).astype(bf16)
         x_ref[:, n * HD : (n + 1) * HD] = x
         wide = x.astype(f32)
+        exact[n * rows : (n + 1) * rows, :] = wide
         square = square + wide * wide
         scaled[n // QH, :, at] = (wide * gain_ref[:, n * HD : (n + 1) * HD].astype(f32)).astype(bf16)
     fresh = jnp.zeros((rows, HD), f32)
     step = 2048
-    for ref, part in ((here_ref, flags[0]), (held_there, 1 - flags[0])):
-        if ref is held_there:
-            bring.wait()
+    for ref, part in ((here_ref, flags[0]), (there_ref, 1 - flags[0])):
         for k in range(0, half, step):
             fresh = fresh + jnp.dot(scaled[part, :, k : k + step], ref[k : k + step, :], preferred_element_type=f32)
     scale = lax.rsqrt(jnp.sum(square, axis=1, keepdims=True) / (2 * half) + 1e-05)
@@ -257,6 +254,15 @@
     own = jnp.where(lane < PER, 1.0 / (1.0 + jnp.exp(lse - score * FACTOR)), 0.0)
     is_key = jnp.full((rows, HD), flags[1], jnp.int32) > 0
     message = jnp.where(is_key, own, fresh).astype(bf16)
+    even = jnp.full((2, HD), flags[0], jnp.int32) == 0
+    for n in range(2 * QH):
+        at = slice(n * HD, (n + 1) * HD)
+        pair = exact[pl.ds(n * rows + flags[3], 2, stride=rows // 2), :]
+        if tick == 3:
+            early = jnp.where(even, found[0][:, at].astype(f32), found[1][:, at].astype(f32))
+            late = jnp.where(even, found[2][:, at].astype(f32), pair)
+            pair = jnp.concatenate([early, late], axis=0)
+        pick_ref[:, at] = pair.astype(bf16)
     if tick < 3:
         for d in range(message_ref.shape[0]):
             message_ref[d] = message
@@ -268,7 +274,7 @@
         message_ref[j] = both[pl.ds(j, 2, stride=rows), :].astype(bf16)
 
 
-def do_tick(tick, flags, x, got, turn, gain, here, there, heard=None, extra=None, spoken=()):
+def do_tick(tick, flags, x, got, turn, gain, here, there, heard=None, extra=None, spoken=(), found=()):
     rows, half = got.shape[0], QH * HD
     small = pl.BlockSpec(memory_space=pltpu.SMEM)
     held = pl.BlockSpec(memory_space=pltpu.VMEM)
@@ -277,63 +283,33 @@
         return pl.BlockSpec((rows, size), lambda i: (0, n))
 
     k = tick // 2
-    specs = [small, block(half, 0), block(half, 1), block(PER * HD, 12 + k), block(8 * HD, 28), held, held, held, pl.BlockSpec(memory_space=pl.ANY)]
+    specs = [small, block(half, 0), block(half, 1), block(PER * HD, 12 + k), block(8 * HD, 28), held, held, held, held]
     operands = [flags, x, x, got, got, turn, gain, here, there]
     if tick:
         specs += [held, block(half, 0 if tick == 3 else 2), block(half, 1)]
         operands += [heard, got, extra]
     specs += [pl.BlockSpec((1, rows, HD), lambda i: (0, 0, 0))] * len(spoken)
     operands += spoken
+    specs += [held] * len(found)
+    operands += found
     return pl.pallas_call(
         functools.partial(tick_kernel, tick),
         grid=(1,),
         out_shape=(
             jax.ShapeDtypeStruct((rows, 2 * half), bf16),
             jax.ShapeDtypeStruct((rows, 2 if tick == 3 else rows, HD), bf16),
+            jax.ShapeDtypeStruct((4 if tick == 3 else 2, 2 * half), bf16),
         ),
         in_specs=specs,
-        out_specs=(held, held),
+        out_specs=(held, held, held),
         scratch_shapes=[
             pltpu.VMEM((2, rows, half), bf16),
-            pltpu.VMEM(there.shape, bf16),
-            pltpu.SemaphoreType.DMA,
+            pltpu.VMEM((2 * QH * rows, HD), f32),
             *[pltpu.VMEM((2 * rows, HD), f32)] * (tick == 3),
         ],
         cost_estimate=pl.CostEstimate(flops=1 << 26, bytes_accessed=6 << 20, transcendentals=0),
         compiler_params=pltpu.CompilerParams(vmem_limit_bytes=20 << 20),
     )(*operands)
-
-
-def pick_kernel(flags, *refs):
-    xs, (mine_ref, other_ref) = refs[:4], refs[4:]
-    rows, width = xs[0].shape
-    sub = lax.broadcasted_iota(jnp.int32, (8, rows), 0)
-    lane = lax.broadcasted_iota(jnp.int32, (8, rows), 1)
-    wanted = jnp.where(sub < 2, flags[0] * 8 + flags[3], (1 - flags[0]) * 8 + flags[3])
-    selects = [jnp.where((lane == wanted) & (sub < 4) & (sub % 2 == k), 1.0, 0.0).astype(bf16) for k in range(2)]
-    for r in range(2):
-
-        @pl.when(flags[0] == r)
-        def _():
-            for n in range(0, width, 2048):
-                at = slice(n, n + 2048)
-                found = jnp.dot(selects[0], xs[r][:, at], preferred_element_type=f32)
-                found = found + jnp.dot(selects[1], xs[2 + r][:, at], preferred_element_type=f32)
-                mine_ref[:, at] = found[0:2].astype(bf16)
-                other_ref[:, at] = found[2:4].astype(bf16)
-
-
-def pick_rows(flags, *xs):
-    held = pl.BlockSpec(memory_space=pltpu.VMEM)
-    pair = jax.ShapeDtypeStruct((2, xs[0].shape[1]), bf16)
-    return pl.pallas_call(
-        pick_kernel,
-        out_shape=(pair, pair),
-        in_specs=[pl.BlockSpec(memory_space=pltpu.SMEM), *[held] * 4],
-        out_specs=(held, held),
-        cost_estimate=pl.CostEstimate(flops=1 << 20, bytes_accessed=2 << 20, transcendentals=0),
-        name="pick_rows",
-    )(flags, *xs)
 
 
 def last_kernel(flags, mine_ref, swap_ref, told_ref, early_ref, late_ref, out_ref, tell, mean):
@@ -344,14 +320,14 @@
             for k in range(2):
                 t = 2 * k + r
                 tell[c, t : t + 1, :] = told_ref[8 * r + c, k : k + 1, :].astype(f32)
-    even = jnp.full((2, HD), flags[0], jnp.int32) == 0
+    even = jnp.full((4, HD), flags[0], jnp.int32) == 0
     for n in range(2 * QH):
         at = slice(n * HD, (n + 1) * HD)
-        mine = mine_ref[:, at].astype(f32)
-        swap = swap_ref[:, at].astype(f32)
-        a = jnp.where(even, mine, swap)
-        b = jnp.where(even, swap, mine)
-        x = jnp.concatenate([a[0:1], b[0:1], a[1:2], b[1:2]], axis=0)
+        e = mine_ref[:, at].astype(f32)
+        f = swap_ref[:, at].astype(f32)
+        a = jnp.concatenate([e[0:1], f[0:1], e[2:3], f[2:3]], axis=0)
+        b = jnp.concatenate([f[1:2], e[1:2], f[3:4], e[3:4]], axis=0)
+        x = jnp.where(even, a, b)
         if n < QH:
             g, i = n // PER, n % PER
             cached = mean[pl.ds(n, 4, stride=QH), :]
@@ -420,11 +396,11 @@
     turns = jnp.stack([t for k in range(2) for t in angles(got[:, aux_at + k].astype(f32))])
     flags = jnp.stack([row_at, 1 - col_at % 2, first.astype(jnp.int32), col_at]).astype(jnp.int32)
 
-    rows, messages = [], []
+    found, messages = [], []
     for tick in range(ticks):
         step = functools.partial(do_tick, tick, flags, got=got, turn=turns, gain=gain, here=w_here, there=w_there)
         if tick == 0:
-            x, message = step(got)
+            x, message, rows = step(got)
         else:
             there = (tick - 1) % 2
             pairs = [(s, there, s + 1, 1 - there) for s in range(sections - 1)]
@@ -433,14 +409,14 @@
             if tick == 1:
                 tails = lax.ppermute(x, ALL, links([(sections - 1, 1, 0, 0), (1, 1, 0, 1)]))
             extra = got if tick == 1 else tails
-            x, message = step(relayed, heard=heard, extra=extra, spoken=messages if tick == 3 else [])
-        rows.append(x)
-        messages.append(message)
+            past = dict(spoken=messages, found=found) if tick == 3 else {}
+            x, message, rows = step(relayed, heard=heard, extra=extra, **past)
+        found = found + [rows]
+        messages = messages + [message]
 
     told = lax.all_to_all(messages[3], RC, split_axis=0, concat_axis=0, tiled=True)
-    mine, other = pick_rows(flags, *rows)
-    swapped = lax.ppermute(other, "row", [(0, 1), (1, 0)])
-    out = finish(flags, mine, swapped, told, early, late)
+    swapped = lax.ppermute(rows, "row", [(0, 1), (1, 0)])
+    out = finish(flags, rows, swapped, told, early, late)
     return out[None, :, None]
 
 

time: 141 us -> 134 us (0.950)
  Pallas kernels: 27.5 us -> 22.8 us
  local copies, waits for them, and re-layouts: 4.54 us -> 2.87 us
    pallas_call x1 -> x0, Pallas kernels: 2.63 us -> none  [pick_rows(): pl.pallas_call(pick_kernel, out_shape=(pair, pair), in_specs=[pl.BlockSpe...]
    pallas_call x4, Pallas kernels: 16.4 us -> 14.4 us  [do_tick(): pl.pallas_call(functools.partial(tick_kernel, tick), grid=(1,), out_shape...]
    unnamed x23 -> x13, local copies, waits for them, and re-layouts: 4.54 us -> 2.87 us
where the time goes in v5:
time: 134 us; the launch traced here: 133 us
  waiting for transfers between devices  45.1 us (34%)
  starting transfers between devices  39.5 us (29%)
  Pallas kernels  22.8 us (17%)
  blocking collectives  22.4 us (17%)
  local copies, waits for them, and re-layouts  2.87 us (2%)
    all_to_all x1, waiting for transfers between devices, inner(): got = lax.all_to_all(sent, RC, split_axis=0, concat_axis=0, tiled=True)  21.1 us
    all_to_all x2, starting transfers between devices, inner(): lax.all_to_all(message, ALL, split_axis=0, concat_axis=0, axis_index_grou...  14.4 us
    pallas_call x4, Pallas kernels, do_tick(): pl.pallas_call(functools.partial(tick_kernel, tick), grid=(1,), out_shape...  14.4 us
    all_to_all x2, waiting for transfers between devices, inner(): lax.all_to_all(message, ALL, split_axis=0, concat_axis=0, axis_index_grou...  13.7 us
    all_to_all x1, blocking collectives, inner(): lax.all_to_all(messages[3], RC, split_axis=0, concat_axis=0, tiled=True)  11.8 us
    all_to_all x1, blocking collectives, inner(): lax.all_to_all(message, ALL, split_axis=0, concat_axis=0, axis_index_grou...  10.6 us
    ppermute x1, waiting for transfers between devices, inner(): lax.ppermute(fed, 'section', [(s, s + 1) for s in range(sections - 1)])  10.3 us
    all_to_all x1, starting transfers between devices, inner(): got = lax.all_to_all(sent, RC, split_axis=0, concat_axis=0, tiled=True)  7.34 us
  transfers between devices with their start and end apart: 10, of which 4 were waited for; matrix products, arithmetic and copies ran while one was open for 1% of the time, Pallas kernels for 5%

profile of v5, /device:TPU:6, one launch (start us, length us, event | category | flops | bytes accessed | tf_op | source)
XLA Modules:
  0.0 133.4 jit_solution(10759371599596463271)
XLA Ops:
  0.0 2.4 %first_part.1 = (f32[192,128]{1,0:T(8,128)}, bf16[192,128]{1,0:T(8,128)(2,1)}, f32[8,128]{1,0:T(8,128)}) custom-call(s32[1]{0:T(128)} %bitcast.4.base, s32[51]{0:T(128)} %bitcast.55, bf16[4,8192]{1,0:T(4,128)(2,1)} %bitcast.51, bf16[4,128,512]{2,1,0:T(8,128)(2,1)} %bitcast.47, bf16[4,128,512]{2,1,0:T(8,128)(2,1)} %bitcast.49), custom_call_target="tpu_custom_call" | custom-call | flops 4194304 | bytes 4194304 | tf_op jit(solution)/shard_map/first_part/pallas_call | solution.py:148
  2.4 4.3 %collective-permute-start = (bf16[192,128]{1,0:T(8,128)(2,1)}, bf16[192,128]{1,0:T(8,128)(2,1)S(1)}, u32[]{:S(2)}, u32[]{:S(2)}) collective-permute-start(bf16[192,128]{1,0:T(8,128)(2,1)} %get-tuple-element.25), channel_id=1, source_target_pairs={{0,16},{16,32},{32,48},{48,64},{64,80},{80,96},{96,112},{112,128},... | collective-permute-start | bytes 147464 | tf_op jit(solution)/shard_map/ppermute | solution.py:390
  6.7 2.5 %second_part.1 = (f32[64,128]{1,0:T(8,128)}, bf16[128,128]{1,0:T(8,128)(2,1)}, bf16[64,128]{1,0:T(8,128)(2,1)}, bf16[192,128]{1,0:T(8,128)(2,1)}, bf16[256,128]{1,0:T(8,128)(2,1)}, /*index=5*/f32[8,128]{1,0:T(8,128)}) custom-call(s32[1]{0:T(128)} %bitcast.4.base, s32[51]{0:T(128)} %bitcast.56, s32[1]{0:T(128)} %bitcast.9.pick, bf16[4,8192]{1,0:T(4,128)(2,1)} %bitcast.52, ...), custom_call_target="tpu_custom_call" | custom-call | flops 16777216 | bytes 16777216 | tf_op jit(solution)/shard_map/second_part/pallas_call | solution.py:163
  9.2 10.3 %collective-permute-done.fed_ref = bf16[192,128]{1,0:T(8,128)(2,1)S(1)} collective-permute-done((bf16[192,128]{1,0:T(8,128)(2,1)}, bf16[192,128]{1,0:T(8,128)(2,1)S(1)}, u32[]{:S(2)}, u32[]{:S(2)}) %collective-permute-start) | collective-permute-done | bytes 49184 | tf_op jit(solution)/shard_map/ppermute | solution.py:390
  19.5 0.6 copy-done.5
  20.2 2.0 %third_part.1 = bf16[16,232,128]{2,1,0:T(8,128)(2,1)} custom-call(s32[1]{0:T(128)} %bitcast.2.flags, bf16[192,128]{1,0:T(8,128)(2,1)} %copy-done.5, bf16[192,128]{1,0:T(8,128)(2,1)} %get-tuple-element.27.head_ref, bf16[128,128]{1,0:T(8,128)(2,1)} %get-tuple-element.28.own_ref, bf16[64,128]{1,0:T(8,128)(2,1)} %get-tuple-element.29.tail_ref, ...), custom_call_target="tpu_custom_call" | custom-call | flops 1048576 | bytes 1048576 | tf_op jit(solution)/shard_map/third_part/pallas_call | solution.py:185
  22.1 7.3 %all-to-all-start = ((bf16[16,232,128]{2,1,0:T(8,128)(2,1)}), bf16[16,232,128]{2,1,0:T(8,128)(2,1)S(1)}, u32[]{:S(2)}, u32[]{:S(2)}) async-start(bf16[16,232,128]{2,1,0:T(8,128)(2,1)} %third_part.1), calls=%async_computation | async-start | bytes 1900544 | tf_op jit(solution)/shard_map/all_to_all | solution.py:392
  29.5 2.3 %collective-permute-start.1 = (bf16[8192,128]{1,0:T(8,128)(2,1)S(1)}, bf16[8192,128]{1,0:T(8,128)(2,1)}, u32[]{:S(2)}, u32[]{:S(2)}) collective-permute-start(bf16[8192,128]{1,0:T(8,128)(2,1)S(1)} %bitcast.41), channel_id=1, source_target_pairs={{0,8},{8,0},{1,9},{9,1},{2,10},{10,2},{3,11},{11,3},{4,12},{12,4},... | collective-permute-start | bytes 6291464 | tf_op jit(solution)/shard_map/ppermute | solution.py:378
  31.8 0.1 pad_add_fusion.refs_0_.flags
  31.9 21.1 %all-to-all-done = bf16[16,232,128]{2,1,0:T(8,128)(2,1)S(1)} async-done(((bf16[16,232,128]{2,1,0:T(8,128)(2,1)}), bf16[16,232,128]{2,1,0:T(8,128)(2,1)S(1)}, u32[]{:S(2)}, u32[]{:S(2)}) %all-to-all-start) | async-done | bytes 950304 | tf_op jit(solution)/shard_map/all_to_all | solution.py:392
  53.0 0.9 copy-done.4
  53.9 1.3 copy.11
  55.2 0.2 convert_reduce_fusion.1
  55.4 0.1 multiply_cosine_fusion.1
  55.6 0.1 maximum_bitcast_fusion
  55.6 0.1 maximum_bitcast_fusion.2
  55.7 3.4 %shard_map.82 = (bf16[16,16384]{1,0:T(8,128)(2,1)}, bf16[16,16,128]{2,1,0:T(8,128)(2,1)}, bf16[2,16384]{1,0:T(2,128)(2,1)S(1)}) custom-call(s32[4]{0:T(128)S(1)} %pad_add_fusion.refs_0_.flags, bf16[16,29696]{1,0:T(8,128)(2,1)S(1)} %bitcast.27, bf16[16,29696]{1,0:T(8,128)(2,1)S(1)} %bitcast.28, bf16[16,29696]{1,0:T(8,128)(2,1)S(1)} %bitcast.29, ...), custom_call_target="tpu_custom_call" | custom-call | flops 67108864 | bytes 6291456 | tf_op jit(solution)/shard_map/pallas_call | solution.py:295
  59.2 2.1 %collective-permute-start.2 = (bf16[16,16384]{1,0:T(8,128)(2,1)}, bf16[16,16384]{1,0:T(8,128)(2,1)}, u32[]{:S(2)}, u32[]{:S(2)}) collective-permute-start(bf16[16,16384]{1,0:T(8,128)(2,1)} %get-tuple-element.32), channel_id=1, source_target_pairs={{0,24},{1,25},{2,26},{3,27},{4,28},{5,29},{6,30},{7,31},{16,40},{1... | collective-permute-start | bytes 1572872 | tf_op jit(solution)/shard_map/ppermute | solution.py:407
  61.2 5.8 %all-to-all-start.1 = ((bf16[16,16,128]{2,1,0:T(8,128)(2,1)}), bf16[16,16,128]{2,1,0:T(8,128)(2,1)S(1)}, u32[]{:S(2)}, u32[]{:S(2)}) async-start(bf16[16,16,128]{2,1,0:T(8,128)(2,1)} %get-tuple-element.33.refs_12_), calls=%async_computation.1 | async-start | bytes 131072 | tf_op jit(solution)/shard_map/all_to_all | solution.py:408
  67.1 1.5 %collective-permute-start.4 = (bf16[16,16384]{1,0:T(8,128)(2,1)}, bf16[16,16384]{1,0:T(8,128)(2,1)}, u32[]{:S(2)}, u32[]{:S(2)}) collective-permute-start(bf16[16,16384]{1,0:T(8,128)(2,1)} %get-tuple-element.32), channel_id=1, source_target_pairs={{760,0},{761,1},{762,2},{763,3},{764,4},{765,5},{766,6},{767,7},{2... | collective-permute-start | bytes 1572872 | tf_op jit(solution)/shard_map/ppermute | solution.py:410
  68.5 6.5 %all-to-all-done.1.refs_9_ = bf16[16,16,128]{2,1,0:T(8,128)(2,1)S(1)} async-done(((bf16[16,16,128]{2,1,0:T(8,128)(2,1)}), bf16[16,16,128]{2,1,0:T(8,128)(2,1)S(1)}, u32[]{:S(2)}, u32[]{:S(2)}) %all-to-all-start.1) | async-done | bytes 65568 | tf_op jit(solution)/shard_map/all_to_all | solution.py:408
  75.0 3.8 %shard_map.83 = (bf16[16,16384]{1,0:T(8,128)(2,1)}, bf16[16,16,128]{2,1,0:T(8,128)(2,1)}, bf16[2,16384]{1,0:T(2,128)(2,1)S(1)}) custom-call(s32[4]{0:T(128)S(1)} %pad_add_fusion.refs_0_.flags, bf16[16,16384]{1,0:T(8,128)(2,1)} %collective-permute-done.2.refs_1_.refs_2_, bf16[16,16384]{1,0:T(8,128)(2,1)} %collective-permute-done.2.refs_1_.refs_2_, ...), custom_call_target="tpu_custom_call" | custom-call | flops 67108864 | bytes 6291456 | tf_op jit(solution)/shard_map/pallas_call | solution.py:295
  78.8 1.3 collective-permute-start.3
  80.1 8.6 %all-to-all-start.2 = ((bf16[16,16,128]{2,1,0:T(8,128)(2,1)}), bf16[16,16,128]{2,1,0:T(8,128)(2,1)S(1)}, u32[]{:S(2)}, u32[]{:S(2)}) async-start(bf16[16,16,128]{2,1,0:T(8,128)(2,1)} %get-tuple-element.35.refs_13_), calls=%async_computation.2 | async-start | bytes 131072 | tf_op jit(solution)/shard_map/all_to_all | solution.py:408
  88.7 7.2 %all-to-all-done.2.refs_9_ = bf16[16,16,128]{2,1,0:T(8,128)(2,1)S(1)} async-done(((bf16[16,16,128]{2,1,0:T(8,128)(2,1)}), bf16[16,16,128]{2,1,0:T(8,128)(2,1)S(1)}, u32[]{:S(2)}, u32[]{:S(2)}) %all-to-all-start.2) | async-done | bytes 65568 | tf_op jit(solution)/shard_map/all_to_all | solution.py:408
  95.9 3.2 %shard_map.84 = (bf16[16,16384]{1,0:T(8,128)(2,1)S(1)}, bf16[16,16,128]{2,1,0:T(8,128)(2,1)S(1)}, bf16[2,16384]{1,0:T(2,128)(2,1)S(1)}) custom-call(s32[4]{0:T(128)S(1)} %pad_add_fusion.refs_0_.flags, bf16[16,16384]{1,0:T(8,128)(2,1)} %collective-permute-done.3.refs_1_.refs_2_, bf16[16,16384]{1,0:T(8,128)(2,1)} %collective-permute-done.3.refs_1_.refs_2_, ...), custom_call_target="tpu_custom_call" | custom-call | flops 67108864 | bytes 6291456 | tf_op jit(solution)/shard_map/pallas_call | solution.py:295
  99.1 1.3 collective-permute-start.5
  100.4 10.6 %all_to_all.25.refs_9_ = bf16[16,16,128]{2,1,0:T(8,128)(2,1)S(1)} all-to-all(bf16[16,16,128]{2,1,0:T(8,128)(2,1)S(1)} %get-tuple-element.37.refs_14_), channel_id=1, replica_groups={{0,1,2,3,4,5,6,7,24,25,26,27,28,29,30,31},{16,17,18,19,20,21,22,23,40,4..., dimensions={0} | all-to-all | bytes 131072 | tf_op jit(solution)/shard_map/all_to_all | solution.py:408
  111.0 4.0 %shard_map.85 = (bf16[16,16384]{1,0:T(8,128)(2,1)}, bf16[16,2,128]{2,1,0:T(2,128)(2,1)S(1)}, bf16[4,16384]{1,0:T(4,128)(2,1)S(1)}) custom-call(s32[4]{0:T(128)S(1)} %pad_add_fusion.refs_0_.flags, bf16[16,16384]{1,0:T(8,128)(2,1)S(1)} %collective-permute-done.5.refs_1_.refs_2_, bf16[16,16384]{1,0:T(8,128)(2,1)S(1)} %collective-permute-done.5.refs_1_.refs_2_, ...), custom_call_target="tpu_custom_call" | custom-call | flops 67108864 | bytes 6291456 | tf_op jit(solution)/shard_map/pallas_call | solution.py:295
  115.0 5.1 %collective-permute-start.6 = (bf16[4,16384]{1,0:T(4,128)(2,1)S(1)}, bf16[4,16384]{1,0:T(4,128)(2,1)S(1)}, u32[]{:S(2)}, u32[]{:S(2)}) collective-permute-start(bf16[4,16384]{1,0:T(4,128)(2,1)S(1)} %get-tuple-element.41.mine_ref), channel_id=1, source_target_pairs={{0,8},{8,0},{1,9},{9,1},{2,10},{10,2},{3,11},{11,3},{4,12},{12,4},... | collective-permute-start | bytes 393224 | tf_op jit(solution)/shard_map/ppermute | solution.py:418
  120.0 11.8 %all_to_all.26.told_ref = bf16[16,2,128]{2,1,0:T(2,128)(2,1)S(1)} all-to-all(bf16[16,2,128]{2,1,0:T(2,128)(2,1)S(1)} %get-tuple-element.42), channel_id=1, replica_groups=mesh['section'=48,'row'=2,'col'=8] {'row','col'}, dimensions={0} | all-to-all | bytes 16384 | tf_op jit(solution)/shard_map/all_to_all | solution.py:417
  131.9 1.5 %last_part.1 = bf16[4,16384]{1,0:T(4,128)(2,1)} custom-call(s32[4]{0:T(128)S(1)} %pad_add_fusion.refs_0_.flags, bf16[4,16384]{1,0:T(4,128)(2,1)S(1)} %get-tuple-element.41.mine_ref, bf16[4,16384]{1,0:T(4,128)(2,1)S(1)} %collective-permute-done.6.swap_ref, bf16[16,2,128]{2,1,0:T(2,128)(2,1)S(1)} %all_to_all.26.told_ref, f32[192,128]{1,0:T(8,128)S(1)} %copy-done.2, ...), custom_call_target="tpu_custom_call" | custom-call | flops 1048576 | bytes 1048576 | tf_op jit(solution)/shard_map/last_part/pallas_call | solution.py:341
  (18 shorter events, 0.0 us)
Async XLA Ops:
  2.4 17.1 %collective-permute-start = (bf16[192,128]{1,0:T(8,128)(2,1)}, bf16[192,128]{1,0:T(8,128)(2,1)S(1)}, u32[]{:S(2)}, u32[]{:S(2)}) collective-permute-start(bf16[192,128]{1,0:T(8,128)(2,1)} %get-tuple-element.25), channel_id=1, source_target_pairs={{0,16},{16,32},{32,48},{48,64},{64,80},{80,96},{96,112},{112,128},... | collective-permute-start | bytes 147464 | tf_op jit(solution)/shard_map/ppermute | solution.py:390
  6.7 22.7 %copy-start = (bf16[1,8192,128]{2,1,0:T(8,128)(2,1)S(1)}, bf16[1,8192,128]{2,1,0:T(8,128)(2,1)}, u32[]{:S(2)}) copy-start(bf16[1,8192,128]{2,1,0:T(8,128)(2,1)} %param.11) | copy-start | bytes 6291460
  19.5 0.6 copy-start.5
  22.1 33.6 %copy-start.1 = (bf16[1,16384]{1,0:T(2,128)(2,1)S(1)}, bf16[1,16384]{1,0:T(2,128)(2,1)}, u32[]{:S(2)}) copy-start(bf16[1,16384]{1,0:T(2,128)(2,1)} %refs_6_.7) | copy-start | bytes 98308
  22.1 30.9 %all-to-all-start = ((bf16[16,232,128]{2,1,0:T(8,128)(2,1)}), bf16[16,232,128]{2,1,0:T(8,128)(2,1)S(1)}, u32[]{:S(2)}, u32[]{:S(2)}) async-start(bf16[16,232,128]{2,1,0:T(8,128)(2,1)} %third_part.1), calls=%async_computation | async-start | bytes 1900544 | tf_op jit(solution)/shard_map/all_to_all | solution.py:392
  29.5 26.2 %collective-permute-start.1 = (bf16[8192,128]{1,0:T(8,128)(2,1)S(1)}, bf16[8192,128]{1,0:T(8,128)(2,1)}, u32[]{:S(2)}, u32[]{:S(2)}) collective-permute-start(bf16[8192,128]{1,0:T(8,128)(2,1)S(1)} %bitcast.41), channel_id=1, source_target_pairs={{0,8},{8,0},{1,9},{9,1},{2,10},{10,2},{3,11},{11,3},{4,12},{12,4},... | collective-permute-start | bytes 6291464 | tf_op jit(solution)/shard_map/ppermute | solution.py:378
  53.0 0.9 copy-start.4
  59.2 15.9 %collective-permute-start.2 = (bf16[16,16384]{1,0:T(8,128)(2,1)}, bf16[16,16384]{1,0:T(8,128)(2,1)}, u32[]{:S(2)}, u32[]{:S(2)}) collective-permute-start(bf16[16,16384]{1,0:T(8,128)(2,1)} %get-tuple-element.32), channel_id=1, source_target_pairs={{0,24},{1,25},{2,26},{3,27},{4,28},{5,29},{6,30},{7,31},{16,40},{1... | collective-permute-start | bytes 1572872 | tf_op jit(solution)/shard_map/ppermute | solution.py:407
  61.2 13.8 %all-to-all-start.1 = ((bf16[16,16,128]{2,1,0:T(8,128)(2,1)}), bf16[16,16,128]{2,1,0:T(8,128)(2,1)S(1)}, u32[]{:S(2)}, u32[]{:S(2)}) async-start(bf16[16,16,128]{2,1,0:T(8,128)(2,1)} %get-tuple-element.33.refs_12_), calls=%async_computation.1 | async-start | bytes 131072 | tf_op jit(solution)/shard_map/all_to_all | solution.py:408
  67.1 21.6 %collective-permute-start.4 = (bf16[16,16384]{1,0:T(8,128)(2,1)}, bf16[16,16384]{1,0:T(8,128)(2,1)}, u32[]{:S(2)}, u32[]{:S(2)}) collective-permute-start(bf16[16,16384]{1,0:T(8,128)(2,1)} %get-tuple-element.32), channel_id=1, source_target_pairs={{760,0},{761,1},{762,2},{763,3},{764,4},{765,5},{766,6},{767,7},{2... | collective-permute-start | bytes 1572872 | tf_op jit(solution)/shard_map/ppermute | solution.py:410
  78.8 17.1 %collective-permute-start.3 = (bf16[16,16384]{1,0:T(8,128)(2,1)}, bf16[16,16384]{1,0:T(8,128)(2,1)}, u32[]{:S(2)}, u32[]{:S(2)}) collective-permute-start(bf16[16,16384]{1,0:T(8,128)(2,1)} %get-tuple-element.34), channel_id=1, source_target_pairs={{8,16},{9,17},{10,18},{11,19},{12,20},{13,21},{14,22},{15,23},{24,... | collective-permute-start | bytes 1572872 | tf_op jit(solution)/shard_map/ppermute | solution.py:407
  80.1 15.8 %all-to-all-start.2 = ((bf16[16,16,128]{2,1,0:T(8,128)(2,1)}), bf16[16,16,128]{2,1,0:T(8,128)(2,1)S(1)}, u32[]{:S(2)}, u32[]{:S(2)}) async-start(bf16[16,16,128]{2,1,0:T(8,128)(2,1)} %get-tuple-element.35.refs_13_), calls=%async_computation.2 | async-start | bytes 131072 | tf_op jit(solution)/shard_map/all_to_all | solution.py:408
  99.1 11.9 %collective-permute-start.5 = (bf16[16,16384]{1,0:T(8,128)(2,1)S(1)}, bf16[16,16384]{1,0:T(8,128)(2,1)S(1)}, u32[]{:S(2)}, u32[]{:S(2)}) collective-permute-start(bf16[16,16384]{1,0:T(8,128)(2,1)S(1)} %get-tuple-element.36), channel_id=1, source_target_pairs={{0,24},{1,25},{2,26},{3,27},{4,28},{5,29},{6,30},{7,31},{16,40},{1... | collective-permute-start | bytes 1572872 | tf_op jit(solution)/shard_map/ppermute | solution.py:407
  111.0 20.9 %copy-start.2 = (f32[192,128]{1,0:T(8,128)S(1)}, f32[192,128]{1,0:T(8,128)}, u32[]{:S(2)}) copy-start(f32[192,128]{1,0:T(8,128)} %get-tuple-element.43.early_ref) | copy-start | bytes 294916
  111.0 20.9 %copy-start.3 = (f32[64,128]{1,0:T(8,128)S(1)}, f32[64,128]{1,0:T(8,128)}, u32[]{:S(2)}) copy-start(f32[64,128]{1,0:T(8,128)} %get-tuple-element.44.late_ref) | copy-start | bytes 98308
  115.0 16.9 %collective-permute-start.6 = (bf16[4,16384]{1,0:T(4,128)(2,1)S(1)}, bf16[4,16384]{1,0:T(4,128)(2,1)S(1)}, u32[]{:S(2)}, u32[]{:S(2)}) collective-permute-start(bf16[4,16384]{1,0:T(4,128)(2,1)S(1)} %get-tuple-element.41.mine_ref), channel_id=1, source_target_pairs={{0,8},{8,0},{1,9},{9,1},{2,10},{10,2},{3,11},{11,3},{4,12},{12,4},... | collective-permute-start | bytes 393224 | tf_op jit(solution)/shard_map/ppermute | solution.py:418

commit v6 on v5

--- a/solution.py
+++ b/solution.py
@@ -202,11 +202,12 @@
         refs = refs[3:]
     if tick == 3:
         spoken, found, refs = refs[:3], refs[3:6], refs[6:]
-        x_ref, message_ref, pick_ref, scaled, exact, both = refs
+        x_ref = None
+        message_ref, pick_ref, scaled, exact, both = refs
     else:
         x_ref, message_ref, pick_ref, scaled, exact = refs
     half = QH * HD
-    rows = x_ref.shape[0]
+    rows = a_ref.shape[0]
     first = jnp.full((rows, HD), flags[2], jnp.int32) > 0
     lane = lax.broadcasted_iota(jnp.int32, (rows, HD), 1)
     square = jnp.zeros((rows, HD), f32)
@@ -228,7 +229,8 @@
             x = b_ref[:, at]
             if combined:
                 x = jnp.where(first, extra_ref[:, at].astype(f32), x.astype(f32)).astype(bf16)
-        x_ref[:, n * HD : (n + 1) * HD] = x
+        if tick < 3:
+            x_ref[:, n * HD : (n + 1) * HD] = x
         wide = x.astype(f32)
         exact[n * rows : (n + 1) * rows, :] = wide
         square = square + wide * wide
@@ -296,12 +298,12 @@
         functools.partial(tick_kernel, tick),
         grid=(1,),
         out_shape=(
-            jax.ShapeDtypeStruct((rows, 2 * half), bf16),
+            *[jax.ShapeDtypeStruct((rows, 2 * half), bf16)] * (tick < 3),
             jax.ShapeDtypeStruct((rows, 2 if tick == 3 else rows, HD), bf16),
             jax.ShapeDtypeStruct((4 if tick == 3 else 2, 2 * half), bf16),
         ),
         in_specs=specs,
-        out_specs=(held, held, held),
+        out_specs=(held,) * (3 if tick < 3 else 2),
         scratch_shapes=[
             pltpu.VMEM((2, rows, half), bf16),
             pltpu.VMEM((2 * QH * rows, HD), f32),
@@ -410,7 +412,8 @@
                 tails = lax.ppermute(x, ALL, links([(sections - 1, 1, 0, 0), (1, 1, 0, 1)]))
             extra = got if tick == 1 else tails
             past = dict(spoken=messages, found=found) if tick == 3 else {}
-            x, message, rows = step(relayed, heard=heard, extra=extra, **past)
+            *x, message, rows = step(relayed, heard=heard, extra=extra, **past)
+            x = x[0] if x else None
         found = found + [rows]
         messages = messages + [message]
 

time: 134 us -> 134 us (level)
  no operation moved by 1% of the time
where the time goes in v6:
time: 134 us; the launch traced here: 133 us
  waiting for transfers between devices  45.1 us (34%)
  starting transfers between devices  39.6 us (30%)
  blocking collectives  22.4 us (17%)
  Pallas kernels  22.1 us (16%)
  local copies, waits for them, and re-layouts  2.87 us (2%)
    all_to_all x1, waiting for transfers between devices, inner(): got = lax.all_to_all(sent, RC, split_axis=0, concat_axis=0, tiled=True)  21.1 us
    all_to_all x2, starting transfers between devices, inner(): lax.all_to_all(message, ALL, split_axis=0, concat_axis=0, axis_index_grou...  14.4 us
    pallas_call x4, Pallas kernels, do_tick(): pl.pallas_call(functools.partial(tick_kernel, tick), grid=(1,), out_shape...  13.7 us
    all_to_all x2, waiting for transfers between devices, inner(): lax.all_to_all(message, ALL, split_axis=0, concat_axis=0, axis_index_grou...  13.7 us
    all_to_all x1, blocking collectives, inner(): lax.all_to_all(messages[3], RC, split_axis=0, concat_axis=0, tiled=True)  11.8 us
    all_to_all x1, blocking collectives, inner(): lax.all_to_all(message, ALL, split_axis=0, concat_axis=0, axis_index_grou...  10.6 us
    ppermute x1, waiting for transfers between devices, inner(): lax.ppermute(fed, 'section', [(s, s + 1) for s in range(sections - 1)])  10.3 us
    all_to_all x1, starting transfers between devices, inner(): got = lax.all_to_all(sent, RC, split_axis=0, concat_axis=0, tiled=True)  7.34 us
  transfers between devices with their start and end apart: 10, of which 4 were waited for; matrix products, arithmetic and copies ran while one was open for 1% of the time, Pallas kernels for 5%

profile of v6, /device:TPU:6, one launch (start us, length us, event | category | flops | bytes accessed | tf_op | source)
XLA Modules:
  0.0 132.7 jit_solution(8091145066642704721)
XLA Ops:
  0.0 2.4 %first_part.1 = (f32[192,128]{1,0:T(8,128)}, bf16[192,128]{1,0:T(8,128)(2,1)}, f32[8,128]{1,0:T(8,128)}) custom-call(s32[1]{0:T(128)} %bitcast.4.base, s32[51]{0:T(128)} %bitcast.55, bf16[4,8192]{1,0:T(4,128)(2,1)} %bitcast.51, bf16[4,128,512]{2,1,0:T(8,128)(2,1)} %bitcast.47, bf16[4,128,512]{2,1,0:T(8,128)(2,1)} %bitcast.49), custom_call_target="tpu_custom_call" | custom-call | flops 4194304 | bytes 4194304 | tf_op jit(solution)/shard_map/first_part/pallas_call | solution.py:148
  2.4 4.3 %collective-permute-start = (bf16[192,128]{1,0:T(8,128)(2,1)}, bf16[192,128]{1,0:T(8,128)(2,1)S(1)}, u32[]{:S(2)}, u32[]{:S(2)}) collective-permute-start(bf16[192,128]{1,0:T(8,128)(2,1)} %get-tuple-element.25), channel_id=1, source_target_pairs={{0,16},{16,32},{32,48},{48,64},{64,80},{80,96},{96,112},{112,128},... | collective-permute-start | bytes 147464 | tf_op jit(solution)/shard_map/ppermute | solution.py:392
  6.7 2.5 %second_part.1 = (f32[64,128]{1,0:T(8,128)}, bf16[128,128]{1,0:T(8,128)(2,1)}, bf16[64,128]{1,0:T(8,128)(2,1)}, bf16[192,128]{1,0:T(8,128)(2,1)}, bf16[256,128]{1,0:T(8,128)(2,1)}, /*index=5*/f32[8,128]{1,0:T(8,128)}) custom-call(s32[1]{0:T(128)} %bitcast.4.base, s32[51]{0:T(128)} %bitcast.56, s32[1]{0:T(128)} %bitcast.9.pick, bf16[4,8192]{1,0:T(4,128)(2,1)} %bitcast.52, ...), custom_call_target="tpu_custom_call" | custom-call | flops 16777216 | bytes 16777216 | tf_op jit(solution)/shard_map/second_part/pallas_call | solution.py:163
  9.2 10.3 %collective-permute-done.fed_ref = bf16[192,128]{1,0:T(8,128)(2,1)S(1)} collective-permute-done((bf16[192,128]{1,0:T(8,128)(2,1)}, bf16[192,128]{1,0:T(8,128)(2,1)S(1)}, u32[]{:S(2)}, u32[]{:S(2)}) %collective-permute-start) | collective-permute-done | bytes 49184 | tf_op jit(solution)/shard_map/ppermute | solution.py:392
  19.5 0.6 copy-done.5
  20.2 2.0 %third_part.1 = bf16[16,232,128]{2,1,0:T(8,128)(2,1)} custom-call(s32[1]{0:T(128)} %bitcast.2.flags, bf16[192,128]{1,0:T(8,128)(2,1)} %copy-done.5, bf16[192,128]{1,0:T(8,128)(2,1)} %get-tuple-element.27.head_ref, bf16[128,128]{1,0:T(8,128)(2,1)} %get-tuple-element.28.own_ref, bf16[64,128]{1,0:T(8,128)(2,1)} %get-tuple-element.29.tail_ref, ...), custom_call_target="tpu_custom_call" | custom-call | flops 1048576 | bytes 1048576 | tf_op jit(solution)/shard_map/third_part/pallas_call | solution.py:185
  22.1 7.3 %all-to-all-start = ((bf16[16,232,128]{2,1,0:T(8,128)(2,1)}), bf16[16,232,128]{2,1,0:T(8,128)(2,1)S(1)}, u32[]{:S(2)}, u32[]{:S(2)}) async-start(bf16[16,232,128]{2,1,0:T(8,128)(2,1)} %third_part.1), calls=%async_computation | async-start | bytes 1900544 | tf_op jit(solution)/shard_map/all_to_all | solution.py:394
  29.5 2.3 %collective-permute-start.1 = (bf16[8192,128]{1,0:T(8,128)(2,1)S(1)}, bf16[8192,128]{1,0:T(8,128)(2,1)}, u32[]{:S(2)}, u32[]{:S(2)}) collective-permute-start(bf16[8192,128]{1,0:T(8,128)(2,1)S(1)} %bitcast.41), channel_id=1, source_target_pairs={{0,8},{8,0},{1,9},{9,1},{2,10},{10,2},{3,11},{11,3},{4,12},{12,4},... | collective-permute-start | bytes 6291464 | tf_op jit(solution)/shard_map/ppermute | solution.py:380
  31.8 0.1 pad_add_fusion.refs_0_.flags
  31.9 21.1 %all-to-all-done = bf16[16,232,128]{2,1,0:T(8,128)(2,1)S(1)} async-done(((bf16[16,232,128]{2,1,0:T(8,128)(2,1)}), bf16[16,232,128]{2,1,0:T(8,128)(2,1)S(1)}, u32[]{:S(2)}, u32[]{:S(2)}) %all-to-all-start) | async-done | bytes 950304 | tf_op jit(solution)/shard_map/all_to_all | solution.py:394
  53.0 0.9 copy-done.4
  53.9 1.3 copy.11
  55.2 0.2 convert_reduce_fusion.1
  55.4 0.1 multiply_cosine_fusion.1
  55.6 0.1 maximum_bitcast_fusion
  55.6 0.1 maximum_bitcast_fusion.2
  55.7 3.4 %shard_map.82 = (bf16[16,16384]{1,0:T(8,128)(2,1)}, bf16[16,16,128]{2,1,0:T(8,128)(2,1)}, bf16[2,16384]{1,0:T(2,128)(2,1)S(1)}) custom-call(s32[4]{0:T(128)S(1)} %pad_add_fusion.refs_0_.flags, bf16[16,29696]{1,0:T(8,128)(2,1)S(1)} %bitcast.27, bf16[16,29696]{1,0:T(8,128)(2,1)S(1)} %bitcast.28, bf16[16,29696]{1,0:T(8,128)(2,1)S(1)} %bitcast.29, ...), custom_call_target="tpu_custom_call" | custom-call | flops 67108864 | bytes 6291456 | tf_op jit(solution)/shard_map/pallas_call | solution.py:297
  59.2 2.1 %collective-permute-start.2 = (bf16[16,16384]{1,0:T(8,128)(2,1)}, bf16[16,16384]{1,0:T(8,128)(2,1)}, u32[]{:S(2)}, u32[]{:S(2)}) collective-permute-start(bf16[16,16384]{1,0:T(8,128)(2,1)} %get-tuple-element.32), channel_id=1, source_target_pairs={{0,24},{1,25},{2,26},{3,27},{4,28},{5,29},{6,30},{7,31},{16,40},{1... | collective-permute-start | bytes 1572872 | tf_op jit(solution)/shard_map/ppermute | solution.py:409
  61.2 5.8 %all-to-all-start.1 = ((bf16[16,16,128]{2,1,0:T(8,128)(2,1)}), bf16[16,16,128]{2,1,0:T(8,128)(2,1)S(1)}, u32[]{:S(2)}, u32[]{:S(2)}) async-start(bf16[16,16,128]{2,1,0:T(8,128)(2,1)} %get-tuple-element.33.refs_12_), calls=%async_computation.1 | async-start | bytes 131072 | tf_op jit(solution)/shard_map/all_to_all | solution.py:410
  67.1 1.5 %collective-permute-start.4 = (bf16[16,16384]{1,0:T(8,128)(2,1)}, bf16[16,16384]{1,0:T(8,128)(2,1)}, u32[]{:S(2)}, u32[]{:S(2)}) collective-permute-start(bf16[16,16384]{1,0:T(8,128)(2,1)} %get-tuple-element.32), channel_id=1, source_target_pairs={{760,0},{761,1},{762,2},{763,3},{764,4},{765,5},{766,6},{767,7},{2... | collective-permute-start | bytes 1572872 | tf_op jit(solution)/shard_map/ppermute | solution.py:412
  68.5 6.5 %all-to-all-done.1.refs_9_ = bf16[16,16,128]{2,1,0:T(8,128)(2,1)S(1)} async-done(((bf16[16,16,128]{2,1,0:T(8,128)(2,1)}), bf16[16,16,128]{2,1,0:T(8,128)(2,1)S(1)}, u32[]{:S(2)}, u32[]{:S(2)}) %all-to-all-start.1) | async-done | bytes 65568 | tf_op jit(solution)/shard_map/all_to_all | solution.py:410
  75.0 3.8 %shard_map.83 = (bf16[16,16384]{1,0:T(8,128)(2,1)}, bf16[16,16,128]{2,1,0:T(8,128)(2,1)}, bf16[2,16384]{1,0:T(2,128)(2,1)S(1)}) custom-call(s32[4]{0:T(128)S(1)} %pad_add_fusion.refs_0_.flags, bf16[16,16384]{1,0:T(8,128)(2,1)} %collective-permute-done.2.refs_1_.refs_2_, bf16[16,16384]{1,0:T(8,128)(2,1)} %collective-permute-done.2.refs_1_.refs_2_, ...), custom_call_target="tpu_custom_call" | custom-call | flops 67108864 | bytes 6291456 | tf_op jit(solution)/shard_map/pallas_call | solution.py:297
  78.8 1.3 collective-permute-start.3
  80.1 8.6 %all-to-all-start.2 = ((bf16[16,16,128]{2,1,0:T(8,128)(2,1)}), bf16[16,16,128]{2,1,0:T(8,128)(2,1)S(1)}, u32[]{:S(2)}, u32[]{:S(2)}) async-start(bf16[16,16,128]{2,1,0:T(8,128)(2,1)} %get-tuple-element.35.refs_13_), calls=%async_computation.2 | async-start | bytes 131072 | tf_op jit(solution)/shard_map/all_to_all | solution.py:410
  88.7 7.2 %all-to-all-done.2.refs_9_ = bf16[16,16,128]{2,1,0:T(8,128)(2,1)S(1)} async-done(((bf16[16,16,128]{2,1,0:T(8,128)(2,1)}), bf16[16,16,128]{2,1,0:T(8,128)(2,1)S(1)}, u32[]{:S(2)}, u32[]{:S(2)}) %all-to-all-start.2) | async-done | bytes 65568 | tf_op jit(solution)/shard_map/all_to_all | solution.py:410
  95.9 3.2 %shard_map.84 = (bf16[16,16384]{1,0:T(8,128)(2,1)S(1)}, bf16[16,16,128]{2,1,0:T(8,128)(2,1)S(1)}, bf16[2,16384]{1,0:T(2,128)(2,1)S(1)}) custom-call(s32[4]{0:T(128)S(1)} %pad_add_fusion.refs_0_.flags, bf16[16,16384]{1,0:T(8,128)(2,1)} %collective-permute-done.3.refs_1_.refs_2_, bf16[16,16384]{1,0:T(8,128)(2,1)} %collective-permute-done.3.refs_1_.refs_2_, ...), custom_call_target="tpu_custom_call" | custom-call | flops 67108864 | bytes 6291456 | tf_op jit(solution)/shard_map/pallas_call | solution.py:297
  99.1 1.3 collective-permute-start.5
  100.4 10.6 %all_to_all.25.refs_9_ = bf16[16,16,128]{2,1,0:T(8,128)(2,1)S(1)} all-to-all(bf16[16,16,128]{2,1,0:T(8,128)(2,1)S(1)} %get-tuple-element.37.refs_14_), channel_id=1, replica_groups={{0,1,2,3,4,5,6,7,24,25,26,27,28,29,30,31},{16,17,18,19,20,21,22,23,40,4..., dimensions={0} | all-to-all | bytes 131072 | tf_op jit(solution)/shard_map/all_to_all | solution.py:410
  111.0 3.3 %shard_map.85 = (bf16[16,2,128]{2,1,0:T(2,128)(2,1)S(1)}, bf16[4,16384]{1,0:T(4,128)(2,1)S(1)}) custom-call(s32[4]{0:T(128)S(1)} %pad_add_fusion.refs_0_.flags, bf16[16,16384]{1,0:T(8,128)(2,1)S(1)} %collective-permute-done.5.refs_1_.refs_2_, bf16[16,16384]{1,0:T(8,128)(2,1)S(1)} %collective-permute-done.5.refs_1_.refs_2_, bf16[16,29696]{1,0:T(8,128)(2,1)S(1)} %bitcast.38, ...), custom_call_target="tpu_custom_call" | custom-call | flops 67108864 | bytes 6291456 | tf_op jit(solution)/shard_map/pallas_call | solution.py:297
  114.3 5.1 %collective-permute-start.6 = (bf16[4,16384]{1,0:T(4,128)(2,1)S(1)}, bf16[4,16384]{1,0:T(4,128)(2,1)S(1)}, u32[]{:S(2)}, u32[]{:S(2)}) collective-permute-start(bf16[4,16384]{1,0:T(4,128)(2,1)S(1)} %get-tuple-element.41.mine_ref), channel_id=1, source_target_pairs={{0,8},{8,0},{1,9},{9,1},{2,10},{10,2},{3,11},{11,3},{4,12},{12,4},... | collective-permute-start | bytes 393224 | tf_op jit(solution)/shard_map/ppermute | solution.py:421
  119.4 11.8 %all_to_all.26.told_ref = bf16[16,2,128]{2,1,0:T(2,128)(2,1)S(1)} all-to-all(bf16[16,2,128]{2,1,0:T(2,128)(2,1)S(1)} %get-tuple-element.42), channel_id=1, replica_groups=mesh['section'=48,'row'=2,'col'=8] {'row','col'}, dimensions={0} | all-to-all | bytes 16384 | tf_op jit(solution)/shard_map/all_to_all | solution.py:420
  131.2 1.5 %last_part.1 = bf16[4,16384]{1,0:T(4,128)(2,1)} custom-call(s32[4]{0:T(128)S(1)} %pad_add_fusion.refs_0_.flags, bf16[4,16384]{1,0:T(4,128)(2,1)S(1)} %get-tuple-element.41.mine_ref, bf16[4,16384]{1,0:T(4,128)(2,1)S(1)} %collective-permute-done.6.swap_ref, bf16[16,2,128]{2,1,0:T(2,128)(2,1)S(1)} %all_to_all.26.told_ref, f32[192,128]{1,0:T(8,128)S(1)} %copy-done.2, ...), custom_call_target="tpu_custom_call" | custom-call | flops 1048576 | bytes 1048576 | tf_op jit(solution)/shard_map/last_part/pallas_call | solution.py:343
  (18 shorter events, 0.0 us)
Async XLA Ops:
  2.4 17.1 %collective-permute-start = (bf16[192,128]{1,0:T(8,128)(2,1)}, bf16[192,128]{1,0:T(8,128)(2,1)S(1)}, u32[]{:S(2)}, u32[]{:S(2)}) collective-permute-start(bf16[192,128]{1,0:T(8,128)(2,1)} %get-tuple-element.25), channel_id=1, source_target_pairs={{0,16},{16,32},{32,48},{48,64},{64,80},{80,96},{96,112},{112,128},... | collective-permute-start | bytes 147464 | tf_op jit(solution)/shard_map/ppermute | solution.py:392
  6.7 22.7 %copy-start = (bf16[1,8192,128]{2,1,0:T(8,128)(2,1)S(1)}, bf16[1,8192,128]{2,1,0:T(8,128)(2,1)}, u32[]{:S(2)}) copy-start(bf16[1,8192,128]{2,1,0:T(8,128)(2,1)} %param.11) | copy-start | bytes 6291460
  19.5 0.6 copy-start.5
  22.1 33.6 %copy-start.1 = (bf16[1,16384]{1,0:T(2,128)(2,1)S(1)}, bf16[1,16384]{1,0:T(2,128)(2,1)}, u32[]{:S(2)}) copy-start(bf16[1,16384]{1,0:T(2,128)(2,1)} %refs_6_.7) | copy-start | bytes 98308
  22.1 30.9 %all-to-all-start = ((bf16[16,232,128]{2,1,0:T(8,128)(2,1)}), bf16[16,232,128]{2,1,0:T(8,128)(2,1)S(1)}, u32[]{:S(2)}, u32[]{:S(2)}) async-start(bf16[16,232,128]{2,1,0:T(8,128)(2,1)} %third_part.1), calls=%async_computation | async-start | bytes 1900544 | tf_op jit(solution)/shard_map/all_to_all | solution.py:394
  29.5 26.2 %collective-permute-start.1 = (bf16[8192,128]{1,0:T(8,128)(2,1)S(1)}, bf16[8192,128]{1,0:T(8,128)(2,1)}, u32[]{:S(2)}, u32[]{:S(2)}) collective-permute-start(bf16[8192,128]{1,0:T(8,128)(2,1)S(1)} %bitcast.41), channel_id=1, source_target_pairs={{0,8},{8,0},{1,9},{9,1},{2,10},{10,2},{3,11},{11,3},{4,12},{12,4},... | collective-permute-start | bytes 6291464 | tf_op jit(solution)/shard_map/ppermute | solution.py:380
  53.0 0.9 copy-start.4
  59.2 15.9 %collective-permute-start.2 = (bf16[16,16384]{1,0:T(8,128)(2,1)}, bf16[16,16384]{1,0:T(8,128)(2,1)}, u32[]{:S(2)}, u32[]{:S(2)}) collective-permute-start(bf16[16,16384]{1,0:T(8,128)(2,1)} %get-tuple-element.32), channel_id=1, source_target_pairs={{0,24},{1,25},{2,26},{3,27},{4,28},{5,29},{6,30},{7,31},{16,40},{1... | collective-permute-start | bytes 1572872 | tf_op jit(solution)/shard_map/ppermute | solution.py:409
  61.2 13.8 %all-to-all-start.1 = ((bf16[16,16,128]{2,1,0:T(8,128)(2,1)}), bf16[16,16,128]{2,1,0:T(8,128)(2,1)S(1)}, u32[]{:S(2)}, u32[]{:S(2)}) async-start(bf16[16,16,128]{2,1,0:T(8,128)(2,1)} %get-tuple-element.33.refs_12_), calls=%async_computation.1 | async-start | bytes 131072 | tf_op jit(solution)/shard_map/all_to_all | solution.py:410
  67.1 21.6 %collective-permute-start.4 = (bf16[16,16384]{1,0:T(8,128)(2,1)}, bf16[16,16384]{1,0:T(8,128)(2,1)}, u32[]{:S(2)}, u32[]{:S(2)}) collective-permute-start(bf16[16,16384]{1,0:T(8,128)(2,1)} %get-tuple-element.32), channel_id=1, source_target_pairs={{760,0},{761,1},{762,2},{763,3},{764,4},{765,5},{766,6},{767,7},{2... | collective-permute-start | bytes 1572872 | tf_op jit(solution)/shard_map/ppermute | solution.py:412
  78.8 17.1 %collective-permute-start.3 = (bf16[16,16384]{1,0:T(8,128)(2,1)}, bf16[16,16384]{1,0:T(8,128)(2,1)}, u32[]{:S(2)}, u32[]{:S(2)}) collective-permute-start(bf16[16,16384]{1,0:T(8,128)(2,1)} %get-tuple-element.34), channel_id=1, source_target_pairs={{8,16},{9,17},{10,18},{11,19},{12,20},{13,21},{14,22},{15,23},{24,... | collective-permute-start | bytes 1572872 | tf_op jit(solution)/shard_map/ppermute | solution.py:409
  80.1 15.8 %all-to-all-start.2 = ((bf16[16,16,128]{2,1,0:T(8,128)(2,1)}), bf16[16,16,128]{2,1,0:T(8,128)(2,1)S(1)}, u32[]{:S(2)}, u32[]{:S(2)}) async-start(bf16[16,16,128]{2,1,0:T(8,128)(2,1)} %get-tuple-element.35.refs_13_), calls=%async_computation.2 | async-start | bytes 131072 | tf_op jit(solution)/shard_map/all_to_all | solution.py:410
  99.1 11.9 %collective-permute-start.5 = (bf16[16,16384]{1,0:T(8,128)(2,1)S(1)}, bf16[16,16384]{1,0:T(8,128)(2,1)S(1)}, u32[]{:S(2)}, u32[]{:S(2)}) collective-permute-start(bf16[16,16384]{1,0:T(8,128)(2,1)S(1)} %get-tuple-element.36), channel_id=1, source_target_pairs={{0,24},{1,25},{2,26},{3,27},{4,28},{5,29},{6,30},{7,31},{16,40},{1... | collective-permute-start | bytes 1572872 | tf_op jit(solution)/shard_map/ppermute | solution.py:409
  111.0 20.2 %copy-start.2 = (f32[192,128]{1,0:T(8,128)S(1)}, f32[192,128]{1,0:T(8,128)}, u32[]{:S(2)}) copy-start(f32[192,128]{1,0:T(8,128)} %get-tuple-element.43.early_ref) | copy-start | bytes 294916
  111.0 20.2 %copy-start.3 = (f32[64,128]{1,0:T(8,128)S(1)}, f32[64,128]{1,0:T(8,128)}, u32[]{:S(2)}) copy-start(f32[64,128]{1,0:T(8,128)} %get-tuple-element.44.late_ref) | copy-start | bytes 98308
  114.3 16.9 %collective-permute-start.6 = (bf16[4,16384]{1,0:T(4,128)(2,1)S(1)}, bf16[4,16384]{1,0:T(4,128)(2,1)S(1)}, u32[]{:S(2)}, u32[]{:S(2)}) collective-permute-start(bf16[4,16384]{1,0:T(4,128)(2,1)S(1)} %get-tuple-element.41.mine_ref), channel_id=1, source_target_pairs={{0,8},{8,0},{1,9},{9,1},{2,10},{10,2},{3,11},{11,3},{4,12},{12,4},... | collective-permute-start | bytes 393224 | tf_op jit(solution)/shard_map/ppermute | solution.py:421
